TPU v7x, 512 devices: a whole 4x8x8 slice. The times are simulated.
512 devices in a mesh: src: 64 (over z_lo, y, core), sub: 8 (over x, z_hi).
Axes of the slice: x: 4, y: 8, z: 8 (z_hi: 2, z_lo: 4; z = z_hi * 4 + z_lo), core: 2. Of those that a mesh axis runs over, the one named last changes fastest.
Arguments:
- child_rhs: float32 [8, 1024, 16384], P('sub', None, 'src'), may hold values from -6 to 6
- root_rhs: float32 [2048, 16384], P('sub', 'src'), may hold values from -6 to 6
- child_inverse: bfloat16 [8, 1024, 1024], P('sub', 'src'), as said below
- coupling_block: bfloat16 [8, 1024, 1024], P('sub', 'src'), may hold values from -0.1875 to 0.1875
- root_inverse: bfloat16 [2048, 2048], P('sub', 'src'), as said below
- child_orders: int32 [8], P('sub'), may hold values from 716 to 1024, as said below
- coupling_rows: int32 [8, 1024], P('sub'), may hold values from 0 to 2047, as said below
Outputs:
- child_solution: float32 [8, 1024, 16384], P('sub', None, 'src')
- root_solution: float32 [2048, 16384], P('sub', 'src')
Inputs may be any that keep to these rules, and one draw needn't show every extreme that they name: Each child_inverse[j] is lower triangular: zero above the diagonal, diagonal entries between 0.8 and 1.25. `root_inverse`: lower triangular: zero above the diagonal, diagonal entries between 0.8 and 1.25. `coupling_rows`: each row holds 1024 distinct root rows in increasing order. `child_orders`: some child has order 1024.
All inputs are finite; a program needn't handle non-finite values.
Results may differ from a plain program's by a relative error of at most 0.0093.
Values may be sent and summed in bfloat16 or wider, within the bound.
No kernel may reach another device: no remote copies, remote signals or barrier semaphores. Data moves between devices by JAX's collectives and lax.ppermute only.
A program may use at most 64 MiB of HBM per device.

v0:
```python
import jax
import jax.numpy as jnp
from jax import lax
from jax.sharding import PartitionSpec as P


def sent_to_all(x, axis):
    length = lax.axis_size(axis)
    return lax.all_to_all(jnp.broadcast_to(x[None], (length, *x.shape)), axis, 0, 0, tiled=True)


def in_order(blocks, dim):
    lengths = list(blocks.shape[1:])
    lengths[dim] *= blocks.shape[0]
    return jnp.moveaxis(blocks, 0, dim).reshape(lengths)


def collect(x, axis, dim):
    blocks = sent_to_all(x, axis)
    return in_order(blocks, dim)


def in_blocks(x, dim, length):
    before, after = (x.shape[:dim], x.shape[dim + 1 :])
    return jnp.moveaxis(x.reshape(*before, length, -1, *after), dim, 0)


def sum_at_owner(x, axis, dim):
    length = lax.axis_size(axis)
    blocks = lax.all_to_all(in_blocks(x, dim, length), axis, 0, 0, tiled=True)
    return jnp.sum(blocks.astype(jnp.float32), axis=0)


def contract_rows(left, right):
    return lax.dot_general(
        left, right, (((0,), (0,)), ((), ())), preferred_element_type=jnp.float32
    )


def on_device(
    child_rhs, root_rhs, child_inverse, coupling_block, root_inverse, child_orders, coupling_rows
):
    inverse = child_inverse[0]
    coupling = coupling_block[0]
    coupling_index = coupling_rows[0]
    columns = child_rhs.shape[2]
    child_order = inverse.shape[1]
    root_order = root_inverse.shape[1] * lax.axis_size("src")
    alive = (lax.iota(jnp.int32, child_order) < child_orders[0])[:, None]
    child_source = jnp.where(alive, child_rhs[0], 0.0).astype(jnp.bfloat16)
    whole_inverse = lax.all_gather(inverse, "src", axis=0, tiled=True)
    whole_coupling = collect(coupling, "src", 0)
    forward = jnp.dot(whole_inverse, child_source, preferred_element_type=jnp.float32)
    child_solved = jnp.where(alive, forward, 0.0)
    solved_round = child_solved.astype(jnp.bfloat16)
    update = jnp.dot(whole_coupling, solved_round, preferred_element_type=jnp.float32)
    placed = jnp.zeros((root_order, columns), jnp.float32).at[coupling_index].add(update)
    share = sum_at_owner(placed.astype(jnp.bfloat16), "sub", 0)
    root_source = collect((root_rhs - share).astype(jnp.bfloat16), "sub", 0)
    root_rows = lax.all_gather(root_inverse, "src", axis=1, tiled=True)
    root_forward = jnp.dot(root_rows, root_source, preferred_element_type=jnp.float32)
    root_round = root_forward.astype(jnp.bfloat16)
    partial_root = contract_rows(root_rows, root_round)
    root_out = sum_at_owner(partial_root.astype(jnp.bfloat16), "sub", 0)
    rounded_all = collect(root_out.astype(jnp.bfloat16), "sub", 0)
    picked = rounded_all[coupling_index]
    pulled = contract_rows(whole_coupling, picked)
    residue = jnp.where(alive, child_solved - pulled, 0.0).astype(jnp.bfloat16)
    backward = contract_rows(whole_inverse, residue)
    child_out = jnp.where(alive, backward, 0.0)[None]
    return (child_out, root_out)


def solution(mesh):
    return jax.shard_map(
        on_device,
        mesh=mesh,
        in_specs=(
            P("sub", None, "src"),
            P("sub", "src"),
            P("sub", "src", None),
            P("sub", "src", None),
            P("sub", "src"),
            P("sub"),
            P("sub", None),
        ),
        out_specs=(P("sub", None, "src"), P("sub", "src")),
        check_vma=False,
    )
```

profile of v0, /device:TPU:73, one launch (start us, length us, event | category | flops | bytes accessed | tf_op | source)
XLA Modules:
  0.0 402.6 jit_solution(723256197187637208)
XLA Ops:
  7.2 0.0 all-gather.6.cloned.1.call-start
  7.2 0.7 all-gather.6.cloned.1.call-update
  7.9 2.3 broadcast_in_dim.62
  10.2 13.1 %all-to-all-start = ((bf16[64,16,1024]{2,1,0:T(8,128)(2,1)}), bf16[64,16,1024]{2,1,0:T(8,128)(2,1)S(1)}, u32[]{:S(2)}, u32[]{:S(2)}) async-start(bf16[64,16,1024]{2,1,0:T(8,128)(2,1)} %broadcast_in_dim.62), calls=%async_computation | async-start | bytes 4194304 | tf_op jit(solution)/shard_map/all_to_all | solution.py:9
  24.0 130.5 %all-gather.6.cloned.1.call-done = bf16[1,1024,1024]{2,1,0:T(8,128)(2,1)} async-done(((bf16[1,16,1024]{2,1,0:T(8,128)(2,1)}), bf16[1,1024,1024]{2,1,0:T(8,128)(2,1)}) %all-gather.6.cloned.1.call-update) | async-done | bytes 2097168 | tf_op jit(solution)/shard_map/all_gather | solution.py:51
  154.5 2.9 fusion.4
  157.4 0.0 copy-start.2
  157.4 0.0 all-to-all-done
  157.4 2.0 convolution_bitcast_fusion
  159.4 2.6 copy.13
  162.0 7.0 %scatter_custom_fusion = f32[2048,256]{1,0:T(8,128)S(1)} fusion(s32[1024]{0:T(1024)S(1)} %bitcast.50, f32[1024,256]{1,0:T(8,128)} %copy.13, f32[]{:T(128)} %constant.3.clone.1), kind=kCustom, calls=%fused_computation.20 | custom fusion | flops 262144 | bytes 2097664 | tf_op jit(solution)/shard_map/scatter-add | solution.py:57
  169.0 1.1 convert_element_type.42
  170.1 9.9 %all-to-all-start.1 = ((bf16[8,256,256]{2,1,0:T(8,128)(2,1)}), bf16[8,256,256]{2,1,0:T(8,128)(2,1)S(1)}, u32[]{:S(2)}, u32[]{:S(2)}) async-start(bf16[8,256,256]{2,1,0:T(8,128)(2,1)} %bitcast.8), calls=%async_computation.1 | async-start | bytes 2097152 | tf_op jit(solution)/shard_map/all_to_all | solution.py:30
  180.0 0.0 all-gather.4.cloned.1.call-start
  180.1 0.7 all-gather.4.cloned.1.call-update
  180.8 30.2 %all-to-all-done.1 = bf16[8,256,256]{2,1,0:T(8,128)(2,1)S(1)} async-done(((bf16[8,256,256]{2,1,0:T(8,128)(2,1)}), bf16[8,256,256]{2,1,0:T(8,128)(2,1)S(1)}, u32[]{:S(2)}, u32[]{:S(2)}) %all-to-all-start.1) | async-done | bytes 1048608 | tf_op jit(solution)/shard_map/all_to_all | solution.py:30
  210.9 0.1 convert_reduce_fusion.1
  211.1 1.1 broadcast_in_dim.63
  212.2 3.6 all-to-all-start.2
  215.8 96.6 %all-gather.4.cloned.1.call-done = bf16[256,2048]{0,1:T(8,128)(2,1)} async-done(((bf16[256,32]{0,1:T(8,128)(2,1)}), bf16[256,2048]{0,1:T(8,128)(2,1)}) %all-gather.4.cloned.1.call-update) | async-done | bytes 1048592 | tf_op jit(solution)/shard_map/all_gather | solution.py:60
  312.4 2.8 convolution_convert_fusion
  315.2 0.1 copy.22
  315.3 42.1 %all_to_all.25 = bf16[8,256,256]{1,2,0:T(8,128)(2,1)S(1)} all-to-all(bf16[8,256,256]{1,2,0:T(8,128)(2,1)S(1)} %bitcast.46), channel_id=1, replica_groups=mesh['src'=64,'sub'=8] {'sub'}, dimensions={0} | all-to-all | bytes 2097152 | tf_op jit(solution)/shard_map/all_to_all | solution.py:30
  357.4 0.1 convert_reduce_fusion
  357.6 0.1 copy.16
  357.7 1.0 broadcast_in_dim.64
  358.7 3.6 all-to-all-start.4
  362.3 0.8 copy.18
  363.2 22.9 %all-to-all-done.4 = bf16[8,256,256]{2,1,0:T(8,128)(2,1)S(1)} async-done(((bf16[8,256,256]{2,1,0:T(8,128)(2,1)}), bf16[8,256,256]{2,1,0:T(8,128)(2,1)S(1)}, u32[]{:S(2)}, u32[]{:S(2)}) %all-to-all-start.4) | async-done | bytes 1048608 | tf_op jit(solution)/shard_map/all_to_all | solution.py:9
  386.1 5.0 %gather_fusion = bf16[1024,256]{1,0:T(8,128)(2,1)} fusion(bf16[2048,256]{1,0:T(8,128)(2,1)S(1)} %bitcast.43, s32[1024]{0:T(1024)S(1)} %broadcast_clamp_fusion), kind=kCustom, calls=%fused_computation | custom fusion | bytes 1052672 | tf_op jit(solution)/shard_map/gather | solution.py:66
  391.1 3.3 fusion.10
  394.4 1.3 copy.17
  (15 shorter events, 0.1 us)
Async XLA Ops:
  7.2 147.3 %all-gather.6.cloned.1.call-start = ((), (), s32[]{:S(2)}) async-start(), calls=%async_computation.6 | async-start | bytes 2129920 | tf_op jit(solution)/shard_map/all_gather | solution.py:51
  10.2 13.7 %copy-start.4 = (s32[1,1024]{1,0:T(1,128)S(1)}, s32[1,1024]{1,0:T(1,128)}, u32[]{:S(2)}) copy-start(s32[1,1024]{1,0:T(1,128)} %param.13) | copy-start | bytes 12292
  10.2 147.2 %all-to-all-start = ((bf16[64,16,1024]{2,1,0:T(8,128)(2,1)}), bf16[64,16,1024]{2,1,0:T(8,128)(2,1)S(1)}, u32[]{:S(2)}, u32[]{:S(2)}) async-start(bf16[64,16,1024]{2,1,0:T(8,128)(2,1)} %broadcast_in_dim.62), calls=%async_computation | async-start | bytes 4194304 | tf_op jit(solution)/shard_map/all_to_all | solution.py:9
  157.4 2.0 copy-start.2
  157.4 2.0 copy-start
  170.1 41.0 %copy-start.3 = (f32[256,256]{1,0:T(8,128)S(1)}, f32[256,256]{1,0:T(8,128)}, u32[]{:S(2)}) copy-start(f32[256,256]{1,0:T(8,128)} %param.8) | copy-start | bytes 786436
  170.1 40.8 %all-to-all-start.1 = ((bf16[8,256,256]{2,1,0:T(8,128)(2,1)}), bf16[8,256,256]{2,1,0:T(8,128)(2,1)S(1)}, u32[]{:S(2)}, u32[]{:S(2)}) async-start(bf16[8,256,256]{2,1,0:T(8,128)(2,1)} %bitcast.8), calls=%async_computation.1 | async-start | bytes 2097152 | tf_op jit(solution)/shard_map/all_to_all | solution.py:30
  180.0 132.4 %all-gather.4.cloned.1.call-start = ((), (), s32[]{:S(2)}) async-start(), calls=%async_computation.5 | async-start | bytes 1064960 | tf_op jit(solution)/shard_map/all_gather | solution.py:60
  212.2 100.2 %all-to-all-start.2 = ((bf16[8,256,256]{2,1,0:T(8,128)(2,1)}), bf16[8,256,256]{2,1,0:T(8,128)(2,1)S(1)}, u32[]{:S(2)}, u32[]{:S(2)}) async-start(bf16[8,256,256]{2,1,0:T(8,128)(2,1)} %broadcast_in_dim.63), calls=%async_computation.2 | async-start | bytes 2097152 | tf_op jit(solution)/shard_map/all_to_all | solution.py:9
  358.7 27.3 %all-to-all-start.4 = ((bf16[8,256,256]{2,1,0:T(8,128)(2,1)}), bf16[8,256,256]{2,1,0:T(8,128)(2,1)S(1)}, u32[]{:S(2)}, u32[]{:S(2)}) async-start(bf16[8,256,256]{2,1,0:T(8,128)(2,1)} %broadcast_in_dim.64), calls=%async_computation.4 | async-start | bytes 2097152 | tf_op jit(solution)/shard_map/all_to_all | solution.py:9
  386.1 5.0 %copy-start.1 = (bf16[64,16,1024]{2,1,0:T(8,128)(2,1)S(1)}, bf16[64,16,1024]{2,1,0:T(8,128)(2,1)}, u32[]{:S(2)}) copy-start(bf16[64,16,1024]{2,1,0:T(8,128)(2,1)} %copy-done) | copy-start | bytes 6291460
Sparse Core Ops, SparseCore 0:
  10.1 144.2 all-gather.5
  183.0 129.3 all-gather.3
where the time goes:
time: 403 us
  waiting for transfers between devices  282 us (70%)
  blocking collectives  42.1 us (10%)
  starting transfers between devices  30.2 us (7%)
  between operations  14.8 us (4%)
  local copies, waits for them, and re-layouts  14.3 us (4%)
  matrix products  11 us (3%)
  other arithmetic  8.5 us (2%)
    all_gather x1, waiting for transfers between devices, on_device(): whole_inverse = lax.all_gather(inverse, 'src', axis=0, tiled=True)  130 us
    all_gather x1, waiting for transfers between devices, on_device(): root_rows = lax.all_gather(root_inverse, 'src', axis=1, tiled=True)  96.6 us
    all_to_all x1, blocking collectives, sum_at_owner(): blocks = lax.all_to_all(in_blocks(x, dim, length), axis, 0, 0, tiled=True)  42.1 us
    all_to_all x1, waiting for transfers between devices, sum_at_owner(): blocks = lax.all_to_all(in_blocks(x, dim, length), axis, 0, 0, tiled=True)  30.2 us
    all_to_all x3, waiting for transfers between devices, sent_to_all(): lax.all_to_all(jnp.broadcast_to(x[None], (length, *x.shape)), axis, 0, 0,...  22.9 us
    all_to_all x3, starting transfers between devices, sent_to_all(): lax.all_to_all(jnp.broadcast_to(x[None], (length, *x.shape)), axis, 0, 0,...  20.2 us
    all_to_all x1, starting transfers between devices, sum_at_owner(): blocks = lax.all_to_all(in_blocks(x, dim, length), axis, 0, 0, tiled=True)  9.91 us
  transfers between devices with their start and end apart: 6, of which 4 were waited for; matrix products, arithmetic and copies ran while one was open for 2% of the time, Pallas kernels for 0%

commit v1 on v0

v1 whole, which is shorter than its diff:
```python
import jax
import jax.numpy as jnp
from jax import lax
from jax.sharding import Mesh, PartitionSpec as P

ZL, Y, CORE, X, ZH = 4, 8, 2, 4, 2
SRC = ("zl", "y", "core")
SUB = ("x", "zh")
BF = jnp.bfloat16
F32 = jnp.float32


def gather_blocks(x, axis, length):
    return lax.all_to_all(jnp.broadcast_to(x[None], (length, *x.shape)), axis, 0, 0, tiled=True)


def both_cores(x):
    other = lax.ppermute(x, "core", [(0, 1), (1, 0)])
    first = lax.axis_index("core") == 0
    return jnp.stack([jnp.where(first, x, other), jnp.where(first, other, x)], axis=1)


def dot(a, b, ca, cb):
    return lax.dot_general(a, b, (((ca,), (cb,)), ((), ())), preferred_element_type=F32)


def on_device(
    child_rhs, root_rhs, child_inverse, coupling_block, root_inverse, child_orders, coupling_rows
):
    n = child_rhs.shape[2]
    s1 = child_rhs.shape[1]
    q1 = s1 // ZL
    s0 = root_rhs.shape[0] * X * ZH
    q0 = s0 // ZL
    k = coupling_rows.shape[1]
    r1 = child_inverse.shape[1]
    block = root_rhs.shape[0]
    sub = lax.axis_index("x") * ZH + lax.axis_index("zh")
    index = coupling_rows[0]

    pair = jnp.concatenate([child_inverse[0], coupling_block[0]], axis=0)
    by_zl = gather_blocks(pair, "zl", ZL)
    cb = by_zl[:, r1:, :].reshape(ZL * r1, s1)
    tri_rows = jnp.concatenate(
        [by_zl[3, :r1], jnp.concatenate([by_zl[2, :r1, : 3 * q1], by_zl[0, :r1, :q1]], axis=1),
         jnp.concatenate([by_zl[1, : r1 // 2, : 2 * q1], by_zl[1, r1 // 2 : r1, : 2 * q1]], axis=1)], axis=0)
    packed = jnp.concatenate([cb, tri_rows], axis=0)
    w = both_cores(gather_blocks(packed, "y", Y))
    nc = ZL * r1
    coupling = w[:, :, :nc].reshape(Y, CORE, ZL, r1, s1).transpose(2, 0, 1, 3, 4).reshape(k, s1)
    a3 = w[:, :, nc : nc + r1].reshape(q1, s1)
    a20 = w[:, :, nc + r1 : nc + 2 * r1].reshape(q1, s1)
    a1 = w[:, :, nc + 2 * r1 :]
    a1 = jnp.concatenate([a1[..., : 2 * q1], a1[..., 2 * q1 :]], axis=2).reshape(q1, 2 * q1)
    pad = lambda m: jnp.pad(m, ((0, 0), (0, s1 - m.shape[1])))
    inverse = jnp.concatenate([pad(a20[:, 3 * q1 :]), pad(a1), pad(a20[:, : 3 * q1]), a3], axis=0)

    rt = gather_blocks(root_inverse.T, SUB, X * ZH)
    rc = rt.shape[1]
    rt = rt.transpose(1, 0, 2).reshape(rc, s0)
    rt = gather_blocks(rt, "zl", ZL)
    rt = jnp.concatenate([rt[q, :, q * q0 :] for q in range(ZL)], axis=1)
    rt = both_cores(gather_blocks(rt, "y", Y)).reshape(q0, -1)
    starts = [sum(s0 - p * q0 for p in range(q)) for q in range(ZL)]
    rts = [rt[:, starts[q] : starts[q] + s0 - q * q0] for q in range(ZL)]

    alive = (lax.iota(jnp.int32, s1) < child_orders[0])[:, None]
    source = jnp.where(alive, child_rhs[0], 0.0).astype(BF)
    solved = jnp.where(alive, dot(inverse, source, 1, 0), 0.0)
    update_t = dot(solved.astype(BF), coupling, 0, 1).astype(BF)
    onehot = (index[:, None] == lax.iota(jnp.int32, s0)[None, :]).astype(BF)
    placed_t = -dot(update_t, onehot, 1, 0)
    mine = lax.dynamic_slice(placed_t, (0, sub * block), (n, block)) + root_rhs.T
    placed_t = lax.dynamic_update_slice(placed_t, mine, (0, sub * block))
    parts = lax.all_to_all(placed_t.astype(BF).reshape(X * ZH, n // (X * ZH), s0), SUB, 0, 0, tiled=True)
    s_t = jnp.sum(parts.astype(F32), axis=0).astype(BF)

    f_t = None
    for q in range(ZL):
        term = dot(s_t[:, q * q0 : (q + 1) * q0], rts[q], 1, 0)
        f_t = term if f_t is None else jnp.concatenate([f_t[:, : q * q0], f_t[:, q * q0 :] + term], axis=1)
    f_t = f_t.astype(BF)
    x_t = jnp.concatenate([dot(f_t[:, q * q0 :], rts[q], 1, 1) for q in range(ZL)], axis=1)
    x_all = gather_blocks(x_t.astype(BF), SUB, X * ZH).reshape(n, s0)
    root_out = lax.dynamic_slice(x_all, (0, sub * block), (n, block)).T.astype(F32)

    picked_t = dot(x_all, onehot, 1, 1).astype(BF)
    pulled_t = dot(picked_t, coupling, 1, 0)
    residue_t = jnp.where(alive.T, solved.T - pulled_t, 0.0).astype(BF)
    back = dot(inverse, residue_t, 0, 1)
    child_out = jnp.where(alive, back, 0.0)[None]
    return (child_out, root_out)


def solution(mesh):
    fine = Mesh(mesh.devices.reshape(ZL, Y, CORE, X, ZH), (*SRC, *SUB))
    return jax.shard_map(
        on_device,
        mesh=fine,
        in_specs=(
            P(SUB, None, SRC),
            P(SUB, SRC),
            P(SUB, SRC, None),
            P(SUB, SRC, None),
            P(SUB, SRC),
            P(SUB),
            P(SUB, None),
        ),
        out_specs=(P(SUB, None, SRC), P(SUB, SRC)),
        check_vma=False,
    )
```

time: 403 us -> 257 us (0.64)
  the two profiles are of different devices: /device:TPU:73 before, /device:TPU:1 now
where the time goes in v1:
time: 257 us; the launch traced here: 253 us
  waiting for transfers between devices  111 us (43%)
  blocking collectives  60.9 us (24%)
  starting transfers between devices  44.5 us (17%)
  matrix products  17 us (7%)
  local copies, waits for them, and re-layouts  11.4 us (4%)
  other arithmetic  7.17 us (3%)
    all_to_all x5, waiting for transfers between devices, gather_blocks(): lax.all_to_all(jnp.broadcast_to(x[None], (length, *x.shape)), axis, 0, 0,...  109 us
    all_to_all x5, starting transfers between devices, gather_blocks(): lax.all_to_all(jnp.broadcast_to(x[None], (length, *x.shape)), axis, 0, 0,...  32.5 us
    all_to_all x1, blocking collectives, on_device(): lax.all_to_all(placed_t.astype(BF).reshape(X * ZH, n // (X * ZH), s0), SU...  32.4 us
    all_to_all x1, blocking collectives, gather_blocks(): lax.all_to_all(jnp.broadcast_to(x[None], (length, *x.shape)), axis, 0, 0,...  28.5 us
    dot_general x12, matrix products, dot(): lax.dot_general(a, b, (((ca,), (cb,)), ((), ())), preferred_element_type=...  17 us
    ppermute x2, starting transfers between devices, both_cores(): other = lax.ppermute(x, 'core', [(0, 1), (1, 0)])  12 us
    broadcast_in_dim x7, local copies, waits for them, and re-layouts, gather_blocks(): jnp.broadcast_to(x[None], (length, *x.shape))  6.56 us
    another operation x4, other arithmetic, both_cores(): jnp.stack([jnp.where(first, x, other), jnp.where(first, other, x)], axis=1)  5.76 us
  transfers between devices with their start and end apart: 7, of which 6 were waited for; matrix products, arithmetic and copies ran while one was open for 5% of the time, Pallas kernels for 0%

profile of v1, /device:TPU:1, one launch (start us, length us, event | category | flops | bytes accessed | tf_op | source)
XLA Modules:
  0.0 253.3 jit_solution(11744014858334599971)
XLA Ops:
  0.6 1.4 broadcast_in_dim.79
  2.0 13.3 %all-to-all-start.3 = ((bf16[8,32,256]{2,1,0:T(8,128)(2,1)}), bf16[8,32,256]{2,1,0:T(8,128)(2,1)S(1)}, u32[]{:S(2)}, u32[]{:S(2)}) async-start(bf16[8,32,256]{2,1,0:T(8,128)(2,1)} %broadcast_in_dim.79), calls=%async_computation.3 | async-start | bytes 262144 | tf_op jit(solution)/shard_map/all_to_all | solution.py:14
  15.3 0.8 pad_maximum_fusion.9
  16.1 8.7 %all-to-all-done.3 = bf16[8,32,256]{2,1,0:T(8,128)(2,1)S(1)} async-done(((bf16[8,32,256]{2,1,0:T(8,128)(2,1)}), bf16[8,32,256]{2,1,0:T(8,128)(2,1)S(1)}, u32[]{:S(2)}, u32[]{:S(2)}) %all-to-all-start.3) | async-done | bytes 131104 | tf_op jit(solution)/shard_map/all_to_all | solution.py:14
  24.8 0.7 broadcast_in_dim.75
  25.5 4.4 %all-to-all-start = ((bf16[4,32,1024]{2,1,0:T(8,128)(2,1)}), bf16[4,32,1024]{2,1,0:T(8,128)(2,1)S(1)}, u32[]{:S(2)}, u32[]{:S(2)}) async-start(bf16[4,32,1024]{2,1,0:T(8,128)(2,1)} %broadcast_in_dim.75), calls=%async_computation | async-start | bytes 524288 | tf_op jit(solution)/shard_map/all_to_all | solution.py:14
  29.9 5.6 %all-to-all-done = bf16[4,32,1024]{2,1,0:T(8,128)(2,1)S(1)} async-done(((bf16[4,32,1024]{2,1,0:T(8,128)(2,1)}), bf16[4,32,1024]{2,1,0:T(8,128)(2,1)S(1)}, u32[]{:S(2)}, u32[]{:S(2)}) %all-to-all-start) | async-done | bytes 262176 | tf_op jit(solution)/shard_map/all_to_all | solution.py:14
  35.5 0.8 broadcast_in_dim.81
  36.4 3.5 %all-to-all-start.4 = ((bf16[4,32,2048]{2,1,0:T(8,128)(2,1)}), bf16[4,32,2048]{2,1,0:T(8,128)(2,1)S(1)}, u32[]{:S(2)}, u32[]{:S(2)}) async-start(bf16[4,32,2048]{2,1,0:T(8,128)(2,1)} %broadcast_in_dim.81), calls=%async_computation.4 | async-start | bytes 1048576 | tf_op jit(solution)/shard_map/all_to_all | solution.py:14
  39.9 10.7 %all-to-all-done.4 = bf16[4,32,2048]{2,1,0:T(8,128)(2,1)S(1)} async-done(((bf16[4,32,2048]{2,1,0:T(8,128)(2,1)}), bf16[4,32,2048]{2,1,0:T(8,128)(2,1)S(1)}, u32[]{:S(2)}, u32[]{:S(2)}) %all-to-all-start.4) | async-done | bytes 524320 | tf_op jit(solution)/shard_map/all_to_all | solution.py:14
  50.7 1.4 broadcast_in_dim.76
  52.1 6.8 %all-to-all-start.1 = ((bf16[8,104,1024]{2,1,0:T(8,128)(2,1)}), bf16[8,104,1024]{2,1,0:T(8,128)(2,1)S(1)}, u32[]{:S(2)}, u32[]{:S(2)}) async-start(bf16[8,104,1024]{2,1,0:T(8,128)(2,1)} %broadcast_in_dim.76), calls=%async_computation.1 | async-start | bytes 3407872 | tf_op jit(solution)/shard_map/all_to_all | solution.py:14
  59.0 39.8 %all-to-all-done.1 = bf16[8,104,1024]{2,1,0:T(8,128)(2,1)S(1)} async-done(((bf16[8,104,1024]{2,1,0:T(8,128)(2,1)}), bf16[8,104,1024]{2,1,0:T(8,128)(2,1)S(1)}, u32[]{:S(2)}, u32[]{:S(2)}) %all-to-all-start.1) | async-done | bytes 1703968 | tf_op jit(solution)/shard_map/all_to_all | solution.py:14
  98.8 2.1 broadcast_in_dim.82
  100.8 4.5 %all-to-all-start.5 = ((bf16[8,32,5120]{2,1,0:T(8,128)(2,1)}), bf16[8,32,5120]{2,1,0:T(8,128)(2,1)}, u32[]{:S(2)}, u32[]{:S(2)}) async-start(bf16[8,32,5120]{2,1,0:T(8,128)(2,1)} %broadcast_in_dim.82), calls=%async_computation.5 | async-start | bytes 5242880 | tf_op jit(solution)/shard_map/all_to_all | solution.py:14
  105.4 5.8 %collective-permute-start = (bf16[8,104,1024]{2,1,0:T(8,128)(2,1)S(1)}, bf16[8,104,1024]{2,1,0:T(8,128)(2,1)}, u32[]{:S(2)}, u32[]{:S(2)}) collective-permute-start(bf16[8,104,1024]{2,1,0:T(8,128)(2,1)S(1)} %all-to-all-done.1), channel_id=1, source_target_pairs={{0,8},{8,0},{1,9},{9,1},{2,10},{10,2},{3,11},{11,3},{4,12},{12,4},... | collective-permute-start | bytes 5111816 | tf_op jit(solution)/shard_map/ppermute | solution.py:18
  111.9 0.8 copy.24
  112.7 1.8 collective-permute-done
  114.5 2.2 select_bitcast_fusion.3
  116.9 0.6 copy-done.9
  118.5 1.9 convolution_select_fusion.1
  120.4 44.1 %all-to-all-done.5 = bf16[8,32,5120]{2,1,0:T(8,128)(2,1)} async-done(((bf16[8,32,5120]{2,1,0:T(8,128)(2,1)}), bf16[8,32,5120]{2,1,0:T(8,128)(2,1)}, u32[]{:S(2)}, u32[]{:S(2)}) %all-to-all-start.5) | async-done | bytes 2621472 | tf_op jit(solution)/shard_map/all_to_all | solution.py:14
  164.5 6.2 %collective-permute-start.1 = (bf16[8,32,5120]{2,1,0:T(8,128)(2,1)}, bf16[8,32,5120]{2,1,0:T(8,128)(2,1)}, u32[]{:S(2)}, u32[]{:S(2)}) collective-permute-start(bf16[8,32,5120]{2,1,0:T(8,128)(2,1)} %all-to-all-done.5), channel_id=1, source_target_pairs={{0,8},{8,0},{1,9},{9,1},{2,10},{10,2},{3,11},{11,3},{4,12},{12,4},... | collective-permute-start | bytes 7864328 | tf_op jit(solution)/shard_map/ppermute | solution.py:18
  170.9 1.5 copy.23
  172.4 4.3 %fusion.7 = f32[256,2048]{1,0:T(8,128)S(1)} fusion(s32[1024]{0:T(1024)S(1)} %bitcast.98, bf16[1024,1024]{1,0:T(8,128)(2,1)} %bitcast.84, f32[1024,256]{1,0:T(8,128)S(1)} %copy-done.12), kind=kOutput, calls=%fused_computation.12 | convolution fusion | flops 1613758464 | bytes 5246976 | tf_op jit(solution)/shard_map/dot_general | solution.py:24
  177.0 32.4 %all_to_all.35 = bf16[8,32,2048]{2,1,0:T(8,128)(2,1)S(1)} all-to-all(bf16[8,32,2048]{2,1,0:T(8,128)(2,1)S(1)} %bitcast.82), channel_id=1, replica_groups=mesh['zl'=4,'y'=8,'core'=2,'x'=4,'zh'=2] {'x','zh'}, dimensions={0} | all-to-all | bytes 2097152 | tf_op jit(solution)/shard_map/all_to_all | solution.py:75
  209.5 2.9 %select_bitcast_fusion.1 = (bf16[8,1,32,5120]{3,2,1,0:T(8,128)(2,1)S(1)}, bf16[8,1,32,5120]{3,2,1,0:T(8,128)(2,1)S(1)}) fusion(bf16[8,32,5120]{2,1,0:T(8,128)(2,1)} %all-to-all-done.5, bf16[8,32,5120]{2,1,0:T(8,128)(2,1)} %collective-permute-done.1, pred[]{:T(512)S(6)} %eq.19), kind=kLoop, calls=%fused_computation.14 | loop fusion | flops 2621440 | bytes 10485761 | tf_op jit(solution)/shard_map/stack | solution.py:20
  215.6 0.7 fusion.25
  216.4 28.5 %all_to_all.36 = bf16[8,32,2048]{2,1,0:T(8,128)(2,1)S(1)} all-to-all(bf16[8,32,2048]{2,1,0:T(8,128)(2,1)S(1)} %broadcast_in_dim.83), channel_id=1, replica_groups=mesh['zl'=4,'y'=8,'core'=2,'x'=4,'zh'=2] {'x','zh'}, dimensions={0} | all-to-all | bytes 2097152 | tf_op jit(solution)/shard_map/all_to_all | solution.py:14
  244.9 2.7 %fusion.21 = bf16[256,1024]{1,0:T(8,128)(2,1)} fusion(bf16[256,2048]{1,0:T(8,128)(2,1)S(1)} %bitcast.86, s32[1024]{0:T(1024)S(1)} %bitcast.99), kind=kOutput, calls=%fused_computation.36 | convolution fusion | flops 1076101120 | bytes 1576960 | tf_op jit(solution)/shard_map/dot_general | solution.py:24
  247.7 4.7 %fusion.18 = f32[1,1024,256]{2,1,0:T(8,128)} fusion(bf16[256,1024]{1,0:T(8,128)(2,1)} %fusion.21, bf16[1024,1024]{1,0:T(8,128)(2,1)S(1)} %bitcast.85, f32[1024,256]{1,0:T(8,128)} %convolution_select_fusion.1, pred[1024]{0:T(1024)(128)(4,1)S(1)} %iota_compare_fusion.11, bf16[256,512]{1,0:T(8,128)(2,1)} %bitcast.94, bf16[256,256]{1,0:T(8,128)(2,1)S(1)} %slice.146, ...), kind=kOutput, calls=%fused_computation.30 | convolution fusion | flops 1089470464 | bytes 6161408 | tf_op jit(solution)/shard_map/dot_general | solution.py:24
  252.4 0.8 copy.28
  (60 shorter events, 5.0 us)
Async XLA Ops:
  2.0 22.8 %all-to-all-start.3 = ((bf16[8,32,256]{2,1,0:T(8,128)(2,1)}), bf16[8,32,256]{2,1,0:T(8,128)(2,1)S(1)}, u32[]{:S(2)}, u32[]{:S(2)}) async-start(bf16[8,32,256]{2,1,0:T(8,128)(2,1)} %broadcast_in_dim.79), calls=%async_computation.3 | async-start | bytes 262144 | tf_op jit(solution)/shard_map/all_to_all | solution.py:14
  25.5 10.0 %all-to-all-start = ((bf16[4,32,1024]{2,1,0:T(8,128)(2,1)}), bf16[4,32,1024]{2,1,0:T(8,128)(2,1)S(1)}, u32[]{:S(2)}, u32[]{:S(2)}) async-start(bf16[4,32,1024]{2,1,0:T(8,128)(2,1)} %broadcast_in_dim.75), calls=%async_computation | async-start | bytes 524288 | tf_op jit(solution)/shard_map/all_to_all | solution.py:14
  36.4 14.3 %all-to-all-start.4 = ((bf16[4,32,2048]{2,1,0:T(8,128)(2,1)}), bf16[4,32,2048]{2,1,0:T(8,128)(2,1)S(1)}, u32[]{:S(2)}, u32[]{:S(2)}) async-start(bf16[4,32,2048]{2,1,0:T(8,128)(2,1)} %broadcast_in_dim.81), calls=%async_computation.4 | async-start | bytes 1048576 | tf_op jit(solution)/shard_map/all_to_all | solution.py:14
  52.1 46.7 %all-to-all-start.1 = ((bf16[8,104,1024]{2,1,0:T(8,128)(2,1)}), bf16[8,104,1024]{2,1,0:T(8,128)(2,1)S(1)}, u32[]{:S(2)}, u32[]{:S(2)}) async-start(bf16[8,104,1024]{2,1,0:T(8,128)(2,1)} %broadcast_in_dim.76), calls=%async_computation.1 | async-start | bytes 3407872 | tf_op jit(solution)/shard_map/all_to_all | solution.py:14
  98.8 6.6 %copy-start = (bf16[8,104,1024]{2,1,0:T(8,128)(2,1)}, bf16[8,104,1024]{2,1,0:T(8,128)(2,1)S(1)}, u32[]{:S(2)}) copy-start(bf16[8,104,1024]{2,1,0:T(8,128)(2,1)S(1)} %all-to-all-done.1) | copy-start | bytes 5111812
  100.8 11.0 %copy-start.8 = (f32[256,256]{1,0:T(8,128)S(1)}, f32[256,256]{1,0:T(8,128)}, u32[]{:S(2)}) copy-start(f32[256,256]{1,0:T(8,128)} %param.8) | copy-start | bytes 786436
  100.8 63.6 %all-to-all-start.5 = ((bf16[8,32,5120]{2,1,0:T(8,128)(2,1)}), bf16[8,32,5120]{2,1,0:T(8,128)(2,1)}, u32[]{:S(2)}, u32[]{:S(2)}) async-start(bf16[8,32,5120]{2,1,0:T(8,128)(2,1)} %broadcast_in_dim.82), calls=%async_computation.5 | async-start | bytes 5242880 | tf_op jit(solution)/shard_map/all_to_all | solution.py:14
  105.4 9.1 %collective-permute-start = (bf16[8,104,1024]{2,1,0:T(8,128)(2,1)S(1)}, bf16[8,104,1024]{2,1,0:T(8,128)(2,1)}, u32[]{:S(2)}, u32[]{:S(2)}) collective-permute-start(bf16[8,104,1024]{2,1,0:T(8,128)(2,1)S(1)} %all-to-all-done.1), channel_id=1, source_target_pairs={{0,8},{8,0},{1,9},{9,1},{2,10},{10,2},{3,11},{11,3},{4,12},{12,4},... | collective-permute-start | bytes 5111816 | tf_op jit(solution)/shard_map/ppermute | solution.py:18
  116.8 0.8 copy-start.3
  116.8 0.7 copy-start.9
  116.9 1.6 copy-start.10
  117.5 0.7 copy-start.7
  117.6 0.9 copy-start.5
  164.5 45.0 %collective-permute-start.1 = (bf16[8,32,5120]{2,1,0:T(8,128)(2,1)}, bf16[8,32,5120]{2,1,0:T(8,128)(2,1)}, u32[]{:S(2)}, u32[]{:S(2)}) collective-permute-start(bf16[8,32,5120]{2,1,0:T(8,128)(2,1)} %all-to-all-done.5), channel_id=1, source_target_pairs={{0,8},{8,0},{1,9},{9,1},{2,10},{10,2},{3,11},{11,3},{4,12},{12,4},... | collective-permute-start | bytes 7864328 | tf_op jit(solution)/shard_map/ppermute | solution.py:18
  170.9 1.5 copy-start.11
  170.9 1.5 copy-start.12
  172.4 4.3 %copy-start.2 = (f32[256,256]{0,1:T(8,128)S(1)}, f32[256,256]{0,1:T(8,128)}, u32[]{:S(2)}) copy-start(f32[256,256]{0,1:T(8,128)} %copy.24) | copy-start | bytes 786436
  244.9 2.7 %copy-start.1 = (bf16[8,2,4,16,1024]{4,3,1,0,2:T(8,128)(2,1)S(1)}, bf16[8,2,4,16,1024]{4,3,1,0,2:T(8,128)(2,1)}, u32[]{:S(2)}) copy-start(bf16[8,2,4,16,1024]{4,3,1,0,2:T(8,128)(2,1)} %copy.23) | copy-start | bytes 6291460
  244.9 2.7 %copy-start.4 = (bf16[8,2,16,1024]{3,2,1,0:T(8,128)(2,1)S(1)}, bf16[8,2,16,1024]{3,2,1,0:T(8,128)(2,1)}, u32[]{:S(2)}) copy-start(bf16[8,2,16,1024]{3,2,1,0:T(8,128)(2,1)} %copy-done.3) | copy-start | bytes 1572868
  244.9 2.8 %copy-start.6 = (bf16[256,1024]{1,0:T(8,128)(2,1)S(1)}, bf16[256,1024]{1,0:T(8,128)(2,1)}, u32[]{:S(2)}) copy-start(bf16[256,1024]{1,0:T(8,128)(2,1)} %copy-done.5) | copy-start | bytes 1572868

commit v2 on v1

--- a/solution.py
+++ b/solution.py
@@ -12,6 +12,25 @@
 
 def gather_blocks(x, axis, length):
     return lax.all_to_all(jnp.broadcast_to(x[None], (length, *x.shape)), axis, 0, 0, tiled=True)
+
+
+def ring(x):
+    forth = [(i, (i + 1) % Y) for i in range(Y)]
+    back = [(i, (i - 1) % Y) for i in range(Y)]
+    here = lax.axis_index("y")
+    blocks = jnp.zeros((Y, *x.shape), x.dtype)
+    place = lambda blocks, piece, at: lax.dynamic_update_slice(
+        blocks, piece[None], (lax.rem(here + at + Y, Y),) + (0,) * x.ndim
+    )
+    blocks = place(blocks, x, 0)
+    up = down = x
+    for step in range(1, Y // 2 + 1):
+        up = lax.ppermute(up, "y", forth)
+        blocks = place(blocks, up, -step)
+        if step < Y // 2:
+            down = lax.ppermute(down, "y", back)
+            blocks = place(blocks, down, step)
+    return blocks
 
 
 def both_cores(x):
@@ -39,13 +58,15 @@
     index = coupling_rows[0]
 
     pair = jnp.concatenate([child_inverse[0], coupling_block[0]], axis=0)
-    by_zl = gather_blocks(pair, "zl", ZL)
+    by_zl = gather_blocks(jnp.concatenate([pair, root_inverse.T], axis=1), "zl", ZL)
+    rt = by_zl[:, :, s1:]
+    by_zl = by_zl[:, :, :s1]
     cb = by_zl[:, r1:, :].reshape(ZL * r1, s1)
     tri_rows = jnp.concatenate(
         [by_zl[3, :r1], jnp.concatenate([by_zl[2, :r1, : 3 * q1], by_zl[0, :r1, :q1]], axis=1),
          jnp.concatenate([by_zl[1, : r1 // 2, : 2 * q1], by_zl[1, r1 // 2 : r1, : 2 * q1]], axis=1)], axis=0)
     packed = jnp.concatenate([cb, tri_rows], axis=0)
-    w = both_cores(gather_blocks(packed, "y", Y))
+    w = both_cores(ring(packed))
     nc = ZL * r1
     coupling = w[:, :, :nc].reshape(Y, CORE, ZL, r1, s1).transpose(2, 0, 1, 3, 4).reshape(k, s1)
     a3 = w[:, :, nc : nc + r1].reshape(q1, s1)
@@ -55,12 +76,9 @@
     pad = lambda m: jnp.pad(m, ((0, 0), (0, s1 - m.shape[1])))
     inverse = jnp.concatenate([pad(a20[:, 3 * q1 :]), pad(a1), pad(a20[:, : 3 * q1]), a3], axis=0)
 
-    rt = gather_blocks(root_inverse.T, SUB, X * ZH)
-    rc = rt.shape[1]
-    rt = rt.transpose(1, 0, 2).reshape(rc, s0)
-    rt = gather_blocks(rt, "zl", ZL)
-    rt = jnp.concatenate([rt[q, :, q * q0 :] for q in range(ZL)], axis=1)
-    rt = both_cores(gather_blocks(rt, "y", Y)).reshape(q0, -1)
+    rt = gather_blocks(rt, SUB, X * ZH)
+    rt = jnp.concatenate([rt[i, q] for q in range(ZL) for i in range(q * q0 // block, X * ZH)], axis=1)
+    rt = both_cores(ring(rt)).reshape(q0, -1)
     starts = [sum(s0 - p * q0 for p in range(q)) for q in range(ZL)]
     rts = [rt[:, starts[q] : starts[q] + s0 - q * q0] for q in range(ZL)]
 
@@ -72,8 +90,9 @@
     placed_t = -dot(update_t, onehot, 1, 0)
     mine = lax.dynamic_slice(placed_t, (0, sub * block), (n, block)) + root_rhs.T
     placed_t = lax.dynamic_update_slice(placed_t, mine, (0, sub * block))
-    parts = lax.all_to_all(placed_t.astype(BF).reshape(X * ZH, n // (X * ZH), s0), SUB, 0, 0, tiled=True)
-    s_t = jnp.sum(parts.astype(F32), axis=0).astype(BF)
+    parts = lax.all_to_all(placed_t.astype(BF).reshape(X, n // X, s0), "x", 0, 0, tiled=True)
+    part = jnp.sum(parts.astype(F32), axis=0)
+    s_t = (part + lax.ppermute(part.astype(BF), "zh", [(0, 1), (1, 0)]).astype(F32)).astype(BF)
 
     f_t = None
     for q in range(ZL):
@@ -81,7 +100,7 @@
         f_t = term if f_t is None else jnp.concatenate([f_t[:, : q * q0], f_t[:, q * q0 :] + term], axis=1)
     f_t = f_t.astype(BF)
     x_t = jnp.concatenate([dot(f_t[:, q * q0 :], rts[q], 1, 1) for q in range(ZL)], axis=1)
-    x_all = gather_blocks(x_t.astype(BF), SUB, X * ZH).reshape(n, s0)
+    x_all = gather_blocks(x_t.astype(BF), "x", X).reshape(n, s0)
     root_out = lax.dynamic_slice(x_all, (0, sub * block), (n, block)).T.astype(F32)
 
     picked_t = dot(x_all, onehot, 1, 1).astype(BF)

time: 257 us -> 206 us (0.80)
  the two profiles are of different devices: /device:TPU:1 before, /device:TPU:64 now
where the time goes in v2:
time: 206 us; the launch traced here: 204 us
  starting transfers between devices  75.7 us (37%)
  waiting for transfers between devices  47.5 us (23%)
  blocking collectives  36.7 us (18%)
  matrix products  18.6 us (9%)
  local copies, waits for them, and re-layouts  13.5 us (7%)
  other arithmetic  10.4 us (5%)
    ppermute x8, waiting for transfers between devices, ring(): up = lax.ppermute(up, 'y', forth)  30.6 us
    ppermute x6, starting transfers between devices, ring(): down = lax.ppermute(down, 'y', back)  29.4 us
    all_to_all x1, blocking collectives, on_device(): lax.all_to_all(placed_t.astype(BF).reshape(X, n // X, s0), 'x', 0, 0, til...  20.3 us
    dot_general x12, matrix products, dot(): lax.dot_general(a, b, (((ca,), (cb,)), ((), ())), preferred_element_type=...  18.6 us
    all_to_all x2, starting transfers between devices, gather_blocks(): lax.all_to_all(jnp.broadcast_to(x[None], (length, *x.shape)), axis, 0, 0,...  18.5 us
    ppermute x8, starting transfers between devices, ring(): up = lax.ppermute(up, 'y', forth)  16.7 us
    all_to_all x1, blocking collectives, gather_blocks(): lax.all_to_all(jnp.broadcast_to(x[None], (length, *x.shape)), axis, 0, 0,...  16.4 us
    ppermute x1, waiting for transfers between devices, on_device(): lax.ppermute(part.astype(BF), 'zh', [(0, 1), (1, 0)]).astype(F32)  11.8 us
  transfers between devices with their start and end apart: 19, of which 9 were waited for; matrix products, arithmetic and copies ran while one was open for 12% of the time, Pallas kernels for 0%

profile of v2, /device:TPU:64, one launch (start us, length us, event | category | flops | bytes accessed | tf_op | source)
XLA Modules:
  0.0 204.5 jit_solution(5781146925534772164)
XLA Ops:
  2.2 8.4 %all-to-all-start = ((bf16[4,32,1280]{2,1,0:T(8,128)(2,1)}), bf16[4,32,1280]{2,1,0:T(8,128)(2,1)S(1)}, u32[]{:S(2)}, u32[]{:S(2)}) async-start(bf16[4,32,1280]{2,1,0:T(8,128)(2,1)} %broadcast_in_dim.111), calls=%async_computation | async-start | bytes 655360 | tf_op jit(solution)/shard_map/all_to_all | solution.py:14
  12.4 5.1 %all-to-all-done = bf16[4,32,1280]{2,1,0:T(8,128)(2,1)S(1)} async-done(((bf16[4,32,1280]{2,1,0:T(8,128)(2,1)}), bf16[4,32,1280]{2,1,0:T(8,128)(2,1)S(1)}, u32[]{:S(2)}, u32[]{:S(2)}) %all-to-all-start) | async-done | bytes 327712 | tf_op jit(solution)/shard_map/all_to_all | solution.py:14
  17.5 3.2 %collective-permute-start = (bf16[104,1024]{1,0:T(8,128)(2,1)S(1)}, bf16[104,1024]{1,0:T(8,128)(2,1)S(1)}, u32[]{:S(2)}, u32[]{:S(2)}) collective-permute-start(bf16[104,1024]{1,0:T(8,128)(2,1)S(1)} %maximum_maximum_fusion), channel_id=1, source_target_pairs={{0,16},{16,32},{32,48},{48,64},{64,80},{80,96},{96,112},{112,0},{1... | collective-permute-start | bytes 638984 | tf_op jit(solution)/shard_map/ppermute | solution.py:28
  20.7 3.9 %collective-permute-start.1 = (bf16[104,1024]{1,0:T(8,128)(2,1)S(1)}, bf16[104,1024]{1,0:T(8,128)(2,1)S(1)}, u32[]{:S(2)}, u32[]{:S(2)}) collective-permute-start(bf16[104,1024]{1,0:T(8,128)(2,1)S(1)} %maximum_maximum_fusion), channel_id=1, source_target_pairs={{0,112},{16,0},{32,16},{48,32},{64,48},{80,64},{96,80},{112,96},{1... | collective-permute-start | bytes 638984 | tf_op jit(solution)/shard_map/ppermute | solution.py:31
  25.5 10.0 %all-to-all-start.2 = ((bf16[8,4,32,256]{3,2,1,0:T(8,128)(2,1)}), bf16[8,4,32,256]{3,2,1,0:T(8,128)(2,1)S(1)}, u32[]{:S(2)}, u32[]{:S(2)}) async-start(bf16[8,4,32,256]{3,2,1,0:T(8,128)(2,1)} %broadcast_in_dim.123), calls=%async_computation.2 | async-start | bytes 1048576 | tf_op jit(solution)/shard_map/all_to_all | solution.py:14
  37.7 2.0 collective-permute-start.2
  39.7 5.0 %collective-permute-start.3 = (bf16[104,1024]{1,0:T(8,128)(2,1)S(1)}, bf16[104,1024]{1,0:T(8,128)(2,1)S(1)}, u32[]{:S(2)}, u32[]{:S(2)}) collective-permute-start(bf16[104,1024]{1,0:T(8,128)(2,1)S(1)} %collective-permute-done.1), channel_id=1, source_target_pairs={{0,112},{16,0},{32,16},{48,32},{64,48},{80,64},{96,80},{112,96},{1... | collective-permute-start | bytes 638984 | tf_op jit(solution)/shard_map/ppermute | solution.py:31
  46.6 1.9 collective-permute-start.4
  48.5 5.1 %collective-permute-start.5 = (bf16[104,1024]{1,0:T(8,128)(2,1)S(1)}, bf16[104,1024]{1,0:T(8,128)(2,1)S(1)}, u32[]{:S(2)}, u32[]{:S(2)}) collective-permute-start(bf16[104,1024]{1,0:T(8,128)(2,1)S(1)} %collective-permute-done.3), channel_id=1, source_target_pairs={{0,112},{16,0},{32,16},{48,32},{64,48},{80,64},{96,80},{112,96},{1... | collective-permute-start | bytes 638984 | tf_op jit(solution)/shard_map/ppermute | solution.py:31
  55.5 1.9 collective-permute-start.6
  58.9 5.6 %collective-permute-done.6 = bf16[104,1024]{1,0:T(8,128)(2,1)S(1)} collective-permute-done((bf16[104,1024]{1,0:T(8,128)(2,1)S(1)}, bf16[104,1024]{1,0:T(8,128)(2,1)S(1)}, u32[]{:S(2)}, u32[]{:S(2)}) %collective-permute-start.6) | collective-permute-done | bytes 213024 | tf_op jit(solution)/shard_map/ppermute | solution.py:28
  65.2 1.9 collective-permute-start.7
  67.3 1.9 collective-permute-start.9
  69.3 5.1 %collective-permute-start.10 = (bf16[32,5120]{1,0:T(8,128)(2,1)S(1)}, bf16[32,5120]{1,0:T(8,128)(2,1)S(1)}, u32[]{:S(2)}, u32[]{:S(2)}) collective-permute-start(bf16[32,5120]{1,0:T(8,128)(2,1)S(1)} %constant_dynamic-update-slice_fusion), channel_id=1, source_target_pairs={{0,112},{16,0},{32,16},{48,32},{64,48},{80,64},{96,80},{112,96},{1... | collective-permute-start | bytes 983048 | tf_op jit(solution)/shard_map/ppermute | solution.py:31
  74.7 5.8 %collective-permute-done.9 = bf16[32,5120]{1,0:T(8,128)(2,1)S(1)} collective-permute-done((bf16[32,5120]{1,0:T(8,128)(2,1)S(1)}, bf16[32,5120]{1,0:T(8,128)(2,1)S(1)}, u32[]{:S(2)}, u32[]{:S(2)}) %collective-permute-start.9) | collective-permute-done | bytes 327712 | tf_op jit(solution)/shard_map/ppermute | solution.py:28
  80.6 1.9 collective-permute-start.11
  82.5 5.1 %collective-permute-start.12 = (bf16[32,5120]{1,0:T(8,128)(2,1)S(1)}, bf16[32,5120]{1,0:T(8,128)(2,1)S(1)}, u32[]{:S(2)}, u32[]{:S(2)}) collective-permute-start(bf16[32,5120]{1,0:T(8,128)(2,1)S(1)} %collective-permute-done.10), channel_id=1, source_target_pairs={{0,112},{16,0},{32,16},{48,32},{64,48},{80,64},{96,80},{112,96},{1... | collective-permute-start | bytes 983048 | tf_op jit(solution)/shard_map/ppermute | solution.py:31
  87.7 5.3 %collective-permute-done.11 = bf16[32,5120]{1,0:T(8,128)(2,1)S(1)} collective-permute-done((bf16[32,5120]{1,0:T(8,128)(2,1)S(1)}, bf16[32,5120]{1,0:T(8,128)(2,1)S(1)}, u32[]{:S(2)}, u32[]{:S(2)}) %collective-permute-start.11) | collective-permute-done | bytes 327712 | tf_op jit(solution)/shard_map/ppermute | solution.py:28
  93.0 1.9 collective-permute-start.13
  95.0 5.1 %collective-permute-start.14 = (bf16[32,5120]{1,0:T(8,128)(2,1)S(1)}, bf16[32,5120]{1,0:T(8,128)(2,1)S(1)}, u32[]{:S(2)}, u32[]{:S(2)}) collective-permute-start(bf16[32,5120]{1,0:T(8,128)(2,1)S(1)} %collective-permute-done.12), channel_id=1, source_target_pairs={{0,112},{16,0},{32,16},{48,32},{64,48},{80,64},{96,80},{112,96},{1... | collective-permute-start | bytes 983048 | tf_op jit(solution)/shard_map/ppermute | solution.py:31
  100.1 4.4 %collective-permute-done.13 = bf16[32,5120]{1,0:T(8,128)(2,1)S(1)} collective-permute-done((bf16[32,5120]{1,0:T(8,128)(2,1)S(1)}, bf16[32,5120]{1,0:T(8,128)(2,1)S(1)}, u32[]{:S(2)}, u32[]{:S(2)}) %collective-permute-start.13) | collective-permute-done | bytes 327712 | tf_op jit(solution)/shard_map/ppermute | solution.py:28
  106.5 8.6 %collective-permute-done.15 = bf16[32,5120]{1,0:T(8,128)(2,1)S(1)} collective-permute-done((bf16[32,5120]{1,0:T(8,128)(2,1)S(1)}, bf16[32,5120]{1,0:T(8,128)(2,1)S(1)}, u32[]{:S(2)}, u32[]{:S(2)}) %collective-permute-start.15) | collective-permute-done | bytes 327712 | tf_op jit(solution)/shard_map/ppermute | solution.py:28
  115.2 1.9 collective-permute-start.16
  117.1 2.2 %select_bitcast_fusion.3 = (bf16[8,1,104,1024]{3,2,1,0:T(8,128)(2,1)S(1)}, bf16[8,1,104,1024]{3,2,1,0:T(8,128)(2,1)S(1)}) fusion(bf16[8,104,1024]{2,1,0:T(8,128)(2,1)} %bitcast_dynamic-update-slice_fusion.8, bf16[8,104,1024]{2,1,0:T(8,128)(2,1)} %collective-permute-done.7, pred[]{:T(512)S(6)} %eq.19), kind=kLoop, calls=%fused_computation.26 | loop fusion | flops 1703936 | bytes 6815745 | tf_op jit(solution)/shard_map/stack | solution.py:39
  124.5 5.9 %fusion.7 = f32[256,2048]{1,0:T(8,128)} fusion(s32[1024]{0:T(1024)S(1)} %bitcast.198, bf16[1024,1024]{1,0:T(8,128)(2,1)} %bitcast.185, f32[1024,256]{1,0:T(8,128)} %convolution_select_fusion.1), kind=kOutput, calls=%fused_computation.12 | convolution fusion | flops 1613758464 | bytes 5246976 | tf_op jit(solution)/shard_map/dot_general | solution.py:43
  133.8 20.3 %all_to_all.20 = bf16[4,64,2048]{2,1,0:T(8,128)(2,1)S(1)} all-to-all(bf16[4,64,2048]{2,1,0:T(8,128)(2,1)S(1)} %bitcast.183), channel_id=1, replica_groups=mesh['zl'=4,'y'=8,'core'=2,'x'=4,'zh'=2] {'x'}, dimensions={0} | all-to-all | bytes 2097152 | tf_op jit(solution)/shard_map/all_to_all | solution.py:93
  154.4 7.3 %collective-permute-start.8 = (bf16[64,2048]{1,0:T(8,128)(2,1)S(1)}, bf16[64,2048]{1,0:T(8,128)(2,1)S(1)}, u32[]{:S(2)}, u32[]{:S(2)}) collective-permute-start(bf16[64,2048]{1,0:T(8,128)(2,1)S(1)} %convert_element_type.54), channel_id=1, source_target_pairs={{0,1},{1,0},{2,3},{3,2},{4,5},{5,4},{6,7},{7,6},{8,9},{9,8},{10,11... | collective-permute-start | bytes 786440 | tf_op jit(solution)/shard_map/ppermute | solution.py:95
  161.6 11.8 %collective-permute-done.8 = bf16[64,2048]{1,0:T(8,128)(2,1)S(1)} collective-permute-done((bf16[64,2048]{1,0:T(8,128)(2,1)S(1)}, bf16[64,2048]{1,0:T(8,128)(2,1)S(1)}, u32[]{:S(2)}, u32[]{:S(2)}) %collective-permute-start.8) | collective-permute-done | bytes 262176 | tf_op jit(solution)/shard_map/ppermute | solution.py:95
  173.5 2.1 %select_bitcast_fusion.1 = (bf16[8,1,32,5120]{3,2,1,0:T(8,128)(2,1)S(1)}, bf16[8,1,32,5120]{3,2,1,0:T(8,128)(2,1)S(1)}) fusion(bf16[8,32,5120]{2,1,0:T(8,128)(2,1)S(1)} %bitcast_dynamic-update-slice_fusion, bf16[8,32,5120]{2,1,0:T(8,128)(2,1)} %collective-permute-done.16, pred[]{:T(512)S(6)} %eq.19), kind=kLoop, calls=%fused_computation.14 | loop fusion | flops 2621440 | bytes 10485761 | tf_op jit(solution)/shard_map/stack | solution.py:39
  179.8 16.4 %all_to_all.21 = bf16[4,64,2048]{2,1,0:T(8,128)(2,1)S(1)} all-to-all(bf16[4,64,2048]{2,1,0:T(8,128)(2,1)S(1)} %broadcast_in_dim.132), channel_id=1, replica_groups=mesh['zl'=4,'y'=8,'core'=2,'x'=4,'zh'=2] {'x'}, dimensions={0} | all-to-all | bytes 2097152 | tf_op jit(solution)/shard_map/all_to_all | solution.py:14
  196.2 2.7 %fusion.21 = bf16[256,1024]{1,0:T(8,128)(2,1)} fusion(bf16[256,2048]{1,0:T(8,128)(2,1)S(1)} %bitcast.187, s32[1024]{0:T(1024)S(1)} %bitcast.199), kind=kOutput, calls=%fused_computation.37 | convolution fusion | flops 1076101120 | bytes 1576960 | tf_op jit(solution)/shard_map/dot_general | solution.py:43
  198.9 4.7 %fusion.18 = f32[1,1024,256]{2,1,0:T(8,128)} fusion(bf16[256,1024]{1,0:T(8,128)(2,1)} %fusion.21, bf16[1024,1024]{1,0:T(8,128)(2,1)S(1)} %bitcast.186, f32[1024,256]{1,0:T(8,128)} %convolution_select_fusion.1, pred[1024]{0:T(1024)(128)(4,1)S(1)} %iota_compare_fusion.11, bf16[256,512]{1,0:T(8,128)(2,1)} %bitcast.194, bf16[256,256]{1,0:T(8,128)(2,1)S(1)} %slice.221, ...), kind=kOutput, calls=%fused_computation.31 | convolution fusion | flops 1089470464 | bytes 6161408 | tf_op jit(solution)/shard_map/dot_general | solution.py:43
  (104 shorter events, 27.8 us)
Async XLA Ops:
  2.2 15.3 %all-to-all-start = ((bf16[4,32,1280]{2,1,0:T(8,128)(2,1)}), bf16[4,32,1280]{2,1,0:T(8,128)(2,1)S(1)}, u32[]{:S(2)}, u32[]{:S(2)}) async-start(bf16[4,32,1280]{2,1,0:T(8,128)(2,1)} %broadcast_in_dim.111), calls=%async_computation | async-start | bytes 655360 | tf_op jit(solution)/shard_map/all_to_all | solution.py:14
  17.5 20.1 %collective-permute-start = (bf16[104,1024]{1,0:T(8,128)(2,1)S(1)}, bf16[104,1024]{1,0:T(8,128)(2,1)S(1)}, u32[]{:S(2)}, u32[]{:S(2)}) collective-permute-start(bf16[104,1024]{1,0:T(8,128)(2,1)S(1)} %maximum_maximum_fusion), channel_id=1, source_target_pairs={{0,16},{16,32},{32,48},{48,64},{64,80},{80,96},{96,112},{112,0},{1... | collective-permute-start | bytes 638984 | tf_op jit(solution)/shard_map/ppermute | solution.py:28
  20.7 18.9 %collective-permute-start.1 = (bf16[104,1024]{1,0:T(8,128)(2,1)S(1)}, bf16[104,1024]{1,0:T(8,128)(2,1)S(1)}, u32[]{:S(2)}, u32[]{:S(2)}) collective-permute-start(bf16[104,1024]{1,0:T(8,128)(2,1)S(1)} %maximum_maximum_fusion), channel_id=1, source_target_pairs={{0,112},{16,0},{32,16},{48,32},{64,48},{80,64},{96,80},{112,96},{1... | collective-permute-start | bytes 638984 | tf_op jit(solution)/shard_map/ppermute | solution.py:31
  25.5 41.6 %all-to-all-start.2 = ((bf16[8,4,32,256]{3,2,1,0:T(8,128)(2,1)}), bf16[8,4,32,256]{3,2,1,0:T(8,128)(2,1)S(1)}, u32[]{:S(2)}, u32[]{:S(2)}) async-start(bf16[8,4,32,256]{3,2,1,0:T(8,128)(2,1)} %broadcast_in_dim.123), calls=%async_computation.2 | async-start | bytes 1048576 | tf_op jit(solution)/shard_map/all_to_all | solution.py:14
  37.7 8.9 %collective-permute-start.2 = (bf16[104,1024]{1,0:T(8,128)(2,1)S(1)}, bf16[104,1024]{1,0:T(8,128)(2,1)S(1)}, u32[]{:S(2)}, u32[]{:S(2)}) collective-permute-start(bf16[104,1024]{1,0:T(8,128)(2,1)S(1)} %collective-permute-done), channel_id=1, source_target_pairs={{0,16},{16,32},{32,48},{48,64},{64,80},{80,96},{96,112},{112,0},{1... | collective-permute-start | bytes 638984 | tf_op jit(solution)/shard_map/ppermute | solution.py:28
  39.7 8.8 %collective-permute-start.3 = (bf16[104,1024]{1,0:T(8,128)(2,1)S(1)}, bf16[104,1024]{1,0:T(8,128)(2,1)S(1)}, u32[]{:S(2)}, u32[]{:S(2)}) collective-permute-start(bf16[104,1024]{1,0:T(8,128)(2,1)S(1)} %collective-permute-done.1), channel_id=1, source_target_pairs={{0,112},{16,0},{32,16},{48,32},{64,48},{80,64},{96,80},{112,96},{1... | collective-permute-start | bytes 638984 | tf_op jit(solution)/shard_map/ppermute | solution.py:31
  46.6 8.9 %collective-permute-start.4 = (bf16[104,1024]{1,0:T(8,128)(2,1)S(1)}, bf16[104,1024]{1,0:T(8,128)(2,1)S(1)}, u32[]{:S(2)}, u32[]{:S(2)}) collective-permute-start(bf16[104,1024]{1,0:T(8,128)(2,1)S(1)} %collective-permute-done.2), channel_id=1, source_target_pairs={{0,16},{16,32},{32,48},{48,64},{64,80},{80,96},{96,112},{112,0},{1... | collective-permute-start | bytes 638984 | tf_op jit(solution)/shard_map/ppermute | solution.py:28
  48.5 9.6 %collective-permute-start.5 = (bf16[104,1024]{1,0:T(8,128)(2,1)S(1)}, bf16[104,1024]{1,0:T(8,128)(2,1)S(1)}, u32[]{:S(2)}, u32[]{:S(2)}) collective-permute-start(bf16[104,1024]{1,0:T(8,128)(2,1)S(1)} %collective-permute-done.3), channel_id=1, source_target_pairs={{0,112},{16,0},{32,16},{48,32},{64,48},{80,64},{96,80},{112,96},{1... | collective-permute-start | bytes 638984 | tf_op jit(solution)/shard_map/ppermute | solution.py:31
  55.5 8.9 %collective-permute-start.6 = (bf16[104,1024]{1,0:T(8,128)(2,1)S(1)}, bf16[104,1024]{1,0:T(8,128)(2,1)S(1)}, u32[]{:S(2)}, u32[]{:S(2)}) collective-permute-start(bf16[104,1024]{1,0:T(8,128)(2,1)S(1)} %collective-permute-done.4), channel_id=1, source_target_pairs={{0,16},{16,32},{32,48},{48,64},{64,80},{80,96},{96,112},{112,0},{1... | collective-permute-start | bytes 638984 | tf_op jit(solution)/shard_map/ppermute | solution.py:28
  65.2 51.9 %collective-permute-start.7 = (bf16[8,104,1024]{2,1,0:T(8,128)(2,1)}, bf16[8,104,1024]{2,1,0:T(8,128)(2,1)}, u32[]{:S(2)}, u32[]{:S(2)}) collective-permute-start(bf16[8,104,1024]{2,1,0:T(8,128)(2,1)} %bitcast_dynamic-update-slice_fusion.8), channel_id=1, source_target_pairs={{0,8},{8,0},{1,9},{9,1},{2,10},{10,2},{3,11},{11,3},{4,12},{12,4},... | collective-permute-start | bytes 5111816 | tf_op jit(solution)/shard_map/ppermute | solution.py:37
  67.3 13.2 %collective-permute-start.9 = (bf16[32,5120]{1,0:T(8,128)(2,1)S(1)}, bf16[32,5120]{1,0:T(8,128)(2,1)S(1)}, u32[]{:S(2)}, u32[]{:S(2)}) collective-permute-start(bf16[32,5120]{1,0:T(8,128)(2,1)S(1)} %constant_dynamic-update-slice_fusion), channel_id=1, source_target_pairs={{0,16},{16,32},{32,48},{48,64},{64,80},{80,96},{96,112},{112,0},{1... | collective-permute-start | bytes 983048 | tf_op jit(solution)/shard_map/ppermute | solution.py:28
  69.3 13.2 %collective-permute-start.10 = (bf16[32,5120]{1,0:T(8,128)(2,1)S(1)}, bf16[32,5120]{1,0:T(8,128)(2,1)S(1)}, u32[]{:S(2)}, u32[]{:S(2)}) collective-permute-start(bf16[32,5120]{1,0:T(8,128)(2,1)S(1)} %constant_dynamic-update-slice_fusion), channel_id=1, source_target_pairs={{0,112},{16,0},{32,16},{48,32},{64,48},{80,64},{96,80},{112,96},{1... | collective-permute-start | bytes 983048 | tf_op jit(solution)/shard_map/ppermute | solution.py:31
  80.6 12.4 %collective-permute-start.11 = (bf16[32,5120]{1,0:T(8,128)(2,1)S(1)}, bf16[32,5120]{1,0:T(8,128)(2,1)S(1)}, u32[]{:S(2)}, u32[]{:S(2)}) collective-permute-start(bf16[32,5120]{1,0:T(8,128)(2,1)S(1)} %collective-permute-done.9), channel_id=1, source_target_pairs={{0,16},{16,32},{32,48},{48,64},{64,80},{80,96},{96,112},{112,0},{1... | collective-permute-start | bytes 983048 | tf_op jit(solution)/shard_map/ppermute | solution.py:28
  82.5 12.4 %collective-permute-start.12 = (bf16[32,5120]{1,0:T(8,128)(2,1)S(1)}, bf16[32,5120]{1,0:T(8,128)(2,1)S(1)}, u32[]{:S(2)}, u32[]{:S(2)}) collective-permute-start(bf16[32,5120]{1,0:T(8,128)(2,1)S(1)} %collective-permute-done.10), channel_id=1, source_target_pairs={{0,112},{16,0},{32,16},{48,32},{64,48},{80,64},{96,80},{112,96},{1... | collective-permute-start | bytes 983048 | tf_op jit(solution)/shard_map/ppermute | solution.py:31
  93.0 11.5 %collective-permute-start.13 = (bf16[32,5120]{1,0:T(8,128)(2,1)S(1)}, bf16[32,5120]{1,0:T(8,128)(2,1)S(1)}, u32[]{:S(2)}, u32[]{:S(2)}) collective-permute-start(bf16[32,5120]{1,0:T(8,128)(2,1)S(1)} %collective-permute-done.11), channel_id=1, source_target_pairs={{0,16},{16,32},{32,48},{48,64},{64,80},{80,96},{96,112},{112,0},{1... | collective-permute-start | bytes 983048 | tf_op jit(solution)/shard_map/ppermute | solution.py:28
  95.0 11.5 %collective-permute-start.14 = (bf16[32,5120]{1,0:T(8,128)(2,1)S(1)}, bf16[32,5120]{1,0:T(8,128)(2,1)S(1)}, u32[]{:S(2)}, u32[]{:S(2)}) collective-permute-start(bf16[32,5120]{1,0:T(8,128)(2,1)S(1)} %collective-permute-done.12), channel_id=1, source_target_pairs={{0,112},{16,0},{32,16},{48,32},{64,48},{80,64},{96,80},{112,96},{1... | collective-permute-start | bytes 983048 | tf_op jit(solution)/shard_map/ppermute | solution.py:31
  104.5 10.6 %collective-permute-start.15 = (bf16[32,5120]{1,0:T(8,128)(2,1)S(1)}, bf16[32,5120]{1,0:T(8,128)(2,1)S(1)}, u32[]{:S(2)}, u32[]{:S(2)}) collective-permute-start(bf16[32,5120]{1,0:T(8,128)(2,1)S(1)} %collective-permute-done.13), channel_id=1, source_target_pairs={{0,16},{16,32},{32,48},{48,64},{64,80},{80,96},{96,112},{112,0},{1... | collective-permute-start | bytes 983048 | tf_op jit(solution)/shard_map/ppermute | solution.py:28
  115.2 58.3 %collective-permute-start.16 = (bf16[8,32,5120]{2,1,0:T(8,128)(2,1)S(1)}, bf16[8,32,5120]{2,1,0:T(8,128)(2,1)}, u32[]{:S(2)}, u32[]{:S(2)}) collective-permute-start(bf16[8,32,5120]{2,1,0:T(8,128)(2,1)S(1)} %bitcast_dynamic-update-slice_fusion), channel_id=1, source_target_pairs={{0,8},{8,0},{1,9},{9,1},{2,10},{10,2},{3,11},{11,3},{4,12},{12,4},... | collective-permute-start | bytes 7864328 | tf_op jit(solution)/shard_map/ppermute | solution.py:37
  119.3 0.8 copy-start.3
  119.3 0.7 copy-start.4
  119.4 1.6 copy-start.5
  120.1 0.8 copy-start.1
  122.9 1.6 copy-start.6
  154.4 19.1 %collective-permute-start.8 = (bf16[64,2048]{1,0:T(8,128)(2,1)S(1)}, bf16[64,2048]{1,0:T(8,128)(2,1)S(1)}, u32[]{:S(2)}, u32[]{:S(2)}) collective-permute-start(bf16[64,2048]{1,0:T(8,128)(2,1)S(1)} %convert_element_type.54), channel_id=1, source_target_pairs={{0,1},{1,0},{2,3},{3,2},{4,5},{5,4},{6,7},{7,6},{8,9},{9,8},{10,11... | collective-permute-start | bytes 786440 | tf_op jit(solution)/shard_map/ppermute | solution.py:95
  196.2 2.7 %copy-start = (bf16[8,2,4,16,1024]{4,3,1,0,2:T(8,128)(2,1)S(1)}, bf16[8,2,4,16,1024]{4,3,1,0,2:T(8,128)(2,1)}, u32[]{:S(2)}) copy-start(bf16[8,2,4,16,1024]{4,3,1,0,2:T(8,128)(2,1)} %copy.12) | copy-start | bytes 6291460
  196.2 2.7 %copy-start.2 = (bf16[256,1024]{1,0:T(8,128)(2,1)S(1)}, bf16[256,1024]{1,0:T(8,128)(2,1)}, u32[]{:S(2)}) copy-start(bf16[256,1024]{1,0:T(8,128)(2,1)} %copy-done.1) | copy-start | bytes 1572868

commit v3 on v1

v3 whole, which is shorter than its diff:
```python
import jax
import jax.numpy as jnp
from jax import lax
from jax.experimental import pallas as pl
from jax.experimental.pallas import tpu as pltpu
from jax.sharding import Mesh, PartitionSpec as P

ZL, Y, CORE, X, ZH = 4, 8, 2, 4, 2
SRC = ("zl", "y", "core")
SUB = ("x", "zh")
BF = jnp.bfloat16
F32 = jnp.float32
FORTH = [(i, (i + 1) % Y) for i in range(Y)]
BACK = [(i, (i - 1) % Y) for i in range(Y)]
SWAP = [(0, 1), (1, 0)]
FIRST = Y // 2


def gather_blocks(x, axis, length):
    return lax.all_to_all(jnp.broadcast_to(x[None], (length, *x.shape)), axis, 0, 0, tiled=True)


def after(x, *others):
    return lax.optimization_barrier((x, *others))[0]


def dot(a, b, ca=1, cb=0):
    return lax.dot_general(a, b, (((ca,), (cb,)), ((), ())), preferred_element_type=F32)


def onehot(idx_ref, at, width):
    k = idx_ref.shape[0]
    cols = lax.broadcasted_iota(jnp.int32, (k, width), 1) + at
    return jnp.where(idx_ref[...] == cols, 1.0, 0.0).astype(BF)


def by_core(core, mine_ref, other_ref, put):
    @pl.when(core == 0)
    def _():
        put(mine_ref, 0)
        put(other_ref, 1)

    @pl.when(core != 0)
    def _():
        put(other_ref, 0)
        put(mine_ref, 1)


def forward_kernel(
    place_ref, mine_ref, other_ref, rhs_ref, root_ref, idx_ref,
    placed_ref, solved_ref, a_ref, c_ref,
):
    here, core, sub, order = (place_ref[i] for i in range(4))
    s1, n = rhs_ref.shape
    r1 = mine_ref.shape[1]
    q1 = s1 // ZL
    block = root_ref.shape[0]

    def put(blocks_ref, c):
        for j in range(Y):
            y = lax.rem(here + (j - FIRST + Y), Y)
            at = pl.multiple_of(y * (CORE * r1), CORE * r1) + c * r1
            for q in range(ZL):
                c_ref[pl.ds(q * q1 + at, r1), :] = blocks_ref[j, :, q * s1 : (q + 1) * s1]
            left = ZL * s1
            for q in reversed(range(ZL)):
                width = (q + 1) * q1
                a_ref[pl.ds(q * q1 + at, r1), :width] = blocks_ref[j, :, left : left + width]
                left += width

    by_core(core, mine_ref, other_ref, put)
    rows = lax.broadcasted_iota(jnp.int32, (s1, n), 0)
    source = jnp.where(rows < order, rhs_ref[...], 0.0).astype(BF)
    for q in range(ZL):
        top = (q + 1) * q1
        part = dot(a_ref[q * q1 : top, :top], source[:top])
        part = jnp.where(rows[q * q1 : top] < order, part, 0.0)
        solved_ref[:, q * q1 : top] = part.T
    update = dot(solved_ref[...].astype(BF), c_ref[...], 1, 1).astype(BF)
    root = root_ref[...].T
    for b in range(placed_ref.shape[1] // block):
        part = dot(update, onehot(idx_ref, b * block, block))
        placed_ref[:, b * block : (b + 1) * block] = (
            jnp.where(sub == b, root, 0.0) - part
        ).astype(BF)


def root_kernel(place_ref, s_ref, mine_ref, other_ref, last_ref, far_ref, out_ref, r_ref, f_ref):
    here, core = place_ref[0], place_ref[1]
    s0 = s_ref.shape[1]
    q0 = s0 // ZL
    rc = mine_ref.shape[1]

    def rows(j, c):
        y = lax.rem(here + (j - FIRST + Y), Y)
        return pl.ds(pl.multiple_of(y * (CORE * rc), CORE * rc) + c * rc, rc)

    def put(blocks_ref, c):
        for j in range(1, Y):
            r_ref[rows(j, c), :] = blocks_ref[j - 1]

    def put_last(block_ref, c):
        r_ref[rows(0, c), :] = block_ref[...]

    by_core(core, mine_ref, other_ref, put)
    by_core(core, last_ref, far_ref, put_last)
    left = 0
    spans = []
    for q in range(ZL):
        spans.append((left, left + s0 - q * q0))
        left = spans[-1][1]
    for q in range(ZL):
        term = dot(s_ref[:, q * q0 : (q + 1) * q0], r_ref[:, spans[q][0] : spans[q][1]])
        f_ref[:, q * q0 :] = term if q == 0 else f_ref[:, q * q0 :] + term
    f = f_ref[...].astype(BF)
    for q in range(ZL):
        part = dot(f[:, q * q0 :], r_ref[:, spans[q][0] : spans[q][1]], 1, 1).astype(BF)
        for i in range(out_ref.shape[0]):
            out_ref[i, :, q * q0 : (q + 1) * q0] = part


def backward_kernel(place_ref, x_ref, solved_ref, a_ref, c_ref, idx_ref, out_ref, root_ref):
    sub, order = place_ref[2], place_ref[3]
    n, s1 = solved_ref.shape
    q1 = s1 // ZL
    block = root_ref.shape[0]
    picked = None
    for b in range(x_ref.shape[1] // block):
        part = dot(x_ref[:, b * block : (b + 1) * block], onehot(idx_ref, b * block, block), 1, 1)
        picked = part if picked is None else picked + part
    pulled = dot(picked.astype(BF), c_ref[...])
    cols = lax.broadcasted_iota(jnp.int32, (n, s1), 1)
    residue = jnp.where(cols < order, solved_ref[...] - pulled, 0.0).astype(BF)
    rows = lax.broadcasted_iota(jnp.int32, (q1, n), 0)
    for q in range(ZL):
        part = dot(residue[:, q * q1 :], a_ref[q * q1 :, q * q1 : (q + 1) * q1])
        out_ref[q * q1 : (q + 1) * q1, :] = jnp.where(rows + q * q1 < order, part.T, 0.0)
    at = pl.multiple_of(sub * block, block)
    root_ref[...] = x_ref[:, pl.ds(at, block)].astype(F32).T


def call(kernel, outs, args, scratch=(), flops=0):
    moved = sum(a.size * a.dtype.itemsize for a in (*args, *outs))
    vmem = pl.BlockSpec(memory_space=pltpu.VMEM)
    return pl.pallas_call(
        kernel,
        out_shape=outs,
        in_specs=[pl.BlockSpec(memory_space=pltpu.SMEM)] + [vmem] * (len(args) - 1),
        out_specs=[vmem] * len(outs),
        scratch_shapes=scratch,
        cost_estimate=pl.CostEstimate(flops=flops, transcendentals=0, bytes_accessed=moved),
        compiler_params=pltpu.CompilerParams(vmem_limit_bytes=40 << 20),
    )(*args)


def on_device(
    child_rhs, root_rhs, child_inverse, coupling_block, root_inverse, child_orders, coupling_rows
):
    n = child_rhs.shape[2]
    s1 = child_rhs.shape[1]
    q1 = s1 // ZL
    s0 = root_rhs.shape[0] * X * ZH
    q0 = s0 // ZL
    k = coupling_rows.shape[1]
    r1 = child_inverse.shape[1]
    block = root_rhs.shape[0]
    sub = lax.axis_index("x") * ZH + lax.axis_index("zh")
    place = jnp.stack([lax.axis_index("y"), lax.axis_index("core"), sub, child_orders[0]])
    idx = coupling_rows[0][:, None]
    shape = jax.ShapeDtypeStruct

    pair = jnp.concatenate([child_inverse[0], coupling_block[0]], axis=0)
    by_zl = gather_blocks(jnp.concatenate([pair, root_inverse.T], axis=1), "zl", ZL)
    own = jnp.concatenate(
        [by_zl[q, r1:, :s1] for q in range(ZL)]
        + [by_zl[q, :r1, : (q + 1) * q1] for q in reversed(range(ZL))],
        axis=1,
    )
    rt = by_zl[:, :, s1:]
    rc = rt.shape[1]

    up = {1: lax.ppermute(own, "y", FORTH)}
    down = {1: lax.ppermute(own, "y", BACK)}
    rz = lax.ppermute(rt, "zh", SWAP)
    low = lax.axis_index("zh") == 0
    rt = jnp.stack([jnp.where(low, rt, rz), jnp.where(low, rz, rt)])
    up[2] = lax.ppermute(up[1], "y", FORTH)
    down[2] = lax.ppermute(down[1], "y", BACK)
    rt = gather_blocks(after(rt, up[1], down[1]), "x", X)
    up[3] = lax.ppermute(up[2], "y", FORTH)
    down[3] = lax.ppermute(down[2], "y", BACK)
    up[4] = lax.ppermute(up[3], "y", FORTH)
    rt = jnp.concatenate(
        [rt[x, z, q] for q in range(ZL) for x in range(q, X) for z in range(ZH)], axis=1
    )
    rt = after(rt, up[3], down[3])
    rup = {1: lax.ppermute(rt, "y", FORTH)}
    rdown = {1: lax.ppermute(rt, "y", BACK)}
    mine = jnp.stack([up[i] for i in (4, 3, 2, 1)] + [own] + [down[i] for i in (1, 2, 3)])
    other = lax.ppermute(mine, "core", SWAP)
    rup[2] = lax.ppermute(after(rup[1], mine), "y", FORTH)
    rdown[2] = lax.ppermute(after(rdown[1], mine), "y", BACK)

    placed, solved, a, c = call(
        forward_kernel,
        [shape((n, s0), BF), shape((n, s1), F32), shape((s1, s1), BF), shape((k, s1), BF)],
        [place, mine, other, child_rhs[0], root_rhs, idx],
        flops=2 * n * (s1 * s1 + k * s1 + k * s0),
    )
    rup[3] = lax.ppermute(after(rup[2], placed), "y", FORTH)
    rdown[3] = lax.ppermute(after(rdown[2], placed), "y", BACK)
    parts = lax.all_to_all(placed.reshape(X, n // X, s0), "x", 0, 0, tiled=True)
    part = jnp.sum(parts.astype(F32), axis=0)
    sent, r3, d3 = lax.optimization_barrier((part.astype(BF), rup[3], rdown[3]))
    far = lax.ppermute(sent, "zh", SWAP)
    last = lax.ppermute(r3, "y", FORTH)
    rmine = jnp.stack([r3, rup[2], rup[1], rt, rdown[1], rdown[2], d3])
    rother = lax.ppermute(rmine, "core", SWAP)
    s_t = (part + far.astype(F32)).astype(BF)
    rlast = lax.ppermute(last, "core", SWAP)

    x_t, = call(
        root_kernel,
        [shape((X, n // X, s0), BF)],
        [place, s_t, rmine, rother, last, rlast],
        [pltpu.VMEM((q0, rt.shape[1]), BF), pltpu.VMEM((n // X, s0), F32)],
        flops=4 * (n // X) * q0 * rt.shape[1],
    )
    x_all = lax.all_to_all(x_t, "x", 0, 0, tiled=True).reshape(n, s0)

    child_out, root_out = call(
        backward_kernel,
        [shape((s1, n), F32), shape((block, n), F32)],
        [place, x_all, solved, a, c, idx],
        flops=2 * n * (s1 * s1 + k * s1 + k * s0),
    )
    return (child_out[None], root_out)


def solution(mesh):
    fine = Mesh(mesh.devices.reshape(ZL, Y, CORE, X, ZH), (*SRC, *SUB))
    return jax.shard_map(
        on_device,
        mesh=fine,
        in_specs=(
            P(SUB, None, SRC),
            P(SUB, SRC),
            P(SUB, SRC, None),
            P(SUB, SRC, None),
            P(SUB, SRC),
            P(SUB),
            P(SUB, None),
        ),
        out_specs=(P(SUB, None, SRC), P(SUB, SRC)),
        check_vma=False,
    )
```

time: 257 us -> 178 us (0.69)
  the two profiles are of different devices: /device:TPU:1 before, /device:TPU:16 now
where the time goes in v3:
time: 178 us; the launch traced here: 177 us
  starting transfers between devices  79.5 us (45%)
  waiting for transfers between devices  51.4 us (29%)
  blocking collectives  18.7 us (11%)
  local copies, waits for them, and re-layouts  11.6 us (7%)
  Pallas kernels  11.6 us (7%)
  other arithmetic  2.44 us (1%)
  between operations  1.92 us (1%)
    all_to_all x1, blocking collectives, on_device(): x_all = lax.all_to_all(x_t, 'x', 0, 0, tiled=True).reshape(n, s0)  18.7 us
    pallas_call x3, Pallas kernels, call(): pl.pallas_call(kernel, out_shape=outs, in_specs=[pl.BlockSpec(memory_spac...  11.6 us
    all_to_all x2, starting transfers between devices, gather_blocks(): lax.all_to_all(jnp.broadcast_to(x[None], (length, *x.shape)), axis, 0, 0,...  11.6 us
    all_to_all x2, waiting for transfers between devices, gather_blocks(): lax.all_to_all(jnp.broadcast_to(x[None], (length, *x.shape)), axis, 0, 0,...  10.3 us
    ppermute x1, starting transfers between devices, on_device(): rz = lax.ppermute(rt, 'zh', SWAP)  8.21 us
    unnamed x53, local copies, waits for them, and re-layouts  7.8 us
    ppermute x1, waiting for transfers between devices, on_device(): far = lax.ppermute(sent, 'zh', SWAP)  7.55 us
    ppermute x1, waiting for transfers between devices, on_device(): rup[2] = lax.ppermute(after(rup[1], mine), 'y', FORTH)  5.8 us
  transfers between devices with their start and end apart: 22, of which 12 were waited for; matrix products, arithmetic and copies ran while one was open for 3% of the time, Pallas kernels for 2%

profile of v3, /device:TPU:16, one launch (start us, length us, event | category | flops | bytes accessed | tf_op | source)
XLA Modules:
  0.0 177.1 jit_solution(9334841364420651070)
XLA Ops:
  2.2 7.3 %all-to-all-start = ((bf16[4,32,1280]{2,1,0:T(8,128)(2,1)}), bf16[4,32,1280]{2,1,0:T(8,128)(2,1)S(1)}, u32[]{:S(2)}, u32[]{:S(2)}) async-start(bf16[4,32,1280]{2,1,0:T(8,128)(2,1)} %broadcast_in_dim.6), calls=%async_computation | async-start | bytes 655360 | tf_op jit(solution)/shard_map/all_to_all | solution.py:20
  9.4 10.3 %all-to-all-done = bf16[4,32,1280]{2,1,0:T(8,128)(2,1)S(1)} async-done(((bf16[4,32,1280]{2,1,0:T(8,128)(2,1)}), bf16[4,32,1280]{2,1,0:T(8,128)(2,1)S(1)}, u32[]{:S(2)}, u32[]{:S(2)}) %all-to-all-start) | async-done | bytes 327712 | tf_op jit(solution)/shard_map/all_to_all | solution.py:20
  19.8 8.2 %collective-permute-start.8 = (bf16[4,32,256]{2,1,0:T(8,128)(2,1)S(1)}, bf16[4,32,256]{2,1,0:T(8,128)(2,1)S(1)}, u32[]{:S(2)}, u32[]{:S(2)}) collective-permute-start(bf16[4,32,256]{2,1,0:T(8,128)(2,1)S(1)} %slice.124), channel_id=1, source_target_pairs={{0,1},{1,0},{2,3},{3,2},{4,5},{5,4},{6,7},{7,6},{8,9},{9,8},{10,11... | collective-permute-start | bytes 196616 | tf_op jit(solution)/shard_map/ppermute | solution.py:184
  28.1 3.5 %collective-permute-start = (bf16[16,6656]{1,0:T(8,128)(2,1)S(1)}, bf16[16,6656]{1,0:T(8,128)(2,1)S(1)}, u32[]{:S(2)}, u32[]{:S(2)}) collective-permute-start(bf16[16,6656]{1,0:T(8,128)(2,1)S(1)} %constant_dynamic-update-slice_fusion), channel_id=1, source_target_pairs={{0,16},{16,32},{32,48},{48,64},{64,80},{80,96},{96,112},{112,0},{1... | collective-permute-start | bytes 638984 | tf_op jit(solution)/shard_map/ppermute | solution.py:182
  31.6 2.4 %collective-permute-start.4 = (bf16[16,6656]{1,0:T(8,128)(2,1)S(1)}, bf16[16,6656]{1,0:T(8,128)(2,1)S(1)}, u32[]{:S(2)}, u32[]{:S(2)}) collective-permute-start(bf16[16,6656]{1,0:T(8,128)(2,1)S(1)} %constant_dynamic-update-slice_fusion), channel_id=1, source_target_pairs={{0,112},{16,0},{32,16},{48,32},{64,48},{80,64},{96,80},{112,96},{1... | collective-permute-start | bytes 638984 | tf_op jit(solution)/shard_map/ppermute | solution.py:183
  35.8 4.3 %collective-permute-done.4 = bf16[16,6656]{1,0:T(8,128)(2,1)S(1)} collective-permute-done((bf16[16,6656]{1,0:T(8,128)(2,1)S(1)}, bf16[16,6656]{1,0:T(8,128)(2,1)S(1)}, u32[]{:S(2)}, u32[]{:S(2)}) %collective-permute-start.4) | collective-permute-done | bytes 213024 | tf_op jit(solution)/shard_map/ppermute | solution.py:183
  40.9 4.3 %all-to-all-start.2 = ((bf16[4,2,4,32,256]{4,3,2,1,0:T(8,128)(2,1)}), bf16[4,2,4,32,256]{4,3,2,1,0:T(8,128)(2,1)S(1)}, u32[]{:S(2)}, u32[]{:S(2)}) async-start(bf16[4,2,4,32,256]{4,3,2,1,0:T(8,128)(2,1)} %broadcast_in_dim.7), calls=%async_computation.2 | async-start | bytes 1048576 | tf_op jit(solution)/shard_map/all_to_all | solution.py:20
  45.2 5.1 %collective-permute-start.1 = (bf16[16,6656]{1,0:T(8,128)(2,1)S(1)}, bf16[16,6656]{1,0:T(8,128)(2,1)}, u32[]{:S(2)}, u32[]{:S(2)}) collective-permute-start(bf16[16,6656]{1,0:T(8,128)(2,1)S(1)} %collective-permute-done), channel_id=1, source_target_pairs={{0,16},{16,32},{32,48},{48,64},{64,80},{80,96},{96,112},{112,0},{1... | collective-permute-start | bytes 638984 | tf_op jit(solution)/shard_map/ppermute | solution.py:187
  50.4 1.9 %collective-permute-start.5 = (bf16[16,6656]{1,0:T(8,128)(2,1)S(1)}, bf16[16,6656]{1,0:T(8,128)(2,1)}, u32[]{:S(2)}, u32[]{:S(2)}) collective-permute-start(bf16[16,6656]{1,0:T(8,128)(2,1)S(1)} %collective-permute-done.4), channel_id=1, source_target_pairs={{0,112},{16,0},{32,16},{48,32},{64,48},{80,64},{96,80},{112,96},{1... | collective-permute-start | bytes 638984 | tf_op jit(solution)/shard_map/ppermute | solution.py:188
  54.1 4.5 %collective-permute-start.2 = (bf16[16,6656]{1,0:T(8,128)(2,1)}, bf16[16,6656]{1,0:T(8,128)(2,1)}, u32[]{:S(2)}, u32[]{:S(2)}) collective-permute-start(bf16[16,6656]{1,0:T(8,128)(2,1)} %collective-permute-done.1), channel_id=1, source_target_pairs={{0,16},{16,32},{32,48},{48,64},{64,80},{80,96},{96,112},{112,0},{1... | collective-permute-start | bytes 638984 | tf_op jit(solution)/shard_map/ppermute | solution.py:190
  58.6 1.9 %collective-permute-start.6 = (bf16[16,6656]{1,0:T(8,128)(2,1)}, bf16[16,6656]{1,0:T(8,128)(2,1)}, u32[]{:S(2)}, u32[]{:S(2)}) collective-permute-start(bf16[16,6656]{1,0:T(8,128)(2,1)} %collective-permute-done.5), channel_id=1, source_target_pairs={{0,112},{16,0},{32,16},{48,32},{64,48},{80,64},{96,80},{112,96},{1... | collective-permute-start | bytes 638984 | tf_op jit(solution)/shard_map/ppermute | solution.py:191
  60.7 2.8 %collective-permute-done.2 = bf16[16,6656]{1,0:T(8,128)(2,1)} collective-permute-done((bf16[16,6656]{1,0:T(8,128)(2,1)}, bf16[16,6656]{1,0:T(8,128)(2,1)}, u32[]{:S(2)}, u32[]{:S(2)}) %collective-permute-start.2) | collective-permute-done | bytes 213024 | tf_op jit(solution)/shard_map/ppermute | solution.py:190
  63.5 4.4 %collective-permute-start.3 = (bf16[16,6656]{1,0:T(8,128)(2,1)}, bf16[16,6656]{1,0:T(8,128)(2,1)S(1)}, u32[]{:S(2)}, u32[]{:S(2)}) collective-permute-start(bf16[16,6656]{1,0:T(8,128)(2,1)} %collective-permute-done.2), channel_id=1, source_target_pairs={{0,16},{16,32},{32,48},{48,64},{64,80},{80,96},{96,112},{112,0},{1... | collective-permute-start | bytes 638984 | tf_op jit(solution)/shard_map/ppermute | solution.py:192
  67.9 3.6 %collective-permute-done.3 = bf16[16,6656]{1,0:T(8,128)(2,1)S(1)} collective-permute-done((bf16[16,6656]{1,0:T(8,128)(2,1)}, bf16[16,6656]{1,0:T(8,128)(2,1)S(1)}, u32[]{:S(2)}, u32[]{:S(2)}) %collective-permute-start.3) | collective-permute-done | bytes 213024 | tf_op jit(solution)/shard_map/ppermute | solution.py:192
  75.4 1.9 %collective-permute-start.7 = (bf16[8,16,6656]{2,1,0:T(8,128)(2,1)S(1)}, bf16[8,16,6656]{2,1,0:T(8,128)(2,1)S(1)}, u32[]{:S(2)}, u32[]{:S(2)}) collective-permute-start(bf16[8,16,6656]{2,1,0:T(8,128)(2,1)S(1)} %bitcast_dynamic-update-slice_fusion.7.mine_ref), channel_id=1, source_target_pairs={{0,8},{8,0},{1,9},{9,1},{2,10},{10,2},{3,11},{11,3},{4,12},{12,4},... | collective-permute-start | bytes 5111816 | tf_op jit(solution)/shard_map/ppermute | solution.py:200
  77.5 4.3 %collective-permute-start.9 = (bf16[32,5120]{1,0:T(8,128)(2,1)S(1)}, bf16[32,5120]{1,0:T(8,128)(2,1)}, u32[]{:S(2)}, u32[]{:S(2)}) collective-permute-start(bf16[32,5120]{1,0:T(8,128)(2,1)S(1)} %constant_dynamic-update-slice_fusion.8), channel_id=1, source_target_pairs={{0,16},{16,32},{32,48},{48,64},{64,80},{80,96},{96,112},{112,0},{1... | collective-permute-start | bytes 983048 | tf_op jit(solution)/shard_map/ppermute | solution.py:197
  81.8 1.9 %collective-permute-start.12 = (bf16[32,5120]{1,0:T(8,128)(2,1)S(1)}, bf16[32,5120]{1,0:T(8,128)(2,1)S(1)}, u32[]{:S(2)}, u32[]{:S(2)}) collective-permute-start(bf16[32,5120]{1,0:T(8,128)(2,1)S(1)} %constant_dynamic-update-slice_fusion.8), channel_id=1, source_target_pairs={{0,112},{16,0},{32,16},{48,32},{64,48},{80,64},{96,80},{112,96},{1... | collective-permute-start | bytes 983048 | tf_op jit(solution)/shard_map/ppermute | solution.py:198
  83.7 4.0 %shard_map.86 = (bf16[256,2048]{1,0:T(8,128)(2,1)}, f32[256,1024]{1,0:T(8,128)S(1)}, bf16[1024,1024]{1,0:T(8,128)(2,1)S(1)}, bf16[1024,1024]{1,0:T(8,128)(2,1)S(1)}) custom-call(s32[4]{0:T(128)S(1)} %pad_add_fusion.place_ref, bf16[8,16,6656]{2,1,0:T(8,128)(2,1)S(1)} %bitcast_dynamic-update-slice_fusion.7.mine_ref, ...), custom_call_target="tpu_custom_call" | custom-call | flops 2147483648 | bytes 11014160 | tf_op jit(solution)/shard_map/pallas_call | solution.py:145
  90.4 5.0 %all-to-all-start.1 = ((bf16[4,64,2048]{2,1,0:T(8,128)(2,1)}), bf16[4,64,2048]{2,1,0:T(8,128)(2,1)}, u32[]{:S(2)}, u32[]{:S(2)}) async-start(bf16[4,64,2048]{2,1,0:T(8,128)(2,1)} %bitcast.24), calls=%async_computation.1 | async-start | bytes 2097152 | tf_op jit(solution)/shard_map/all_to_all | solution.py:212
  95.4 4.0 %collective-permute-start.10 = (bf16[32,5120]{1,0:T(8,128)(2,1)}, bf16[32,5120]{1,0:T(8,128)(2,1)}, u32[]{:S(2)}, u32[]{:S(2)}) collective-permute-start(bf16[32,5120]{1,0:T(8,128)(2,1)} %collective-permute-done.9), channel_id=1, source_target_pairs={{0,16},{16,32},{32,48},{48,64},{64,80},{80,96},{96,112},{112,0},{1... | collective-permute-start | bytes 983048 | tf_op jit(solution)/shard_map/ppermute | solution.py:201
  99.5 1.9 %collective-permute-start.13 = (bf16[32,5120]{1,0:T(8,128)(2,1)S(1)}, bf16[32,5120]{1,0:T(8,128)(2,1)S(1)}, u32[]{:S(2)}, u32[]{:S(2)}) collective-permute-start(bf16[32,5120]{1,0:T(8,128)(2,1)S(1)} %collective-permute-done.12), channel_id=1, source_target_pairs={{0,112},{16,0},{32,16},{48,32},{64,48},{80,64},{96,80},{112,96},{1... | collective-permute-start | bytes 983048 | tf_op jit(solution)/shard_map/ppermute | solution.py:202
  101.4 5.8 %collective-permute-done.10 = bf16[32,5120]{1,0:T(8,128)(2,1)} collective-permute-done((bf16[32,5120]{1,0:T(8,128)(2,1)}, bf16[32,5120]{1,0:T(8,128)(2,1)}, u32[]{:S(2)}, u32[]{:S(2)}) %collective-permute-start.10) | collective-permute-done | bytes 327712 | tf_op jit(solution)/shard_map/ppermute | solution.py:201
  107.2 4.5 %collective-permute-start.11 = (bf16[32,5120]{1,0:T(8,128)(2,1)}, bf16[32,5120]{1,0:T(8,128)(2,1)S(1)}, u32[]{:S(2)}, u32[]{:S(2)}) collective-permute-start(bf16[32,5120]{1,0:T(8,128)(2,1)} %collective-permute-done.10), channel_id=1, source_target_pairs={{0,16},{16,32},{32,48},{48,64},{64,80},{80,96},{96,112},{112,0},{1... | collective-permute-start | bytes 983048 | tf_op jit(solution)/shard_map/ppermute | solution.py:210
  115.3 2.7 %collective-permute-done.11 = bf16[32,5120]{1,0:T(8,128)(2,1)S(1)} collective-permute-done((bf16[32,5120]{1,0:T(8,128)(2,1)}, bf16[32,5120]{1,0:T(8,128)(2,1)S(1)}, u32[]{:S(2)}, u32[]{:S(2)}) %collective-permute-start.11) | collective-permute-done | bytes 327712 | tf_op jit(solution)/shard_map/ppermute | solution.py:210
  118.0 5.8 %collective-permute-done.14 = bf16[32,5120]{1,0:T(8,128)(2,1)} collective-permute-done((bf16[32,5120]{1,0:T(8,128)(2,1)S(1)}, bf16[32,5120]{1,0:T(8,128)(2,1)}, u32[]{:S(2)}, u32[]{:S(2)}) %collective-permute-start.14) | collective-permute-done | bytes 327712 | tf_op jit(solution)/shard_map/ppermute | solution.py:211
  126.9 1.9 %collective-permute-start.16 = (bf16[7,32,5120]{2,1,0:T(8,128)(2,1)S(1)}, bf16[7,32,5120]{2,1,0:T(8,128)(2,1)S(1)}, u32[]{:S(2)}, u32[]{:S(2)}) collective-permute-start(bf16[7,32,5120]{2,1,0:T(8,128)(2,1)S(1)} %bitcast_dynamic-update-slice_fusion.mine_ref), channel_id=1, source_target_pairs={{0,8},{8,0},{1,9},{9,1},{2,10},{10,2},{3,11},{11,3},{4,12},{12,4},... | collective-permute-start | bytes 6881288 | tf_op jit(solution)/shard_map/ppermute | solution.py:218
  128.8 4.9 %collective-permute-start.17 = (bf16[32,5120]{1,0:T(8,128)(2,1)S(1)}, bf16[32,5120]{1,0:T(8,128)(2,1)S(1)}, u32[]{:S(2)}, u32[]{:S(2)}) collective-permute-start(bf16[32,5120]{1,0:T(8,128)(2,1)S(1)} %collective-permute-done.11), channel_id=1, source_target_pairs={{0,16},{16,32},{32,48},{48,64},{64,80},{80,96},{96,112},{112,0},{1... | collective-permute-start | bytes 983048 | tf_op jit(solution)/shard_map/ppermute | solution.py:216
  135.6 5.7 %collective-permute-done.17.last_ref = bf16[32,5120]{1,0:T(8,128)(2,1)S(1)} collective-permute-done((bf16[32,5120]{1,0:T(8,128)(2,1)S(1)}, bf16[32,5120]{1,0:T(8,128)(2,1)S(1)}, u32[]{:S(2)}, u32[]{:S(2)}) %collective-permute-start.17) | collective-permute-done | bytes 327712 | tf_op jit(solution)/shard_map/ppermute | solution.py:216
  143.2 7.5 %collective-permute-done.15 = bf16[64,2048]{1,0:T(8,128)(2,1)S(1)} collective-permute-done((bf16[64,2048]{1,0:T(8,128)(2,1)S(1)}, bf16[64,2048]{1,0:T(8,128)(2,1)S(1)}, u32[]{:S(2)}, u32[]{:S(2)}) %collective-permute-start.15) | collective-permute-done | bytes 262176 | tf_op jit(solution)/shard_map/ppermute | solution.py:215
  150.8 3.5 %shard_map.87 = bf16[4,64,2048]{2,1,0:T(8,128)(2,1)S(1)} custom-call(s32[4]{0:T(128)S(1)} %pad_add_fusion.place_ref, bf16[64,2048]{1,0:T(8,128)(2,1)S(1)} %add_convert_fusion.s_ref, bf16[7,32,5120]{2,1,0:T(8,128)(2,1)S(1)} %bitcast_dynamic-update-slice_fusion.mine_ref, bf16[7,32,5120]{2,1,0:T(8,128)(2,1)S(1)} %collective-permute-done.16.other_ref, ...), custom_call_target="tpu_custom_call" | custom-call | flops 671088640 | bytes 6553616 | tf_op jit(solution)/shard_map/pallas_call | solution.py:145
  154.4 18.7 %all_to_all.20 = bf16[4,64,2048]{2,1,0:T(8,128)(2,1)S(1)} all-to-all(bf16[4,64,2048]{2,1,0:T(8,128)(2,1)S(1)} %shard_map.87), channel_id=1, replica_groups=mesh['zl'=4,'y'=8,'core'=2,'x'=4,'zh'=2] {'x'}, dimensions={0} | all-to-all | bytes 2097152 | tf_op jit(solution)/shard_map/all_to_all | solution.py:229
  173.1 4.0 %shard_map.88 = (f32[1024,256]{1,0:T(8,128)}, f32[256,256]{1,0:T(8,128)}) custom-call(s32[4]{0:T(128)S(1)} %pad_add_fusion.place_ref, bf16[256,2048]{1,0:T(8,128)(2,1)S(1)} %bitcast.157, f32[256,1024]{1,0:T(8,128)S(1)} %get-tuple-element.27.solved_ref, bf16[1024,1024]{1,0:T(8,128)(2,1)S(1)} %copy-done.3, bf16[1024,1024]{1,0:T(8,128)(2,1)S(1)} %copy-done.5, ...), custom_call_target="tpu_custom_call" | custom-call | flops 2147483648 | bytes 7606288 | tf_op jit(solution)/shard_map/pallas_call | solution.py:145
  (84 shorter events, 22.6 us)
Async XLA Ops:
  0.6 52.3 %copy-start.6 = (s32[1,1024]{1,0:T(1,128)S(1)}, s32[1,1024]{1,0:T(1,128)}, u32[]{:S(2)}) copy-start(s32[1,1024]{1,0:T(1,128)} %param.13) | copy-start | bytes 12292
  2.2 17.6 %all-to-all-start = ((bf16[4,32,1280]{2,1,0:T(8,128)(2,1)}), bf16[4,32,1280]{2,1,0:T(8,128)(2,1)S(1)}, u32[]{:S(2)}, u32[]{:S(2)}) async-start(bf16[4,32,1280]{2,1,0:T(8,128)(2,1)} %broadcast_in_dim.6), calls=%async_computation | async-start | bytes 655360 | tf_op jit(solution)/shard_map/all_to_all | solution.py:20
  19.8 14.2 %collective-permute-start.8 = (bf16[4,32,256]{2,1,0:T(8,128)(2,1)S(1)}, bf16[4,32,256]{2,1,0:T(8,128)(2,1)S(1)}, u32[]{:S(2)}, u32[]{:S(2)}) collective-permute-start(bf16[4,32,256]{2,1,0:T(8,128)(2,1)S(1)} %slice.124), channel_id=1, source_target_pairs={{0,1},{1,0},{2,3},{3,2},{4,5},{5,4},{6,7},{7,6},{8,9},{9,8},{10,11... | collective-permute-start | bytes 196616 | tf_op jit(solution)/shard_map/ppermute | solution.py:184
  28.1 7.7 %collective-permute-start = (bf16[16,6656]{1,0:T(8,128)(2,1)S(1)}, bf16[16,6656]{1,0:T(8,128)(2,1)S(1)}, u32[]{:S(2)}, u32[]{:S(2)}) collective-permute-start(bf16[16,6656]{1,0:T(8,128)(2,1)S(1)} %constant_dynamic-update-slice_fusion), channel_id=1, source_target_pairs={{0,16},{16,32},{32,48},{48,64},{64,80},{80,96},{96,112},{112,0},{1... | collective-permute-start | bytes 638984 | tf_op jit(solution)/shard_map/ppermute | solution.py:182
  31.6 8.5 %collective-permute-start.4 = (bf16[16,6656]{1,0:T(8,128)(2,1)S(1)}, bf16[16,6656]{1,0:T(8,128)(2,1)S(1)}, u32[]{:S(2)}, u32[]{:S(2)}) collective-permute-start(bf16[16,6656]{1,0:T(8,128)(2,1)S(1)} %constant_dynamic-update-slice_fusion), channel_id=1, source_target_pairs={{0,112},{16,0},{32,16},{48,32},{64,48},{80,64},{96,80},{112,96},{1... | collective-permute-start | bytes 638984 | tf_op jit(solution)/shard_map/ppermute | solution.py:183
  40.9 19.6 %all-to-all-start.2 = ((bf16[4,2,4,32,256]{4,3,2,1,0:T(8,128)(2,1)}), bf16[4,2,4,32,256]{4,3,2,1,0:T(8,128)(2,1)S(1)}, u32[]{:S(2)}, u32[]{:S(2)}) async-start(bf16[4,2,4,32,256]{4,3,2,1,0:T(8,128)(2,1)} %broadcast_in_dim.7), calls=%async_computation.2 | async-start | bytes 1048576 | tf_op jit(solution)/shard_map/all_to_all | solution.py:20
  45.2 8.9 %collective-permute-start.1 = (bf16[16,6656]{1,0:T(8,128)(2,1)S(1)}, bf16[16,6656]{1,0:T(8,128)(2,1)}, u32[]{:S(2)}, u32[]{:S(2)}) collective-permute-start(bf16[16,6656]{1,0:T(8,128)(2,1)S(1)} %collective-permute-done), channel_id=1, source_target_pairs={{0,16},{16,32},{32,48},{48,64},{64,80},{80,96},{96,112},{112,0},{1... | collective-permute-start | bytes 638984 | tf_op jit(solution)/shard_map/ppermute | solution.py:187
  50.4 8.2 %collective-permute-start.5 = (bf16[16,6656]{1,0:T(8,128)(2,1)S(1)}, bf16[16,6656]{1,0:T(8,128)(2,1)}, u32[]{:S(2)}, u32[]{:S(2)}) collective-permute-start(bf16[16,6656]{1,0:T(8,128)(2,1)S(1)} %collective-permute-done.4), channel_id=1, source_target_pairs={{0,112},{16,0},{32,16},{48,32},{64,48},{80,64},{96,80},{112,96},{1... | collective-permute-start | bytes 638984 | tf_op jit(solution)/shard_map/ppermute | solution.py:188
  53.2 30.5 %copy-start = (f32[1,1024,256]{2,1,0:T(8,128)S(1)}, f32[1,1024,256]{2,1,0:T(8,128)}, u32[]{:S(2)}) copy-start(f32[1,1024,256]{2,1,0:T(8,128)} %param.7) | copy-start | bytes 3145732
  53.2 30.5 %copy-start.1 = (f32[256,256]{1,0:T(8,128)S(1)}, f32[256,256]{1,0:T(8,128)}, u32[]{:S(2)}) copy-start(f32[256,256]{1,0:T(8,128)} %root_ref.1) | copy-start | bytes 786436
  54.1 9.4 %collective-permute-start.2 = (bf16[16,6656]{1,0:T(8,128)(2,1)}, bf16[16,6656]{1,0:T(8,128)(2,1)}, u32[]{:S(2)}, u32[]{:S(2)}) collective-permute-start(bf16[16,6656]{1,0:T(8,128)(2,1)} %collective-permute-done.1), channel_id=1, source_target_pairs={{0,16},{16,32},{32,48},{48,64},{64,80},{80,96},{96,112},{112,0},{1... | collective-permute-start | bytes 638984 | tf_op jit(solution)/shard_map/ppermute | solution.py:190
  58.6 15.9 %collective-permute-start.6 = (bf16[16,6656]{1,0:T(8,128)(2,1)}, bf16[16,6656]{1,0:T(8,128)(2,1)}, u32[]{:S(2)}, u32[]{:S(2)}) collective-permute-start(bf16[16,6656]{1,0:T(8,128)(2,1)} %collective-permute-done.5), channel_id=1, source_target_pairs={{0,112},{16,0},{32,16},{48,32},{64,48},{80,64},{96,80},{112,96},{1... | collective-permute-start | bytes 638984 | tf_op jit(solution)/shard_map/ppermute | solution.py:191
  63.5 8.0 %collective-permute-start.3 = (bf16[16,6656]{1,0:T(8,128)(2,1)}, bf16[16,6656]{1,0:T(8,128)(2,1)S(1)}, u32[]{:S(2)}, u32[]{:S(2)}) collective-permute-start(bf16[16,6656]{1,0:T(8,128)(2,1)} %collective-permute-done.2), channel_id=1, source_target_pairs={{0,16},{16,32},{32,48},{48,64},{64,80},{80,96},{96,112},{112,0},{1... | collective-permute-start | bytes 638984 | tf_op jit(solution)/shard_map/ppermute | solution.py:192
  75.4 8.2 %collective-permute-start.7 = (bf16[8,16,6656]{2,1,0:T(8,128)(2,1)S(1)}, bf16[8,16,6656]{2,1,0:T(8,128)(2,1)S(1)}, u32[]{:S(2)}, u32[]{:S(2)}) collective-permute-start(bf16[8,16,6656]{2,1,0:T(8,128)(2,1)S(1)} %bitcast_dynamic-update-slice_fusion.7.mine_ref), channel_id=1, source_target_pairs={{0,8},{8,0},{1,9},{9,1},{2,10},{10,2},{3,11},{11,3},{4,12},{12,4},... | collective-permute-start | bytes 5111816 | tf_op jit(solution)/shard_map/ppermute | solution.py:200
  77.5 18.0 %collective-permute-start.9 = (bf16[32,5120]{1,0:T(8,128)(2,1)S(1)}, bf16[32,5120]{1,0:T(8,128)(2,1)}, u32[]{:S(2)}, u32[]{:S(2)}) collective-permute-start(bf16[32,5120]{1,0:T(8,128)(2,1)S(1)} %constant_dynamic-update-slice_fusion.8), channel_id=1, source_target_pairs={{0,16},{16,32},{32,48},{48,64},{64,80},{80,96},{96,112},{112,0},{1... | collective-permute-start | bytes 983048 | tf_op jit(solution)/shard_map/ppermute | solution.py:197
  81.8 17.7 %collective-permute-start.12 = (bf16[32,5120]{1,0:T(8,128)(2,1)S(1)}, bf16[32,5120]{1,0:T(8,128)(2,1)S(1)}, u32[]{:S(2)}, u32[]{:S(2)}) collective-permute-start(bf16[32,5120]{1,0:T(8,128)(2,1)S(1)} %constant_dynamic-update-slice_fusion.8), channel_id=1, source_target_pairs={{0,112},{16,0},{32,16},{48,32},{64,48},{80,64},{96,80},{112,96},{1... | collective-permute-start | bytes 983048 | tf_op jit(solution)/shard_map/ppermute | solution.py:198
  87.7 1.4 copy-start.2
  89.1 1.3 copy-start.4
  90.4 23.3 %all-to-all-start.1 = ((bf16[4,64,2048]{2,1,0:T(8,128)(2,1)}), bf16[4,64,2048]{2,1,0:T(8,128)(2,1)}, u32[]{:S(2)}, u32[]{:S(2)}) async-start(bf16[4,64,2048]{2,1,0:T(8,128)(2,1)} %bitcast.24), calls=%async_computation.1 | async-start | bytes 2097152 | tf_op jit(solution)/shard_map/all_to_all | solution.py:212
  95.4 11.8 %collective-permute-start.10 = (bf16[32,5120]{1,0:T(8,128)(2,1)}, bf16[32,5120]{1,0:T(8,128)(2,1)}, u32[]{:S(2)}, u32[]{:S(2)}) collective-permute-start(bf16[32,5120]{1,0:T(8,128)(2,1)} %collective-permute-done.9), channel_id=1, source_target_pairs={{0,16},{16,32},{32,48},{48,64},{64,80},{80,96},{96,112},{112,0},{1... | collective-permute-start | bytes 983048 | tf_op jit(solution)/shard_map/ppermute | solution.py:201
  99.5 12.4 %collective-permute-start.13 = (bf16[32,5120]{1,0:T(8,128)(2,1)S(1)}, bf16[32,5120]{1,0:T(8,128)(2,1)S(1)}, u32[]{:S(2)}, u32[]{:S(2)}) collective-permute-start(bf16[32,5120]{1,0:T(8,128)(2,1)S(1)} %collective-permute-done.12), channel_id=1, source_target_pairs={{0,112},{16,0},{32,16},{48,32},{64,48},{80,64},{96,80},{112,96},{1... | collective-permute-start | bytes 983048 | tf_op jit(solution)/shard_map/ppermute | solution.py:202
  107.2 10.8 %collective-permute-start.11 = (bf16[32,5120]{1,0:T(8,128)(2,1)}, bf16[32,5120]{1,0:T(8,128)(2,1)S(1)}, u32[]{:S(2)}, u32[]{:S(2)}) collective-permute-start(bf16[32,5120]{1,0:T(8,128)(2,1)} %collective-permute-done.10), channel_id=1, source_target_pairs={{0,16},{16,32},{32,48},{48,64},{64,80},{80,96},{96,112},{112,0},{1... | collective-permute-start | bytes 983048 | tf_op jit(solution)/shard_map/ppermute | solution.py:210
  111.8 11.9 %collective-permute-start.14 = (bf16[32,5120]{1,0:T(8,128)(2,1)S(1)}, bf16[32,5120]{1,0:T(8,128)(2,1)}, u32[]{:S(2)}, u32[]{:S(2)}) collective-permute-start(bf16[32,5120]{1,0:T(8,128)(2,1)S(1)} %collective-permute-done.13), channel_id=1, source_target_pairs={{0,112},{16,0},{32,16},{48,32},{64,48},{80,64},{96,80},{112,96},{1... | collective-permute-start | bytes 983048 | tf_op jit(solution)/shard_map/ppermute | solution.py:211
  126.9 23.9 %collective-permute-start.16 = (bf16[7,32,5120]{2,1,0:T(8,128)(2,1)S(1)}, bf16[7,32,5120]{2,1,0:T(8,128)(2,1)S(1)}, u32[]{:S(2)}, u32[]{:S(2)}) collective-permute-start(bf16[7,32,5120]{2,1,0:T(8,128)(2,1)S(1)} %bitcast_dynamic-update-slice_fusion.mine_ref), channel_id=1, source_target_pairs={{0,8},{8,0},{1,9},{9,1},{2,10},{10,2},{3,11},{11,3},{4,12},{12,4},... | collective-permute-start | bytes 6881288 | tf_op jit(solution)/shard_map/ppermute | solution.py:218
  128.8 12.5 %collective-permute-start.17 = (bf16[32,5120]{1,0:T(8,128)(2,1)S(1)}, bf16[32,5120]{1,0:T(8,128)(2,1)S(1)}, u32[]{:S(2)}, u32[]{:S(2)}) collective-permute-start(bf16[32,5120]{1,0:T(8,128)(2,1)S(1)} %collective-permute-done.11), channel_id=1, source_target_pairs={{0,16},{16,32},{32,48},{48,64},{64,80},{80,96},{96,112},{112,0},{1... | collective-permute-start | bytes 983048 | tf_op jit(solution)/shard_map/ppermute | solution.py:216
  133.7 17.1 %collective-permute-start.15 = (bf16[64,2048]{1,0:T(8,128)(2,1)S(1)}, bf16[64,2048]{1,0:T(8,128)(2,1)S(1)}, u32[]{:S(2)}, u32[]{:S(2)}) collective-permute-start(bf16[64,2048]{1,0:T(8,128)(2,1)S(1)} %convert_element_type.13), channel_id=1, source_target_pairs={{0,1},{1,0},{2,3},{3,2},{4,5},{5,4},{6,7},{7,6},{8,9},{9,8},{10,11... | collective-permute-start | bytes 786440 | tf_op jit(solution)/shard_map/ppermute | solution.py:215
  141.3 9.5 %collective-permute-start.18 = (bf16[32,5120]{1,0:T(8,128)(2,1)S(1)}, bf16[32,5120]{1,0:T(8,128)(2,1)S(1)}, u32[]{:S(2)}, u32[]{:S(2)}) collective-permute-start(bf16[32,5120]{1,0:T(8,128)(2,1)S(1)} %collective-permute-done.17.last_ref), channel_id=1, source_target_pairs={{0,8},{8,0},{1,9},{9,1},{2,10},{10,2},{3,11},{11,3},{4,12},{12,4},... | collective-permute-start | bytes 983048 | tf_op jit(solution)/shard_map/ppermute | solution.py:220
  150.8 22.3 %copy-start.5 = (bf16[1024,1024]{1,0:T(8,128)(2,1)S(1)}, bf16[1024,1024]{1,0:T(8,128)(2,1)}, u32[]{:S(2)}) copy-start(bf16[1024,1024]{1,0:T(8,128)(2,1)} %copy-done.4) | copy-start | bytes 6291460
  154.4 18.7 %copy-start.3 = (bf16[1024,1024]{1,0:T(8,128)(2,1)S(1)}, bf16[1024,1024]{1,0:T(8,128)(2,1)}, u32[]{:S(2)}) copy-start(bf16[1024,1024]{1,0:T(8,128)(2,1)} %copy-done.2) | copy-start | bytes 6291460

commit v4 on v3

v4 whole, which is shorter than its diff:
```python
import jax
import jax.numpy as jnp
from jax import lax
from jax.experimental import pallas as pl
from jax.experimental.pallas import tpu as pltpu
from jax.sharding import Mesh, PartitionSpec as P

ZL, Y, CORE, X, ZH = 4, 8, 2, 4, 2
SRC = ("zl", "y", "core")
SUB = ("x", "zh")
BF = jnp.bfloat16
F32 = jnp.float32
FORTH = [(i, (i + 1) % Y) for i in range(Y)]
BACK = [(i, (i - 1) % Y) for i in range(Y)]
SWAP = [(0, 1), (1, 0)]
EARLY, LATE = (0, -1, 1, -2, 2), (-3, 3, -4)


def gather_blocks(x, axis, length):
    return lax.all_to_all(jnp.broadcast_to(x[None], (length, *x.shape)), axis, 0, 0, tiled=True)


def after(x, *others):
    return lax.optimization_barrier((x, *others))[0]


def dot(a, b, ca=1, cb=0):
    return lax.dot_general(a, b, (((ca,), (cb,)), ((), ())), preferred_element_type=F32)


def onehot(idx_ref, at, width):
    k = idx_ref.shape[0]
    cols = lax.broadcasted_iota(jnp.int32, (k, width), 1) + at
    return jnp.where(idx_ref[...] == cols, 1.0, 0.0).astype(BF)


def by_core(core, early, late, put):
    for mine, other in ((0, 1), (1, 0)):

        @pl.when(core == mine)
        def _():
            for blocks, steps in ((early, EARLY), (late, LATE)):
                put(blocks[0], steps, mine)
                put(blocks[1], steps, other)


def child_weights(here, core, early, late, a_ref, c_ref):
    s1 = a_ref.shape[0]
    r1 = early[0].shape[1]
    q1 = s1 // ZL

    def put(blocks_ref, steps, c):
        for j, step in enumerate(steps):
            y = lax.rem(here + (step + Y), Y)
            at = pl.multiple_of(y * (CORE * r1), CORE * r1) + c * r1
            for q in range(ZL):
                c_ref[pl.ds(q * q1 + at, r1), :] = blocks_ref[j, :, q * s1 : (q + 1) * s1]
            left = ZL * s1
            for q in reversed(range(ZL)):
                width = (q + 1) * q1
                a_ref[pl.ds(q * q1 + at, r1), :width] = blocks_ref[j, :, left : left + width]
                left += width

    by_core(core, early, late, put)


def forward_kernel(
    place_ref, early_ref, early_far_ref, late_ref, late_far_ref, rhs_ref, root_ref, idx_ref,
    placed_ref, out_ref, solved_ref, a_ref, c_ref, sem,
):
    here, core, sub, order = (place_ref[i] for i in range(4))
    s1, n = rhs_ref.shape
    q1 = s1 // ZL
    block = root_ref.shape[0]
    child_weights(here, core, (early_ref, early_far_ref), (late_ref, late_far_ref), a_ref, c_ref)
    rows = lax.broadcasted_iota(jnp.int32, (s1, n), 0)
    source = jnp.where(rows < order, rhs_ref[...], 0.0).astype(BF)
    for q in range(ZL):
        top = (q + 1) * q1
        part = dot(a_ref[q * q1 : top, :top], source[:top])
        part = jnp.where(rows[q * q1 : top] < order, part, 0.0)
        solved_ref[:, q * q1 : top] = part.T
    copy = pltpu.make_async_copy(solved_ref, out_ref, sem)
    copy.start()
    update = dot(solved_ref[...].astype(BF), c_ref[...], 1, 1).astype(BF)
    root = root_ref[...].T
    for b in range(placed_ref.shape[1] // block):
        part = dot(update, onehot(idx_ref, b * block, block))
        placed_ref[:, b * block : (b + 1) * block] = (
            jnp.where(sub == b, root, 0.0) - part
        ).astype(BF)
    copy.wait()


def root_kernel(
    place_ref, s_ref, early_ref, early_far_ref, late_ref, late_far_ref, out_ref, r_ref, f_ref
):
    here, core = place_ref[0], place_ref[1]
    s0 = s_ref.shape[1]
    q0 = s0 // ZL
    half, width = r_ref.shape[0] // (Y * CORE * 2), r_ref.shape[1]

    def put(blocks_ref, steps, c):
        for j, step in enumerate(steps):
            y = lax.rem(here + (step + Y), Y)
            at = pl.multiple_of(y * (CORE * 2 * half), CORE * 2 * half) + c * 2 * half
            for h in range(2):
                r_ref[pl.ds(at + h * half, half), :] = blocks_ref[
                    j, :, h * width : (h + 1) * width
                ]

    by_core(core, (early_ref, early_far_ref), (late_ref, late_far_ref), put)
    left = 0
    spans = []
    for q in range(ZL):
        spans.append((left, left + s0 - q * q0))
        left = spans[-1][1]
    for q in range(ZL):
        term = dot(s_ref[:, q * q0 : (q + 1) * q0], r_ref[:, spans[q][0] : spans[q][1]])
        f_ref[:, q * q0 :] = term if q == 0 else f_ref[:, q * q0 :] + term
    f = f_ref[...].astype(BF)
    for q in range(ZL):
        part = dot(f[:, q * q0 :], r_ref[:, spans[q][0] : spans[q][1]], 1, 1).astype(BF)
        for i in range(out_ref.shape[0]):
            out_ref[i, :, q * q0 : (q + 1) * q0] = part


def backward_kernel(
    place_ref, x_ref, in_ref, early_ref, early_far_ref, late_ref, late_far_ref, idx_ref,
    out_ref, root_ref, solved_ref, a_ref, c_ref, sem,
):
    here, core, sub, order = (place_ref[i] for i in range(4))
    copy = pltpu.make_async_copy(in_ref, solved_ref, sem)
    copy.start()
    child_weights(here, core, (early_ref, early_far_ref), (late_ref, late_far_ref), a_ref, c_ref)
    n, s1 = solved_ref.shape
    q1 = s1 // ZL
    block = root_ref.shape[0]
    picked = None
    for b in range(x_ref.shape[1] // block):
        part = dot(x_ref[:, b * block : (b + 1) * block], onehot(idx_ref, b * block, block), 1, 1)
        picked = part if picked is None else picked + part
    pulled = dot(picked.astype(BF), c_ref[...])
    cols = lax.broadcasted_iota(jnp.int32, (n, s1), 1)
    copy.wait()
    residue = jnp.where(cols < order, solved_ref[...] - pulled, 0.0).astype(BF)
    rows = lax.broadcasted_iota(jnp.int32, (q1, n), 0)
    for q in range(ZL):
        part = dot(residue[:, q * q1 :], a_ref[q * q1 :, q * q1 : (q + 1) * q1])
        out_ref[q * q1 : (q + 1) * q1, :] = jnp.where(rows + q * q1 < order, part.T, 0.0)
    at = pl.multiple_of(sub * block, block)
    root_ref[...] = x_ref[:, pl.ds(at, block)].astype(F32).T


def call(kernel, outs, args, scratch=(), flops=0, far=((), ())):
    moved = sum(a.size * a.dtype.itemsize for a in (*args, *outs))
    vmem = pl.BlockSpec(memory_space=pltpu.VMEM)
    hbm = pl.BlockSpec(memory_space=pltpu.HBM)
    return pl.pallas_call(
        kernel,
        out_shape=outs,
        in_specs=[pl.BlockSpec(memory_space=pltpu.SMEM)]
        + [hbm if i in far[0] else vmem for i in range(1, len(args))],
        out_specs=[hbm if i in far[1] else vmem for i in range(len(outs))],
        scratch_shapes=scratch,
        cost_estimate=pl.CostEstimate(flops=flops, transcendentals=0, bytes_accessed=moved),
        compiler_params=pltpu.CompilerParams(vmem_limit_bytes=20 << 20),
    )(*args)


def on_device(
    child_rhs, root_rhs, child_inverse, coupling_block, root_inverse, child_orders, coupling_rows
):
    n = child_rhs.shape[2]
    s1 = child_rhs.shape[1]
    q1 = s1 // ZL
    s0 = root_rhs.shape[0] * X * ZH
    q0 = s0 // ZL
    k = coupling_rows.shape[1]
    r1 = child_inverse.shape[1]
    block = root_rhs.shape[0]
    sub = lax.axis_index("x") * ZH + lax.axis_index("zh")
    place = jnp.stack([lax.axis_index("y"), lax.axis_index("core"), sub, child_orders[0]])
    idx = coupling_rows[0][:, None]
    shape = jax.ShapeDtypeStruct

    pair = jnp.concatenate([child_inverse[0], coupling_block[0]], axis=0)
    by_zl = gather_blocks(jnp.concatenate([pair, root_inverse.T], axis=1), "zl", ZL)
    own = jnp.concatenate(
        [by_zl[q, r1:, :s1] for q in range(ZL)]
        + [by_zl[q, :r1, : (q + 1) * q1] for q in reversed(range(ZL))],
        axis=1,
    )
    rt = after(by_zl[:, :, s1:], own)
    width = own.shape[1]

    up = {1: lax.ppermute(own, "y", FORTH)}
    down = {1: lax.ppermute(own, "y", BACK)}
    rz = lax.ppermute(rt, "zh", SWAP)
    low = lax.axis_index("zh") == 0
    rt = jnp.stack([jnp.where(low, rt, rz), jnp.where(low, rz, rt)])
    up[2] = lax.ppermute(up[1], "y", FORTH)
    down[2] = lax.ppermute(down[1], "y", BACK)
    rt = gather_blocks(rt, "x", X)
    half = own.shape[0]
    rt = jnp.concatenate(
        [
            rt[x, z, q, h * half : (h + 1) * half]
            for h in range(2) for q in range(ZL) for x in range(q, X) for z in range(ZH)
        ],
        axis=1,
    )
    early = jnp.stack([own, up[1], down[1], up[2], down[2]])
    early_far = lax.ppermute(early, "core", SWAP)
    both_up = lax.ppermute(jnp.concatenate([up[2], rt], axis=1), "y", FORTH)
    both_down = lax.ppermute(jnp.concatenate([down[2], rt], axis=1), "y", BACK)
    both_up2 = lax.ppermute(both_up, "y", FORTH)
    rdown2 = lax.ppermute(both_down[:, width:], "y", BACK)
    late = jnp.stack([both_up[:, :width], both_down[:, :width], both_up2[:, :width]])
    late_far = lax.ppermute(late, "core", SWAP)

    weights = [early, early_far, late, late_far]
    scratch = [pltpu.VMEM((s1, s1), BF), pltpu.VMEM((k, s1), BF)]
    flops = 2 * n * (s1 * s1 + k * s1 + k * s0)
    placed, solved = call(
        forward_kernel,
        [shape((n, s0), BF), shape((n, s1), F32)],
        [place, *weights, child_rhs[0], root_rhs, idx],
        [pltpu.VMEM((n, s1), F32), *scratch, pltpu.SemaphoreType.DMA],
        flops,
        ((), (1,)),
    )
    rup2 = after(both_up2[:, width:], placed)
    rup3 = lax.ppermute(rup2, "y", FORTH)
    rdown3 = lax.ppermute(after(rdown2, placed), "y", BACK)
    rearly = jnp.stack([rt, both_up[:, width:], both_down[:, width:], rup2, rdown2])
    rearly_far = lax.ppermute(rearly, "core", SWAP)
    parts = lax.all_to_all(placed.reshape(X, n // X, s0), "x", 0, 0, tiled=True)
    part = jnp.sum(parts.astype(F32), axis=0)
    far = lax.ppermute(part.astype(BF), "zh", SWAP)
    rup4 = lax.ppermute(rup3, "y", FORTH)
    rlate = jnp.stack([rup3, rdown3, rup4])
    rlate_far = lax.ppermute(rlate, "core", SWAP)
    s_t = (part + far.astype(F32)).astype(BF)

    x_t, = call(
        root_kernel,
        [shape((X, n // X, s0), BF)],
        [place, s_t, rearly, rearly_far, rlate, rlate_far],
        [pltpu.VMEM((q0, rt.shape[1] // 2), BF), pltpu.VMEM((n // X, s0), F32)],
        flops=2 * (n // X) * q0 * rt.shape[1],
    )
    x_all = lax.all_to_all(x_t, "x", 0, 0, tiled=True).reshape(n, s0)

    child_out, root_out = call(
        backward_kernel,
        [shape((s1, n), F32), shape((block, n), F32)],
        [place, x_all, solved, *weights, idx],
        [pltpu.VMEM((n, s1), F32), *scratch, pltpu.SemaphoreType.DMA],
        flops,
        ((2,), ()),
    )
    return (child_out[None], root_out)


def solution(mesh):
    fine = Mesh(mesh.devices.reshape(ZL, Y, CORE, X, ZH), (*SRC, *SUB))
    return jax.shard_map(
        on_device,
        mesh=fine,
        in_specs=(
            P(SUB, None, SRC),
            P(SUB, SRC),
            P(SUB, SRC, None),
            P(SUB, SRC, None),
            P(SUB, SRC),
            P(SUB),
            P(SUB, None),
        ),
        out_specs=(P(SUB, None, SRC), P(SUB, SRC)),
        check_vma=False,
    )
```

time: 178 us -> 244 us (1.37)
  the two profiles are of different devices: /device:TPU:16 before, /device:TPU:1 now
where the time goes in v4:
time: 244 us; the launch traced here: 241 us
  starting transfers between devices  85.2 us (35%)
  local copies, waits for them, and re-layouts  62.8 us (26%)
  waiting for transfers between devices  52.9 us (22%)
  blocking collectives  18.6 us (8%)
  Pallas kernels  15.9 us (7%)
  other arithmetic  3.59 us (1%)
    unnamed x76, local copies, waits for them, and re-layouts  56.5 us
    all_to_all x1, blocking collectives, on_device(): x_all = lax.all_to_all(x_t, 'x', 0, 0, tiled=True).reshape(n, s0)  18.6 us
    pallas_call x3, Pallas kernels, call(): pl.pallas_call(kernel, out_shape=outs, in_specs=[pl.BlockSpec(memory_spac...  15.9 us
    ppermute x1, waiting for transfers between devices, on_device(): both_up2 = lax.ppermute(both_up, 'y', FORTH)  14 us
    ppermute x1, waiting for transfers between devices, on_device(): far = lax.ppermute(part.astype(BF), 'zh', SWAP)  12.1 us
    all_to_all x2, starting transfers between devices, gather_blocks(): lax.all_to_all(jnp.broadcast_to(x[None], (length, *x.shape)), axis, 0, 0,...  11.8 us
    ppermute x1, waiting for transfers between devices, on_device(): both_down = lax.ppermute(jnp.concatenate([down[2], rt], axis=1), 'y', BACK)  10.7 us
    ppermute x1, starting transfers between devices, on_device(): rz = lax.ppermute(rt, 'zh', SWAP)  7.94 us
  transfers between devices with their start and end apart: 20, of which 10 were waited for; matrix products, arithmetic and copies ran while one was open for 26% of the time, Pallas kernels for 2%

profile of v4, /device:TPU:1, one launch (start us, length us, event | category | flops | bytes accessed | tf_op | source)
XLA Modules:
  0.0 240.8 jit_solution(4626769506806455449)
XLA Ops:
  2.2 7.8 %all-to-all-start = ((bf16[4,32,1280]{2,1,0:T(8,128)(2,1)}), bf16[4,32,1280]{2,1,0:T(8,128)(2,1)S(1)}, u32[]{:S(2)}, u32[]{:S(2)}) async-start(bf16[4,32,1280]{2,1,0:T(8,128)(2,1)} %broadcast_in_dim.6), calls=%async_computation | async-start | bytes 655360 | tf_op jit(solution)/shard_map/all_to_all | solution.py:20
  11.6 4.6 %all-to-all-done = bf16[4,32,1280]{2,1,0:T(8,128)(2,1)S(1)} async-done(((bf16[4,32,1280]{2,1,0:T(8,128)(2,1)}), bf16[4,32,1280]{2,1,0:T(8,128)(2,1)S(1)}, u32[]{:S(2)}, u32[]{:S(2)}) %all-to-all-start) | async-done | bytes 327712 | tf_op jit(solution)/shard_map/all_to_all | solution.py:20
  16.3 7.5 %collective-permute-start.1 = (bf16[16,6656]{1,0:T(8,128)(2,1)S(1)}, bf16[16,6656]{1,0:T(8,128)(2,1)S(1)}, u32[]{:S(2)}, u32[]{:S(2)}) collective-permute-start(bf16[16,6656]{1,0:T(8,128)(2,1)S(1)} %constant_dynamic-update-slice_fusion), channel_id=1, source_target_pairs={{0,112},{16,0},{32,16},{48,32},{64,48},{80,64},{96,80},{112,96},{1... | collective-permute-start | bytes 638984 | tf_op jit(solution)/shard_map/ppermute | solution.py:198
  23.8 1.9 collective-permute-start
  25.8 7.9 %collective-permute-start.5 = (bf16[4,32,256]{2,1,0:T(8,128)(2,1)S(1)}, bf16[4,32,256]{2,1,0:T(8,128)(2,1)S(1)}, u32[]{:S(2)}, u32[]{:S(2)}) collective-permute-start(bf16[4,32,256]{2,1,0:T(8,128)(2,1)S(1)} %slice.229), channel_id=1, source_target_pairs={{0,1},{1,0},{2,3},{3,2},{4,5},{5,4},{6,7},{7,6},{8,9},{9,8},{10,11... | collective-permute-start | bytes 196616 | tf_op jit(solution)/shard_map/ppermute | solution.py:199
  36.3 4.0 %all-to-all-start.1 = ((bf16[4,2,4,32,256]{4,3,2,1,0:T(8,128)(2,1)}), bf16[4,2,4,32,256]{4,3,2,1,0:T(8,128)(2,1)S(1)}, u32[]{:S(2)}, u32[]{:S(2)}) async-start(bf16[4,2,4,32,256]{4,3,2,1,0:T(8,128)(2,1)} %broadcast_in_dim.7), calls=%async_computation.1 | async-start | bytes 1048576 | tf_op jit(solution)/shard_map/all_to_all | solution.py:20
  40.3 4.5 %collective-permute-start.3 = (bf16[16,6656]{1,0:T(8,128)(2,1)S(1)}, bf16[16,6656]{1,0:T(8,128)(2,1)S(1)}, u32[]{:S(2)}, u32[]{:S(2)}) collective-permute-start(bf16[16,6656]{1,0:T(8,128)(2,1)S(1)} %collective-permute-done.1), channel_id=1, source_target_pairs={{0,112},{16,0},{32,16},{48,32},{64,48},{80,64},{96,80},{112,96},{1... | collective-permute-start | bytes 638984 | tf_op jit(solution)/shard_map/ppermute | solution.py:203
  44.8 1.9 collective-permute-start.2
  48.2 4.5 %collective-permute-done.2 = bf16[16,6656]{1,0:T(8,128)(2,1)S(1)} collective-permute-done((bf16[16,6656]{1,0:T(8,128)(2,1)S(1)}, bf16[16,6656]{1,0:T(8,128)(2,1)S(1)}, u32[]{:S(2)}, u32[]{:S(2)}) %collective-permute-start.2) | collective-permute-done | bytes 213024 | tf_op jit(solution)/shard_map/ppermute | solution.py:202
  54.0 7.7 %collective-permute-start.4 = (bf16[5,16,6656]{2,1,0:T(8,128)(2,1)}, bf16[5,16,6656]{2,1,0:T(8,128)(2,1)}, u32[]{:S(2)}, u32[]{:S(2)}) collective-permute-start(bf16[5,16,6656]{2,1,0:T(8,128)(2,1)} %constant_dynamic-update-slice_fusion.8.early_ref), channel_id=1, source_target_pairs={{0,8},{8,0},{1,9},{9,1},{2,10},{10,2},{3,11},{11,3},{4,12},{12,4},... | collective-permute-start | bytes 3194888 | tf_op jit(solution)/shard_map/ppermute | solution.py:214
  105.5 1.3 constant_dynamic-update-slice_fusion.101
  114.6 1.9 collective-permute-start.7
  116.5 3.4 %collective-permute-start.6 = (bf16[16,16896]{1,0:T(8,128)(2,1)}, bf16[16,16896]{1,0:T(8,128)(2,1)S(1)}, u32[]{:S(2)}, u32[]{:S(2)}) collective-permute-start(bf16[16,16896]{1,0:T(8,128)(2,1)} %get-tuple-element.18), channel_id=1, source_target_pairs={{0,16},{16,32},{32,48},{48,64},{64,80},{80,96},{96,112},{112,0},{1... | collective-permute-start | bytes 1622024 | tf_op jit(solution)/shard_map/ppermute | solution.py:215
  119.9 10.7 %collective-permute-done.7 = bf16[16,16896]{1,0:T(8,128)(2,1)S(1)} collective-permute-done((bf16[16,16896]{1,0:T(8,128)(2,1)}, bf16[16,16896]{1,0:T(8,128)(2,1)S(1)}, u32[]{:S(2)}, u32[]{:S(2)}) %collective-permute-start.7) | collective-permute-done | bytes 540704 | tf_op jit(solution)/shard_map/ppermute | solution.py:216
  130.6 3.3 %collective-permute-start.11 = (bf16[16,10240]{1,0:T(8,128)(2,1)S(1)}, bf16[16,10240]{1,0:T(8,128)(2,1)}, u32[]{:S(2)}, u32[]{:S(2)}) collective-permute-start(bf16[16,10240]{1,0:T(8,128)(2,1)S(1)} %slice.274), channel_id=1, source_target_pairs={{0,112},{16,0},{32,16},{48,32},{64,48},{80,64},{96,80},{112,96},{1... | collective-permute-start | bytes 983048 | tf_op jit(solution)/shard_map/ppermute | solution.py:218
  134.0 1.9 collective-permute-start.8
  136.0 14.0 %collective-permute-done.8 = bf16[16,16896]{1,0:T(8,128)(2,1)S(1)} collective-permute-done((bf16[16,16896]{1,0:T(8,128)(2,1)S(1)}, bf16[16,16896]{1,0:T(8,128)(2,1)S(1)}, u32[]{:S(2)}, u32[]{:S(2)}) %collective-permute-start.8) | collective-permute-done | bytes 540704 | tf_op jit(solution)/shard_map/ppermute | solution.py:217
  150.1 3.7 %collective-permute-start.9 = (bf16[3,16,6656]{2,1,0:T(8,128)(2,1)S(1)}, bf16[3,16,6656]{2,1,0:T(8,128)(2,1)S(1)}, u32[]{:S(2)}, u32[]{:S(2)}) collective-permute-start(bf16[3,16,6656]{2,1,0:T(8,128)(2,1)S(1)} %pad_maximum_fusion.1.late_ref), channel_id=1, source_target_pairs={{0,8},{8,0},{1,9},{9,1},{2,10},{10,2},{3,11},{11,3},{4,12},{12,4},... | collective-permute-start | bytes 1916936 | tf_op jit(solution)/shard_map/ppermute | solution.py:220
  155.5 5.6 %shard_map.86 = (bf16[256,2048]{1,0:T(8,128)(2,1)}, f32[256,1024]{1,0:T(8,128)S(1)}) custom-call(s32[4]{0:T(128)S(1)} %pad_add_fusion.place_ref, bf16[5,16,6656]{2,1,0:T(8,128)(2,1)} %constant_dynamic-update-slice_fusion.8.early_ref, bf16[5,16,6656]{2,1,0:T(8,128)(2,1)} %collective-permute-done.4.early_far_ref, ...), custom_call_target="tpu_custom_call" | custom-call | flops 2147483648 | bytes 6819856 | tf_op jit(solution)/shard_map/pallas_call | solution.py:159
  162.2 1.9 collective-permute-start.13
  165.1 4.5 %all-to-all-start.2 = ((bf16[4,64,2048]{2,1,0:T(8,128)(2,1)}), bf16[4,64,2048]{2,1,0:T(8,128)(2,1)}, u32[]{:S(2)}, u32[]{:S(2)}) async-start(bf16[4,64,2048]{2,1,0:T(8,128)(2,1)} %bitcast.66), calls=%async_computation.2 | async-start | bytes 2097152 | tf_op jit(solution)/shard_map/all_to_all | solution.py:238
  169.6 4.6 %collective-permute-start.14 = (bf16[16,10240]{1,0:T(8,128)(2,1)}, bf16[16,10240]{1,0:T(8,128)(2,1)S(1)}, u32[]{:S(2)}, u32[]{:S(2)}) collective-permute-start(bf16[16,10240]{1,0:T(8,128)(2,1)} %collective-permute-done.11), channel_id=1, source_target_pairs={{0,112},{16,0},{32,16},{48,32},{64,48},{80,64},{96,80},{112,96},{1... | collective-permute-start | bytes 983048 | tf_op jit(solution)/shard_map/ppermute | solution.py:235
  174.4 1.9 collective-permute-start.15
  177.3 3.1 %collective-permute-start.12 = (bf16[5,16,10240]{2,1,0:T(8,128)(2,1)S(1)}, bf16[5,16,10240]{2,1,0:T(8,128)(2,1)}, u32[]{:S(2)}, u32[]{:S(2)}) collective-permute-start(bf16[5,16,10240]{2,1,0:T(8,128)(2,1)S(1)} %bitcast_dynamic-update-slice_fusion.early_ref), channel_id=1, source_target_pairs={{0,8},{8,0},{1,9},{9,1},{2,10},{10,2},{3,11},{11,3},{4,12},{12,4},... | collective-permute-start | bytes 4915208 | tf_op jit(solution)/shard_map/ppermute | solution.py:237
  180.6 4.9 %collective-permute-done.15 = bf16[16,10240]{1,0:T(8,128)(2,1)S(1)} collective-permute-done((bf16[16,10240]{1,0:T(8,128)(2,1)S(1)}, bf16[16,10240]{1,0:T(8,128)(2,1)S(1)}, u32[]{:S(2)}, u32[]{:S(2)}) %collective-permute-start.15) | collective-permute-done | bytes 327712 | tf_op jit(solution)/shard_map/ppermute | solution.py:241
  186.6 4.0 %collective-permute-start.16 = (bf16[3,16,10240]{2,1,0:T(8,128)(2,1)S(1)}, bf16[3,16,10240]{2,1,0:T(8,128)(2,1)}, u32[]{:S(2)}, u32[]{:S(2)}) collective-permute-start(bf16[3,16,10240]{2,1,0:T(8,128)(2,1)S(1)} %pad_maximum_fusion.late_ref), channel_id=1, source_target_pairs={{0,8},{8,0},{1,9},{9,1},{2,10},{10,2},{3,11},{11,3},{4,12},{12,4},... | collective-permute-start | bytes 2949128 | tf_op jit(solution)/shard_map/ppermute | solution.py:243
  190.6 1.4 convert_reduce_fusion
  192.1 7.5 %collective-permute-start.10 = (bf16[64,2048]{1,0:T(8,128)(2,1)S(1)}, bf16[64,2048]{1,0:T(8,128)(2,1)S(1)}, u32[]{:S(2)}, u32[]{:S(2)}) collective-permute-start(bf16[64,2048]{1,0:T(8,128)(2,1)S(1)} %convert_element_type.13), channel_id=1, source_target_pairs={{0,1},{1,0},{2,3},{3,2},{4,5},{5,4},{6,7},{7,6},{8,9},{9,8},{10,11... | collective-permute-start | bytes 786440 | tf_op jit(solution)/shard_map/ppermute | solution.py:240
  199.6 12.1 %collective-permute-done.10 = bf16[64,2048]{1,0:T(8,128)(2,1)S(1)} collective-permute-done((bf16[64,2048]{1,0:T(8,128)(2,1)S(1)}, bf16[64,2048]{1,0:T(8,128)(2,1)S(1)}, u32[]{:S(2)}, u32[]{:S(2)}) %collective-permute-start.10) | collective-permute-done | bytes 262176 | tf_op jit(solution)/shard_map/ppermute | solution.py:240
  211.8 4.8 %shard_map.87 = bf16[4,64,2048]{2,1,0:T(8,128)(2,1)S(1)} custom-call(s32[4]{0:T(128)S(1)} %pad_add_fusion.place_ref, bf16[64,2048]{1,0:T(8,128)(2,1)S(1)} %add_convert_fusion.s_ref, bf16[5,16,10240]{2,1,0:T(8,128)(2,1)S(1)} %bitcast_dynamic-update-slice_fusion.early_ref, bf16[5,16,10240]{2,1,0:T(8,128)(2,1)} %collective-permute-done.12.early_far_ref, ...), custom_call_target="tpu_custom_call" | custom-call | flops 671088640 | bytes 6553616 | tf_op jit(solution)/shard_map/pallas_call | solution.py:159
  216.6 18.6 %all_to_all.20 = bf16[4,64,2048]{2,1,0:T(8,128)(2,1)S(1)} all-to-all(bf16[4,64,2048]{2,1,0:T(8,128)(2,1)S(1)} %shard_map.87), channel_id=1, replica_groups=mesh['zl'=4,'y'=8,'core'=2,'x'=4,'zh'=2] {'x'}, dimensions={0} | all-to-all | bytes 2097152 | tf_op jit(solution)/shard_map/all_to_all | solution.py:253
  235.3 5.5 %shard_map.88 = (f32[1024,256]{1,0:T(8,128)}, f32[256,256]{1,0:T(8,128)}) custom-call(s32[4]{0:T(128)S(1)} %pad_add_fusion.place_ref, bf16[256,2048]{1,0:T(8,128)(2,1)S(1)} %bitcast.398, f32[256,1024]{1,0:T(8,128)S(1)} %copy-done.7, bf16[5,16,6656]{2,1,0:T(8,128)(2,1)} %constant_dynamic-update-slice_fusion.8.early_ref, ...), custom_call_target="tpu_custom_call" | custom-call | flops 2147483648 | bytes 6819856 | tf_op jit(solution)/shard_map/pallas_call | solution.py:159
  (110 shorter events, 65.9 us)
Async XLA Ops:
  2.2 14.0 %all-to-all-start = ((bf16[4,32,1280]{2,1,0:T(8,128)(2,1)}), bf16[4,32,1280]{2,1,0:T(8,128)(2,1)S(1)}, u32[]{:S(2)}, u32[]{:S(2)}) async-start(bf16[4,32,1280]{2,1,0:T(8,128)(2,1)} %broadcast_in_dim.6), calls=%async_computation | async-start | bytes 655360 | tf_op jit(solution)/shard_map/all_to_all | solution.py:20
  11.5 143.9 %copy-start = (s32[1024,1]{1,0:T(8,128)}, s32[1024,1]{1,0:T(8,128)S(1)}, u32[]{:S(2)}) copy-start(s32[1024,1]{1,0:T(8,128)S(1)} %copy.9.idx_ref) | copy-start | bytes 12292
  16.3 24.0 %collective-permute-start.1 = (bf16[16,6656]{1,0:T(8,128)(2,1)S(1)}, bf16[16,6656]{1,0:T(8,128)(2,1)S(1)}, u32[]{:S(2)}, u32[]{:S(2)}) collective-permute-start(bf16[16,6656]{1,0:T(8,128)(2,1)S(1)} %constant_dynamic-update-slice_fusion), channel_id=1, source_target_pairs={{0,112},{16,0},{32,16},{48,32},{64,48},{80,64},{96,80},{112,96},{1... | collective-permute-start | bytes 638984 | tf_op jit(solution)/shard_map/ppermute | solution.py:198
  23.8 21.0 %collective-permute-start = (bf16[16,6656]{1,0:T(8,128)(2,1)S(1)}, bf16[16,6656]{1,0:T(8,128)(2,1)S(1)}, u32[]{:S(2)}, u32[]{:S(2)}) collective-permute-start(bf16[16,6656]{1,0:T(8,128)(2,1)S(1)} %constant_dynamic-update-slice_fusion), channel_id=1, source_target_pairs={{0,16},{16,32},{32,48},{48,64},{64,80},{80,96},{96,112},{112,0},{1... | collective-permute-start | bytes 638984 | tf_op jit(solution)/shard_map/ppermute | solution.py:197
  25.8 9.6 %collective-permute-start.5 = (bf16[4,32,256]{2,1,0:T(8,128)(2,1)S(1)}, bf16[4,32,256]{2,1,0:T(8,128)(2,1)S(1)}, u32[]{:S(2)}, u32[]{:S(2)}) collective-permute-start(bf16[4,32,256]{2,1,0:T(8,128)(2,1)S(1)} %slice.229), channel_id=1, source_target_pairs={{0,1},{1,0},{2,3},{3,2},{4,5},{5,4},{6,7},{7,6},{8,9},{9,8},{10,11... | collective-permute-start | bytes 196616 | tf_op jit(solution)/shard_map/ppermute | solution.py:199
  36.3 26.8 %all-to-all-start.1 = ((bf16[4,2,4,32,256]{4,3,2,1,0:T(8,128)(2,1)}), bf16[4,2,4,32,256]{4,3,2,1,0:T(8,128)(2,1)S(1)}, u32[]{:S(2)}, u32[]{:S(2)}) async-start(bf16[4,2,4,32,256]{4,3,2,1,0:T(8,128)(2,1)} %broadcast_in_dim.7), calls=%async_computation.1 | async-start | bytes 1048576 | tf_op jit(solution)/shard_map/all_to_all | solution.py:20
  40.3 13.1 %collective-permute-start.3 = (bf16[16,6656]{1,0:T(8,128)(2,1)S(1)}, bf16[16,6656]{1,0:T(8,128)(2,1)S(1)}, u32[]{:S(2)}, u32[]{:S(2)}) collective-permute-start(bf16[16,6656]{1,0:T(8,128)(2,1)S(1)} %collective-permute-done.1), channel_id=1, source_target_pairs={{0,112},{16,0},{32,16},{48,32},{64,48},{80,64},{96,80},{112,96},{1... | collective-permute-start | bytes 638984 | tf_op jit(solution)/shard_map/ppermute | solution.py:203
  44.8 7.8 %collective-permute-start.2 = (bf16[16,6656]{1,0:T(8,128)(2,1)S(1)}, bf16[16,6656]{1,0:T(8,128)(2,1)S(1)}, u32[]{:S(2)}, u32[]{:S(2)}) collective-permute-start(bf16[16,6656]{1,0:T(8,128)(2,1)S(1)} %collective-permute-done), channel_id=1, source_target_pairs={{0,16},{16,32},{32,48},{48,64},{64,80},{80,96},{96,112},{112,0},{1... | collective-permute-start | bytes 638984 | tf_op jit(solution)/shard_map/ppermute | solution.py:202
  54.0 100.5 %collective-permute-start.4 = (bf16[5,16,6656]{2,1,0:T(8,128)(2,1)}, bf16[5,16,6656]{2,1,0:T(8,128)(2,1)}, u32[]{:S(2)}, u32[]{:S(2)}) collective-permute-start(bf16[5,16,6656]{2,1,0:T(8,128)(2,1)} %constant_dynamic-update-slice_fusion.8.early_ref), channel_id=1, source_target_pairs={{0,8},{8,0},{1,9},{9,1},{2,10},{10,2},{3,11},{11,3},{4,12},{12,4},... | collective-permute-start | bytes 3194888 | tf_op jit(solution)/shard_map/ppermute | solution.py:214
  63.1 0.8 copy-start.8
  114.6 16.0 %collective-permute-start.7 = (bf16[16,16896]{1,0:T(8,128)(2,1)}, bf16[16,16896]{1,0:T(8,128)(2,1)S(1)}, u32[]{:S(2)}, u32[]{:S(2)}) collective-permute-start(bf16[16,16896]{1,0:T(8,128)(2,1)} %get-tuple-element.17), channel_id=1, source_target_pairs={{0,112},{16,0},{32,16},{48,32},{64,48},{80,64},{96,80},{112,96},{1... | collective-permute-start | bytes 1622024 | tf_op jit(solution)/shard_map/ppermute | solution.py:216
  116.5 17.5 %collective-permute-start.6 = (bf16[16,16896]{1,0:T(8,128)(2,1)}, bf16[16,16896]{1,0:T(8,128)(2,1)S(1)}, u32[]{:S(2)}, u32[]{:S(2)}) collective-permute-start(bf16[16,16896]{1,0:T(8,128)(2,1)} %get-tuple-element.18), channel_id=1, source_target_pairs={{0,16},{16,32},{32,48},{48,64},{64,80},{80,96},{96,112},{112,0},{1... | collective-permute-start | bytes 1622024 | tf_op jit(solution)/shard_map/ppermute | solution.py:215
  130.6 34.5 %collective-permute-start.11 = (bf16[16,10240]{1,0:T(8,128)(2,1)S(1)}, bf16[16,10240]{1,0:T(8,128)(2,1)}, u32[]{:S(2)}, u32[]{:S(2)}) collective-permute-start(bf16[16,10240]{1,0:T(8,128)(2,1)S(1)} %slice.274), channel_id=1, source_target_pairs={{0,112},{16,0},{32,16},{48,32},{64,48},{80,64},{96,80},{112,96},{1... | collective-permute-start | bytes 983048 | tf_op jit(solution)/shard_map/ppermute | solution.py:218
  134.0 16.0 %collective-permute-start.8 = (bf16[16,16896]{1,0:T(8,128)(2,1)S(1)}, bf16[16,16896]{1,0:T(8,128)(2,1)S(1)}, u32[]{:S(2)}, u32[]{:S(2)}) collective-permute-start(bf16[16,16896]{1,0:T(8,128)(2,1)S(1)} %collective-permute-done.6), channel_id=1, source_target_pairs={{0,16},{16,32},{32,48},{48,64},{64,80},{80,96},{96,112},{112,0},{1... | collective-permute-start | bytes 1622024 | tf_op jit(solution)/shard_map/ppermute | solution.py:217
  136.0 19.5 %copy-start.2 = (f32[1,1024,256]{2,1,0:T(8,128)S(1)}, f32[1,1024,256]{2,1,0:T(8,128)}, u32[]{:S(2)}) copy-start(f32[1,1024,256]{2,1,0:T(8,128)} %param.7) | copy-start | bytes 3145732
  136.0 19.5 %copy-start.5 = (f32[256,256]{1,0:T(8,128)S(1)}, f32[256,256]{1,0:T(8,128)}, u32[]{:S(2)}) copy-start(f32[256,256]{1,0:T(8,128)} %root_ref.1) | copy-start | bytes 786436
  150.1 5.4 %collective-permute-start.9 = (bf16[3,16,6656]{2,1,0:T(8,128)(2,1)S(1)}, bf16[3,16,6656]{2,1,0:T(8,128)(2,1)S(1)}, u32[]{:S(2)}, u32[]{:S(2)}) collective-permute-start(bf16[3,16,6656]{2,1,0:T(8,128)(2,1)S(1)} %pad_maximum_fusion.1.late_ref), channel_id=1, source_target_pairs={{0,8},{8,0},{1,9},{9,1},{2,10},{10,2},{3,11},{11,3},{4,12},{12,4},... | collective-permute-start | bytes 1916936 | tf_op jit(solution)/shard_map/ppermute | solution.py:220
  155.5 5.7 %copy-start.3 = (bf16[3,16,6656]{2,1,0:T(8,128)(2,1)}, bf16[3,16,6656]{2,1,0:T(8,128)(2,1)S(1)}, u32[]{:S(2)}) copy-start(bf16[3,16,6656]{2,1,0:T(8,128)(2,1)S(1)} %collective-permute-done.9.late_far_ref) | copy-start | bytes 1916932
  161.2 1.0 copy-start.6
  162.2 12.2 %collective-permute-start.13 = (bf16[16,10240]{1,0:T(8,128)(2,1)}, bf16[16,10240]{1,0:T(8,128)(2,1)S(1)}, u32[]{:S(2)}, u32[]{:S(2)}) collective-permute-start(bf16[16,10240]{1,0:T(8,128)(2,1)} %slice.275), channel_id=1, source_target_pairs={{0,16},{16,32},{32,48},{48,64},{64,80},{80,96},{96,112},{112,0},{1... | collective-permute-start | bytes 983048 | tf_op jit(solution)/shard_map/ppermute | solution.py:234
  165.1 25.5 %all-to-all-start.2 = ((bf16[4,64,2048]{2,1,0:T(8,128)(2,1)}), bf16[4,64,2048]{2,1,0:T(8,128)(2,1)}, u32[]{:S(2)}, u32[]{:S(2)}) async-start(bf16[4,64,2048]{2,1,0:T(8,128)(2,1)} %bitcast.66), calls=%async_computation.2 | async-start | bytes 2097152 | tf_op jit(solution)/shard_map/all_to_all | solution.py:238
  169.6 10.9 %collective-permute-start.14 = (bf16[16,10240]{1,0:T(8,128)(2,1)}, bf16[16,10240]{1,0:T(8,128)(2,1)S(1)}, u32[]{:S(2)}, u32[]{:S(2)}) collective-permute-start(bf16[16,10240]{1,0:T(8,128)(2,1)} %collective-permute-done.11), channel_id=1, source_target_pairs={{0,112},{16,0},{32,16},{48,32},{64,48},{80,64},{96,80},{112,96},{1... | collective-permute-start | bytes 983048 | tf_op jit(solution)/shard_map/ppermute | solution.py:235
  174.4 11.1 %copy-start.9 = (bf16[16,10240]{1,0:T(8,128)(2,1)}, bf16[16,10240]{1,0:T(8,128)(2,1)S(1)}, u32[]{:S(2)}) copy-start(bf16[16,10240]{1,0:T(8,128)(2,1)S(1)} %collective-permute-done.13) | copy-start | bytes 983044
  174.4 11.1 %collective-permute-start.15 = (bf16[16,10240]{1,0:T(8,128)(2,1)S(1)}, bf16[16,10240]{1,0:T(8,128)(2,1)S(1)}, u32[]{:S(2)}, u32[]{:S(2)}) collective-permute-start(bf16[16,10240]{1,0:T(8,128)(2,1)S(1)} %collective-permute-done.13), channel_id=1, source_target_pairs={{0,16},{16,32},{32,48},{48,64},{64,80},{80,96},{96,112},{112,0},{1... | collective-permute-start | bytes 983048 | tf_op jit(solution)/shard_map/ppermute | solution.py:241
  177.3 34.5 %collective-permute-start.12 = (bf16[5,16,10240]{2,1,0:T(8,128)(2,1)S(1)}, bf16[5,16,10240]{2,1,0:T(8,128)(2,1)}, u32[]{:S(2)}, u32[]{:S(2)}) collective-permute-start(bf16[5,16,10240]{2,1,0:T(8,128)(2,1)S(1)} %bitcast_dynamic-update-slice_fusion.early_ref), channel_id=1, source_target_pairs={{0,8},{8,0},{1,9},{9,1},{2,10},{10,2},{3,11},{11,3},{4,12},{12,4},... | collective-permute-start | bytes 4915208 | tf_op jit(solution)/shard_map/ppermute | solution.py:237
  186.6 25.2 %collective-permute-start.16 = (bf16[3,16,10240]{2,1,0:T(8,128)(2,1)S(1)}, bf16[3,16,10240]{2,1,0:T(8,128)(2,1)}, u32[]{:S(2)}, u32[]{:S(2)}) collective-permute-start(bf16[3,16,10240]{2,1,0:T(8,128)(2,1)S(1)} %pad_maximum_fusion.late_ref), channel_id=1, source_target_pairs={{0,8},{8,0},{1,9},{9,1},{2,10},{10,2},{3,11},{11,3},{4,12},{12,4},... | collective-permute-start | bytes 2949128 | tf_op jit(solution)/shard_map/ppermute | solution.py:243
  192.1 19.6 %collective-permute-start.10 = (bf16[64,2048]{1,0:T(8,128)(2,1)S(1)}, bf16[64,2048]{1,0:T(8,128)(2,1)S(1)}, u32[]{:S(2)}, u32[]{:S(2)}) collective-permute-start(bf16[64,2048]{1,0:T(8,128)(2,1)S(1)} %convert_element_type.13), channel_id=1, source_target_pairs={{0,1},{1,0},{2,3},{3,2},{4,5},{5,4},{6,7},{7,6},{8,9},{9,8},{10,11... | collective-permute-start | bytes 786440 | tf_op jit(solution)/shard_map/ppermute | solution.py:240
  211.8 23.4 %copy-start.7 = (f32[256,1024]{1,0:T(8,128)S(1)}, f32[256,1024]{1,0:T(8,128)}, u32[]{:S(2)}) copy-start(f32[256,1024]{1,0:T(8,128)} %copy-done.6) | copy-start | bytes 3145732
  216.6 18.7 %copy-start.1 = (s32[1024,1]{1,0:T(8,128)S(1)}, s32[1024,1]{1,0:T(8,128)}, u32[]{:S(2)}) copy-start(s32[1024,1]{1,0:T(8,128)} %copy-done) | copy-start | bytes 12292
  216.6 18.7 %copy-start.4 = (bf16[3,16,6656]{2,1,0:T(8,128)(2,1)S(1)}, bf16[3,16,6656]{2,1,0:T(8,128)(2,1)}, u32[]{:S(2)}) copy-start(bf16[3,16,6656]{2,1,0:T(8,128)(2,1)} %copy-done.3) | copy-start | bytes 1916932

commit v5 on v4

--- a/solution.py
+++ b/solution.py
@@ -98,16 +98,13 @@
     here, core = place_ref[0], place_ref[1]
     s0 = s_ref.shape[1]
     q0 = s0 // ZL
-    half, width = r_ref.shape[0] // (Y * CORE * 2), r_ref.shape[1]
+    rc = early_ref.shape[1]
 
     def put(blocks_ref, steps, c):
         for j, step in enumerate(steps):
             y = lax.rem(here + (step + Y), Y)
-            at = pl.multiple_of(y * (CORE * 2 * half), CORE * 2 * half) + c * 2 * half
-            for h in range(2):
-                r_ref[pl.ds(at + h * half, half), :] = blocks_ref[
-                    j, :, h * width : (h + 1) * width
-                ]
+            at = pl.multiple_of(y * (CORE * rc), CORE * rc) + c * rc
+            r_ref[pl.ds(at, rc), :] = blocks_ref[j]
 
     by_core(core, (early_ref, early_far_ref), (late_ref, late_far_ref), put)
     left = 0
@@ -150,6 +147,16 @@
         out_ref[q * q1 : (q + 1) * q1, :] = jnp.where(rows + q * q1 < order, part.T, 0.0)
     at = pl.multiple_of(sub * block, block)
     root_ref[...] = x_ref[:, pl.ds(at, block)].astype(F32).T
+
+
+def pack_kernel(place_ref, r_ref, out_ref):
+    block = r_ref.shape[4]
+    left = 0
+    for q in range(ZL):
+        for x in range(q, X):
+            for z in range(ZH):
+                out_ref[:, left : left + block] = r_ref[x, z, q]
+                left += block
 
 
 def call(kernel, outs, args, scratch=(), flops=0, far=((), ())):
@@ -192,7 +199,6 @@
         axis=1,
     )
     rt = after(by_zl[:, :, s1:], own)
-    width = own.shape[1]
 
     up = {1: lax.ppermute(own, "y", FORTH)}
     down = {1: lax.ppermute(own, "y", BACK)}
@@ -202,21 +208,20 @@
     up[2] = lax.ppermute(up[1], "y", FORTH)
     down[2] = lax.ppermute(down[1], "y", BACK)
     rt = gather_blocks(rt, "x", X)
-    half = own.shape[0]
-    rt = jnp.concatenate(
-        [
-            rt[x, z, q, h * half : (h + 1) * half]
-            for h in range(2) for q in range(ZL) for x in range(q, X) for z in range(ZH)
-        ],
-        axis=1,
-    )
+    rwidth = block * ZH * sum(X - q for q in range(ZL))
+    rt, = call(pack_kernel, [shape((rt.shape[3], rwidth), BF)], [place, rt])
     early = jnp.stack([own, up[1], down[1], up[2], down[2]])
     early_far = lax.ppermute(early, "core", SWAP)
-    both_up = lax.ppermute(jnp.concatenate([up[2], rt], axis=1), "y", FORTH)
-    both_down = lax.ppermute(jnp.concatenate([down[2], rt], axis=1), "y", BACK)
-    both_up2 = lax.ppermute(both_up, "y", FORTH)
-    rdown2 = lax.ppermute(both_down[:, width:], "y", BACK)
-    late = jnp.stack([both_up[:, :width], both_down[:, :width], both_up2[:, :width]])
+    up[3] = lax.ppermute(up[2], "y", FORTH)
+    down[3] = lax.ppermute(down[2], "y", BACK)
+    up[4] = lax.ppermute(up[3], "y", FORTH)
+    rt = after(rt, up[3], down[3])
+    rup = {1: lax.ppermute(rt, "y", FORTH)}
+    rdown = {1: lax.ppermute(rt, "y", BACK)}
+    rup[2] = lax.ppermute(rup[1], "y", FORTH)
+    rdown[2] = lax.ppermute(rdown[1], "y", BACK)
+    last, ru, rd = lax.optimization_barrier((up[4], rup[1], rdown[1]))
+    late = jnp.stack([up[3], down[3], last])
     late_far = lax.ppermute(late, "core", SWAP)
 
     weights = [early, early_far, late, late_far]
@@ -230,16 +235,15 @@
         flops,
         ((), (1,)),
     )
-    rup2 = after(both_up2[:, width:], placed)
-    rup3 = lax.ppermute(rup2, "y", FORTH)
-    rdown3 = lax.ppermute(after(rdown2, placed), "y", BACK)
-    rearly = jnp.stack([rt, both_up[:, width:], both_down[:, width:], rup2, rdown2])
+    rup[3] = lax.ppermute(after(rup[2], placed), "y", FORTH)
+    rdown[3] = lax.ppermute(after(rdown[2], placed), "y", BACK)
+    rearly = jnp.stack([rt, ru, rd, rup[2], rdown[2]])
     rearly_far = lax.ppermute(rearly, "core", SWAP)
     parts = lax.all_to_all(placed.reshape(X, n // X, s0), "x", 0, 0, tiled=True)
     part = jnp.sum(parts.astype(F32), axis=0)
     far = lax.ppermute(part.astype(BF), "zh", SWAP)
-    rup4 = lax.ppermute(rup3, "y", FORTH)
-    rlate = jnp.stack([rup3, rdown3, rup4])
+    rup[4] = lax.ppermute(rup[3], "y", FORTH)
+    rlate = jnp.stack([rup[3], rdown[3], rup[4]])
     rlate_far = lax.ppermute(rlate, "core", SWAP)
     s_t = (part + far.astype(F32)).astype(BF)
 
@@ -247,8 +251,8 @@
         root_kernel,
         [shape((X, n // X, s0), BF)],
         [place, s_t, rearly, rearly_far, rlate, rlate_far],
-        [pltpu.VMEM((q0, rt.shape[1] // 2), BF), pltpu.VMEM((n // X, s0), F32)],
-        flops=2 * (n // X) * q0 * rt.shape[1],
+        [pltpu.VMEM((q0, rwidth), BF), pltpu.VMEM((n // X, s0), F32)],
+        flops=4 * (n // X) * q0 * rwidth,
     )
     x_all = lax.all_to_all(x_t, "x", 0, 0, tiled=True).reshape(n, s0)
 

time: 244 us -> 184 us (0.75)
  local copies, waits for them, and re-layouts: 62.8 us -> 8.87 us
  waiting for transfers between devices: 52.9 us -> 36.1 us
  starting transfers between devices: 85.2 us -> 96.1 us
    unnamed x76 -> x39, local copies, waits for them, and re-layouts: 56.5 us -> 5.65 us
    ppermute x7 -> x10, waiting for transfers between devices: 29.9 us -> 18.5 us  [the longest x1 12.8 us: on_device(): up[4] = lax.ppermute(up[3], 'y', FORTH)]
    ppermute x7 -> x10, starting transfers between devices: 18.9 us -> 30.2 us  [the longest x1 4.98 us: on_device(): rdown = {1: lax.ppermute(rt, 'y', BACK)}]
    ppermute x1, waiting for transfers between devices: 4.49 us -> 0.01 us  [on_device(): up[2] = lax.ppermute(up[1], 'y', FORTH)]
    pallas_call x3 -> x4, Pallas kernels: 15.9 us -> 16.4 us  [call(): pl.pallas_call(kernel, out_shape=outs, in_specs=[pl.BlockSpec(memory_spac...]
  transfers between devices with their start and end apart: 20 -> 23, of which waited for: 10 -> 6; matrix products, arithmetic and copies ran while one was open for 26% -> 6% of each run, Pallas kernels for 2% -> 3%
where the time goes in v5:
time: 184 us; the launch traced here: 182 us
  starting transfers between devices  96.1 us (52%)
  waiting for transfers between devices  36.1 us (20%)
  blocking collectives  18.4 us (10%)
  Pallas kernels  16.4 us (9%)
  local copies, waits for them, and re-layouts  8.87 us (5%)
  other arithmetic  4.52 us (2%)
    all_to_all x1, blocking collectives, on_device(): x_all = lax.all_to_all(x_t, 'x', 0, 0, tiled=True).reshape(n, s0)  18.4 us
    pallas_call x4, Pallas kernels, call(): pl.pallas_call(kernel, out_shape=outs, in_specs=[pl.BlockSpec(memory_spac...  16.4 us
    ppermute x1, waiting for transfers between devices, on_device(): up[4] = lax.ppermute(up[3], 'y', FORTH)  12.8 us
    ppermute x1, waiting for transfers between devices, on_device(): far = lax.ppermute(part.astype(BF), 'zh', SWAP)  12.1 us
    all_to_all x2, starting transfers between devices, gather_blocks(): lax.all_to_all(jnp.broadcast_to(x[None], (length, *x.shape)), axis, 0, 0,...  11.8 us
    ppermute x1, starting transfers between devices, on_device(): rz = lax.ppermute(rt, 'zh', SWAP)  7.94 us
    ppermute x1, starting transfers between devices, on_device(): far = lax.ppermute(part.astype(BF), 'zh', SWAP)  7.55 us
    ppermute x1, starting transfers between devices, on_device(): early_far = lax.ppermute(early, 'core', SWAP)  7.54 us
  transfers between devices with their start and end apart: 23, of which 6 were waited for; matrix products, arithmetic and copies ran while one was open for 6% of the time, Pallas kernels for 3%

profile of v5, /device:TPU:1, one launch (start us, length us, event | category | flops | bytes accessed | tf_op | source)
XLA Modules:
  0.0 182.3 jit_solution(13924017811557068379)
XLA Ops:
  2.2 7.8 %all-to-all-start = ((bf16[4,32,1280]{2,1,0:T(8,128)(2,1)}), bf16[4,32,1280]{2,1,0:T(8,128)(2,1)S(1)}, u32[]{:S(2)}, u32[]{:S(2)}) async-start(bf16[4,32,1280]{2,1,0:T(8,128)(2,1)} %broadcast_in_dim.6), calls=%async_computation | async-start | bytes 655360 | tf_op jit(solution)/shard_map/all_to_all | solution.py:20
  11.6 4.6 %all-to-all-done = bf16[4,32,1280]{2,1,0:T(8,128)(2,1)S(1)} async-done(((bf16[4,32,1280]{2,1,0:T(8,128)(2,1)}), bf16[4,32,1280]{2,1,0:T(8,128)(2,1)S(1)}, u32[]{:S(2)}, u32[]{:S(2)}) %all-to-all-start) | async-done | bytes 327712 | tf_op jit(solution)/shard_map/all_to_all | solution.py:20
  16.3 7.5 %collective-permute-start.1 = (bf16[16,6656]{1,0:T(8,128)(2,1)S(1)}, bf16[16,6656]{1,0:T(8,128)(2,1)S(1)}, u32[]{:S(2)}, u32[]{:S(2)}) collective-permute-start(bf16[16,6656]{1,0:T(8,128)(2,1)S(1)} %constant_dynamic-update-slice_fusion), channel_id=1, source_target_pairs={{0,112},{16,0},{32,16},{48,32},{64,48},{80,64},{96,80},{112,96},{1... | collective-permute-start | bytes 638984 | tf_op jit(solution)/shard_map/ppermute | solution.py:204
  23.8 1.9 %collective-permute-start = (bf16[16,6656]{1,0:T(8,128)(2,1)S(1)}, bf16[16,6656]{1,0:T(8,128)(2,1)S(1)}, u32[]{:S(2)}, u32[]{:S(2)}) collective-permute-start(bf16[16,6656]{1,0:T(8,128)(2,1)S(1)} %constant_dynamic-update-slice_fusion), channel_id=1, source_target_pairs={{0,16},{16,32},{32,48},{48,64},{64,80},{80,96},{96,112},{112,0},{1... | collective-permute-start | bytes 638984 | tf_op jit(solution)/shard_map/ppermute | solution.py:203
  25.8 7.9 %collective-permute-start.8 = (bf16[4,32,256]{2,1,0:T(8,128)(2,1)S(1)}, bf16[4,32,256]{2,1,0:T(8,128)(2,1)S(1)}, u32[]{:S(2)}, u32[]{:S(2)}) collective-permute-start(bf16[4,32,256]{2,1,0:T(8,128)(2,1)S(1)} %slice.44), channel_id=1, source_target_pairs={{0,1},{1,0},{2,3},{3,2},{4,5},{5,4},{6,7},{7,6},{8,9},{9,8},{10,11... | collective-permute-start | bytes 196616 | tf_op jit(solution)/shard_map/ppermute | solution.py:205
  36.3 4.0 %all-to-all-start.1 = ((bf16[4,2,4,32,256]{4,3,2,1,0:T(8,128)(2,1)}), bf16[4,2,4,32,256]{4,3,2,1,0:T(8,128)(2,1)S(1)}, u32[]{:S(2)}, u32[]{:S(2)}) async-start(bf16[4,2,4,32,256]{4,3,2,1,0:T(8,128)(2,1)} %broadcast_in_dim.7), calls=%async_computation.1 | async-start | bytes 1048576 | tf_op jit(solution)/shard_map/all_to_all | solution.py:20
  40.3 4.5 %collective-permute-start.3 = (bf16[16,6656]{1,0:T(8,128)(2,1)S(1)}, bf16[16,6656]{1,0:T(8,128)(2,1)S(1)}, u32[]{:S(2)}, u32[]{:S(2)}) collective-permute-start(bf16[16,6656]{1,0:T(8,128)(2,1)S(1)} %collective-permute-done.1), channel_id=1, source_target_pairs={{0,112},{16,0},{32,16},{48,32},{64,48},{80,64},{96,80},{112,96},{1... | collective-permute-start | bytes 638984 | tf_op jit(solution)/shard_map/ppermute | solution.py:209
  44.8 1.9 %collective-permute-start.2 = (bf16[16,6656]{1,0:T(8,128)(2,1)S(1)}, bf16[16,6656]{1,0:T(8,128)(2,1)S(1)}, u32[]{:S(2)}, u32[]{:S(2)}) collective-permute-start(bf16[16,6656]{1,0:T(8,128)(2,1)S(1)} %collective-permute-done), channel_id=1, source_target_pairs={{0,16},{16,32},{32,48},{48,64},{64,80},{80,96},{96,112},{112,0},{1... | collective-permute-start | bytes 638984 | tf_op jit(solution)/shard_map/ppermute | solution.py:208
  48.2 4.6 %collective-permute-start.6 = (bf16[16,6656]{1,0:T(8,128)(2,1)S(1)}, bf16[16,6656]{1,0:T(8,128)(2,1)S(1)}, u32[]{:S(2)}, u32[]{:S(2)}) collective-permute-start(bf16[16,6656]{1,0:T(8,128)(2,1)S(1)} %collective-permute-done.3), channel_id=1, source_target_pairs={{0,112},{16,0},{32,16},{48,32},{64,48},{80,64},{96,80},{112,96},{1... | collective-permute-start | bytes 638984 | tf_op jit(solution)/shard_map/ppermute | solution.py:216
  52.7 1.9 %collective-permute-start.5 = (bf16[16,6656]{1,0:T(8,128)(2,1)S(1)}, bf16[16,6656]{1,0:T(8,128)(2,1)S(1)}, u32[]{:S(2)}, u32[]{:S(2)}) collective-permute-start(bf16[16,6656]{1,0:T(8,128)(2,1)S(1)} %collective-permute-done.2), channel_id=1, source_target_pairs={{0,16},{16,32},{32,48},{48,64},{64,80},{80,96},{96,112},{112,0},{1... | collective-permute-start | bytes 638984 | tf_op jit(solution)/shard_map/ppermute | solution.py:215
  56.1 7.5 %collective-permute-start.4 = (bf16[5,16,6656]{2,1,0:T(8,128)(2,1)}, bf16[5,16,6656]{2,1,0:T(8,128)(2,1)}, u32[]{:S(2)}, u32[]{:S(2)}) collective-permute-start(bf16[5,16,6656]{2,1,0:T(8,128)(2,1)} %bitcast_dynamic-update-slice_fusion.5.early_ref), channel_id=1, source_target_pairs={{0,8},{8,0},{1,9},{9,1},{2,10},{10,2},{3,11},{11,3},{4,12},{12,4},... | collective-permute-start | bytes 3194888 | tf_op jit(solution)/shard_map/ppermute | solution.py:214
  64.3 5.0 %collective-permute-start.10 = (bf16[32,5120]{1,0:T(8,128)(2,1)S(1)}, bf16[32,5120]{1,0:T(8,128)(2,1)S(1)}, u32[]{:S(2)}, u32[]{:S(2)}) collective-permute-start(bf16[32,5120]{1,0:T(8,128)(2,1)S(1)} %shard_map.86), channel_id=1, source_target_pairs={{0,112},{16,0},{32,16},{48,32},{64,48},{80,64},{96,80},{112,96},{1... | collective-permute-start | bytes 983048 | tf_op jit(solution)/shard_map/ppermute | solution.py:220
  69.3 1.9 %collective-permute-start.9 = (bf16[32,5120]{1,0:T(8,128)(2,1)S(1)}, bf16[32,5120]{1,0:T(8,128)(2,1)S(1)}, u32[]{:S(2)}, u32[]{:S(2)}) collective-permute-start(bf16[32,5120]{1,0:T(8,128)(2,1)S(1)} %shard_map.86), channel_id=1, source_target_pairs={{0,16},{16,32},{32,48},{48,64},{64,80},{80,96},{96,112},{112,0},{1... | collective-permute-start | bytes 983048 | tf_op jit(solution)/shard_map/ppermute | solution.py:219
  71.2 1.9 %collective-permute-start.7 = (bf16[16,6656]{1,0:T(8,128)(2,1)S(1)}, bf16[16,6656]{1,0:T(8,128)(2,1)S(1)}, u32[]{:S(2)}, u32[]{:S(2)}) collective-permute-start(bf16[16,6656]{1,0:T(8,128)(2,1)S(1)} %collective-permute-done.5), channel_id=1, source_target_pairs={{0,16},{16,32},{32,48},{48,64},{64,80},{80,96},{96,112},{112,0},{1... | collective-permute-start | bytes 638984 | tf_op jit(solution)/shard_map/ppermute | solution.py:217
  73.1 12.8 %collective-permute-done.7 = bf16[16,6656]{1,0:T(8,128)(2,1)S(1)} collective-permute-done((bf16[16,6656]{1,0:T(8,128)(2,1)S(1)}, bf16[16,6656]{1,0:T(8,128)(2,1)S(1)}, u32[]{:S(2)}, u32[]{:S(2)}) %collective-permute-start.7) | collective-permute-done | bytes 213024 | tf_op jit(solution)/shard_map/ppermute | solution.py:217
  87.0 3.0 %collective-permute-start.11 = (bf16[3,16,6656]{2,1,0:T(8,128)(2,1)S(1)}, bf16[3,16,6656]{2,1,0:T(8,128)(2,1)S(1)}, u32[]{:S(2)}, u32[]{:S(2)}) collective-permute-start(bf16[3,16,6656]{2,1,0:T(8,128)(2,1)S(1)} %pad_maximum_fusion.1.late_ref), channel_id=1, source_target_pairs={{0,8},{8,0},{1,9},{9,1},{2,10},{10,2},{3,11},{11,3},{4,12},{12,4},... | collective-permute-start | bytes 1916936 | tf_op jit(solution)/shard_map/ppermute | solution.py:225
  90.0 1.9 %collective-permute-start.13 = (bf16[32,5120]{1,0:T(8,128)(2,1)S(1)}, bf16[32,5120]{1,0:T(8,128)(2,1)}, u32[]{:S(2)}, u32[]{:S(2)}) collective-permute-start(bf16[32,5120]{1,0:T(8,128)(2,1)S(1)} %collective-permute-done.9), channel_id=1, source_target_pairs={{0,16},{16,32},{32,48},{48,64},{64,80},{80,96},{96,112},{112,0},{1... | collective-permute-start | bytes 983048 | tf_op jit(solution)/shard_map/ppermute | solution.py:221
  92.0 4.6 %collective-permute-start.14 = (bf16[32,5120]{1,0:T(8,128)(2,1)S(1)}, bf16[32,5120]{1,0:T(8,128)(2,1)S(1)}, u32[]{:S(2)}, u32[]{:S(2)}) collective-permute-start(bf16[32,5120]{1,0:T(8,128)(2,1)S(1)} %collective-permute-done.10), channel_id=1, source_target_pairs={{0,112},{16,0},{32,16},{48,32},{64,48},{80,64},{96,80},{112,96},{1... | collective-permute-start | bytes 983048 | tf_op jit(solution)/shard_map/ppermute | solution.py:222
  96.6 5.6 %shard_map.87 = (bf16[256,2048]{1,0:T(8,128)(2,1)}, f32[256,1024]{1,0:T(8,128)S(1)}) custom-call(s32[4]{0:T(128)S(1)} %pad_add_fusion.place_ref, bf16[5,16,6656]{2,1,0:T(8,128)(2,1)} %bitcast_dynamic-update-slice_fusion.5.early_ref, bf16[5,16,6656]{2,1,0:T(8,128)(2,1)} %collective-permute-done.4.early_far_ref, ...), custom_call_target="tpu_custom_call" | custom-call | flops 2147483648 | bytes 6819856 | tf_op jit(solution)/shard_map/pallas_call | solution.py:166
  103.2 1.9 %collective-permute-start.16 = (bf16[32,5120]{1,0:T(8,128)(2,1)}, bf16[32,5120]{1,0:T(8,128)(2,1)S(1)}, u32[]{:S(2)}, u32[]{:S(2)}) collective-permute-start(bf16[32,5120]{1,0:T(8,128)(2,1)} %collective-permute-done.13), channel_id=1, source_target_pairs={{0,16},{16,32},{32,48},{48,64},{64,80},{80,96},{96,112},{112,0},{1... | collective-permute-start | bytes 983048 | tf_op jit(solution)/shard_map/ppermute | solution.py:238
  106.9 4.6 %all-to-all-start.2 = ((bf16[4,64,2048]{2,1,0:T(8,128)(2,1)}), bf16[4,64,2048]{2,1,0:T(8,128)(2,1)}, u32[]{:S(2)}, u32[]{:S(2)}) async-start(bf16[4,64,2048]{2,1,0:T(8,128)(2,1)} %bitcast.26), calls=%async_computation.2 | async-start | bytes 2097152 | tf_op jit(solution)/shard_map/all_to_all | solution.py:242
  111.5 4.6 %collective-permute-start.17 = (bf16[32,5120]{1,0:T(8,128)(2,1)S(1)}, bf16[32,5120]{1,0:T(8,128)(2,1)S(1)}, u32[]{:S(2)}, u32[]{:S(2)}) collective-permute-start(bf16[32,5120]{1,0:T(8,128)(2,1)S(1)} %copy-done.9), channel_id=1, source_target_pairs={{0,112},{16,0},{32,16},{48,32},{64,48},{80,64},{96,80},{112,96},{1... | collective-permute-start | bytes 983048 | tf_op jit(solution)/shard_map/ppermute | solution.py:239
  116.1 1.9 %collective-permute-start.18 = (bf16[32,5120]{1,0:T(8,128)(2,1)S(1)}, bf16[32,5120]{1,0:T(8,128)(2,1)S(1)}, u32[]{:S(2)}, u32[]{:S(2)}) collective-permute-start(bf16[32,5120]{1,0:T(8,128)(2,1)S(1)} %collective-permute-done.16), channel_id=1, source_target_pairs={{0,16},{16,32},{32,48},{48,64},{64,80},{80,96},{96,112},{112,0},{1... | collective-permute-start | bytes 983048 | tf_op jit(solution)/shard_map/ppermute | solution.py:245
  118.1 3.3 %collective-permute-start.15 = (bf16[5,32,5120]{2,1,0:T(8,128)(2,1)S(1)}, bf16[5,32,5120]{2,1,0:T(8,128)(2,1)}, u32[]{:S(2)}, u32[]{:S(2)}) collective-permute-start(bf16[5,32,5120]{2,1,0:T(8,128)(2,1)S(1)} %bitcast_dynamic-update-slice_fusion.early_ref), channel_id=1, source_target_pairs={{0,8},{8,0},{1,9},{9,1},{2,10},{10,2},{3,11},{11,3},{4,12},{12,4},... | collective-permute-start | bytes 4915208 | tf_op jit(solution)/shard_map/ppermute | solution.py:241
  122.0 5.2 %collective-permute-done.18 = bf16[32,5120]{1,0:T(8,128)(2,1)S(1)} collective-permute-done((bf16[32,5120]{1,0:T(8,128)(2,1)S(1)}, bf16[32,5120]{1,0:T(8,128)(2,1)S(1)}, u32[]{:S(2)}, u32[]{:S(2)}) %collective-permute-start.18) | collective-permute-done | bytes 327712 | tf_op jit(solution)/shard_map/ppermute | solution.py:245
  128.2 4.1 %collective-permute-start.19 = (bf16[3,32,5120]{2,1,0:T(8,128)(2,1)S(1)}, bf16[3,32,5120]{2,1,0:T(8,128)(2,1)}, u32[]{:S(2)}, u32[]{:S(2)}) collective-permute-start(bf16[3,32,5120]{2,1,0:T(8,128)(2,1)S(1)} %pad_maximum_fusion.late_ref), channel_id=1, source_target_pairs={{0,8},{8,0},{1,9},{9,1},{2,10},{10,2},{3,11},{11,3},{4,12},{12,4},... | collective-permute-start | bytes 2949128 | tf_op jit(solution)/shard_map/ppermute | solution.py:247
  132.4 1.4 convert_reduce_fusion
  133.9 7.6 %collective-permute-start.12 = (bf16[64,2048]{1,0:T(8,128)(2,1)S(1)}, bf16[64,2048]{1,0:T(8,128)(2,1)S(1)}, u32[]{:S(2)}, u32[]{:S(2)}) collective-permute-start(bf16[64,2048]{1,0:T(8,128)(2,1)S(1)} %convert_element_type.13), channel_id=1, source_target_pairs={{0,1},{1,0},{2,3},{3,2},{4,5},{5,4},{6,7},{7,6},{8,9},{9,8},{10,11... | collective-permute-start | bytes 786440 | tf_op jit(solution)/shard_map/ppermute | solution.py:244
  141.4 12.1 %collective-permute-done.12 = bf16[64,2048]{1,0:T(8,128)(2,1)S(1)} collective-permute-done((bf16[64,2048]{1,0:T(8,128)(2,1)S(1)}, bf16[64,2048]{1,0:T(8,128)(2,1)S(1)}, u32[]{:S(2)}, u32[]{:S(2)}) %collective-permute-start.12) | collective-permute-done | bytes 262176 | tf_op jit(solution)/shard_map/ppermute | solution.py:244
  153.6 4.8 %shard_map.88 = bf16[4,64,2048]{2,1,0:T(8,128)(2,1)S(1)} custom-call(s32[4]{0:T(128)S(1)} %pad_add_fusion.place_ref, bf16[64,2048]{1,0:T(8,128)(2,1)S(1)} %add_convert_fusion.s_ref, bf16[5,32,5120]{2,1,0:T(8,128)(2,1)S(1)} %bitcast_dynamic-update-slice_fusion.early_ref, bf16[5,32,5120]{2,1,0:T(8,128)(2,1)} %collective-permute-done.15.early_far_ref, ...), custom_call_target="tpu_custom_call" | custom-call | flops 671088640 | bytes 6553616 | tf_op jit(solution)/shard_map/pallas_call | solution.py:166
  158.4 18.4 %all_to_all.20 = bf16[4,64,2048]{2,1,0:T(8,128)(2,1)S(1)} all-to-all(bf16[4,64,2048]{2,1,0:T(8,128)(2,1)S(1)} %shard_map.88), channel_id=1, replica_groups=mesh['zl'=4,'y'=8,'core'=2,'x'=4,'zh'=2] {'x'}, dimensions={0} | all-to-all | bytes 2097152 | tf_op jit(solution)/shard_map/all_to_all | solution.py:257
  176.8 5.5 %shard_map.89 = (f32[1024,256]{1,0:T(8,128)}, f32[256,256]{1,0:T(8,128)}) custom-call(s32[4]{0:T(128)S(1)} %pad_add_fusion.place_ref, bf16[256,2048]{1,0:T(8,128)(2,1)S(1)} %bitcast.73, f32[256,1024]{1,0:T(8,128)S(1)} %copy-done.7, bf16[5,16,6656]{2,1,0:T(8,128)(2,1)} %bitcast_dynamic-update-slice_fusion.5.early_ref, ...), custom_call_target="tpu_custom_call" | custom-call | flops 2147483648 | bytes 6819856 | tf_op jit(solution)/shard_map/pallas_call | solution.py:166
  (74 shorter events, 14.1 us)
Async XLA Ops:
  2.2 14.0 %all-to-all-start = ((bf16[4,32,1280]{2,1,0:T(8,128)(2,1)}), bf16[4,32,1280]{2,1,0:T(8,128)(2,1)S(1)}, u32[]{:S(2)}, u32[]{:S(2)}) async-start(bf16[4,32,1280]{2,1,0:T(8,128)(2,1)} %broadcast_in_dim.6), calls=%async_computation | async-start | bytes 655360 | tf_op jit(solution)/shard_map/all_to_all | solution.py:20
  11.5 85.0 %copy-start = (s32[1024,1]{1,0:T(8,128)}, s32[1024,1]{1,0:T(8,128)S(1)}, u32[]{:S(2)}) copy-start(s32[1024,1]{1,0:T(8,128)S(1)} %copy.9.idx_ref) | copy-start | bytes 12292
  16.3 24.0 %collective-permute-start.1 = (bf16[16,6656]{1,0:T(8,128)(2,1)S(1)}, bf16[16,6656]{1,0:T(8,128)(2,1)S(1)}, u32[]{:S(2)}, u32[]{:S(2)}) collective-permute-start(bf16[16,6656]{1,0:T(8,128)(2,1)S(1)} %constant_dynamic-update-slice_fusion), channel_id=1, source_target_pairs={{0,112},{16,0},{32,16},{48,32},{64,48},{80,64},{96,80},{112,96},{1... | collective-permute-start | bytes 638984 | tf_op jit(solution)/shard_map/ppermute | solution.py:204
  23.8 21.0 %collective-permute-start = (bf16[16,6656]{1,0:T(8,128)(2,1)S(1)}, bf16[16,6656]{1,0:T(8,128)(2,1)S(1)}, u32[]{:S(2)}, u32[]{:S(2)}) collective-permute-start(bf16[16,6656]{1,0:T(8,128)(2,1)S(1)} %constant_dynamic-update-slice_fusion), channel_id=1, source_target_pairs={{0,16},{16,32},{32,48},{48,64},{64,80},{80,96},{96,112},{112,0},{1... | collective-permute-start | bytes 638984 | tf_op jit(solution)/shard_map/ppermute | solution.py:203
  25.8 9.6 %collective-permute-start.8 = (bf16[4,32,256]{2,1,0:T(8,128)(2,1)S(1)}, bf16[4,32,256]{2,1,0:T(8,128)(2,1)S(1)}, u32[]{:S(2)}, u32[]{:S(2)}) collective-permute-start(bf16[4,32,256]{2,1,0:T(8,128)(2,1)S(1)} %slice.44), channel_id=1, source_target_pairs={{0,1},{1,0},{2,3},{3,2},{4,5},{5,4},{6,7},{7,6},{8,9},{9,8},{10,11... | collective-permute-start | bytes 196616 | tf_op jit(solution)/shard_map/ppermute | solution.py:205
  36.3 27.3 %all-to-all-start.1 = ((bf16[4,2,4,32,256]{4,3,2,1,0:T(8,128)(2,1)}), bf16[4,2,4,32,256]{4,3,2,1,0:T(8,128)(2,1)S(1)}, u32[]{:S(2)}, u32[]{:S(2)}) async-start(bf16[4,2,4,32,256]{4,3,2,1,0:T(8,128)(2,1)} %broadcast_in_dim.7), calls=%async_computation.1 | async-start | bytes 1048576 | tf_op jit(solution)/shard_map/all_to_all | solution.py:20
  40.3 7.9 %collective-permute-start.3 = (bf16[16,6656]{1,0:T(8,128)(2,1)S(1)}, bf16[16,6656]{1,0:T(8,128)(2,1)S(1)}, u32[]{:S(2)}, u32[]{:S(2)}) collective-permute-start(bf16[16,6656]{1,0:T(8,128)(2,1)S(1)} %collective-permute-done.1), channel_id=1, source_target_pairs={{0,112},{16,0},{32,16},{48,32},{64,48},{80,64},{96,80},{112,96},{1... | collective-permute-start | bytes 638984 | tf_op jit(solution)/shard_map/ppermute | solution.py:209
  44.8 7.9 %collective-permute-start.2 = (bf16[16,6656]{1,0:T(8,128)(2,1)S(1)}, bf16[16,6656]{1,0:T(8,128)(2,1)S(1)}, u32[]{:S(2)}, u32[]{:S(2)}) collective-permute-start(bf16[16,6656]{1,0:T(8,128)(2,1)S(1)} %collective-permute-done), channel_id=1, source_target_pairs={{0,16},{16,32},{32,48},{48,64},{64,80},{80,96},{96,112},{112,0},{1... | collective-permute-start | bytes 638984 | tf_op jit(solution)/shard_map/ppermute | solution.py:208
  48.2 16.1 %collective-permute-start.6 = (bf16[16,6656]{1,0:T(8,128)(2,1)S(1)}, bf16[16,6656]{1,0:T(8,128)(2,1)S(1)}, u32[]{:S(2)}, u32[]{:S(2)}) collective-permute-start(bf16[16,6656]{1,0:T(8,128)(2,1)S(1)} %collective-permute-done.3), channel_id=1, source_target_pairs={{0,112},{16,0},{32,16},{48,32},{64,48},{80,64},{96,80},{112,96},{1... | collective-permute-start | bytes 638984 | tf_op jit(solution)/shard_map/ppermute | solution.py:216
  52.7 11.5 %collective-permute-start.5 = (bf16[16,6656]{1,0:T(8,128)(2,1)S(1)}, bf16[16,6656]{1,0:T(8,128)(2,1)S(1)}, u32[]{:S(2)}, u32[]{:S(2)}) collective-permute-start(bf16[16,6656]{1,0:T(8,128)(2,1)S(1)} %collective-permute-done.2), channel_id=1, source_target_pairs={{0,16},{16,32},{32,48},{48,64},{64,80},{80,96},{96,112},{112,0},{1... | collective-permute-start | bytes 638984 | tf_op jit(solution)/shard_map/ppermute | solution.py:215
  56.1 40.5 %collective-permute-start.4 = (bf16[5,16,6656]{2,1,0:T(8,128)(2,1)}, bf16[5,16,6656]{2,1,0:T(8,128)(2,1)}, u32[]{:S(2)}, u32[]{:S(2)}) collective-permute-start(bf16[5,16,6656]{2,1,0:T(8,128)(2,1)} %bitcast_dynamic-update-slice_fusion.5.early_ref), channel_id=1, source_target_pairs={{0,8},{8,0},{1,9},{9,1},{2,10},{10,2},{3,11},{11,3},{4,12},{12,4},... | collective-permute-start | bytes 3194888 | tf_op jit(solution)/shard_map/ppermute | solution.py:214
  64.2 32.4 %copy-start.2 = (f32[1,1024,256]{2,1,0:T(8,128)S(1)}, f32[1,1024,256]{2,1,0:T(8,128)}, u32[]{:S(2)}) copy-start(f32[1,1024,256]{2,1,0:T(8,128)} %param.7) | copy-start | bytes 3145732
  64.2 32.4 %copy-start.5 = (f32[256,256]{1,0:T(8,128)S(1)}, f32[256,256]{1,0:T(8,128)}, u32[]{:S(2)}) copy-start(f32[256,256]{1,0:T(8,128)} %root_ref.1) | copy-start | bytes 786436
  64.3 21.7 %copy-start.11 = (bf16[16,6656]{1,0:T(8,128)(2,1)}, bf16[16,6656]{1,0:T(8,128)(2,1)S(1)}, u32[]{:S(2)}) copy-start(bf16[16,6656]{1,0:T(8,128)(2,1)S(1)} %collective-permute-done.5) | copy-start | bytes 638980
  64.3 21.7 %collective-permute-start.10 = (bf16[32,5120]{1,0:T(8,128)(2,1)S(1)}, bf16[32,5120]{1,0:T(8,128)(2,1)S(1)}, u32[]{:S(2)}, u32[]{:S(2)}) collective-permute-start(bf16[32,5120]{1,0:T(8,128)(2,1)S(1)} %shard_map.86), channel_id=1, source_target_pairs={{0,112},{16,0},{32,16},{48,32},{64,48},{80,64},{96,80},{112,96},{1... | collective-permute-start | bytes 983048 | tf_op jit(solution)/shard_map/ppermute | solution.py:220
  69.3 16.7 %collective-permute-start.9 = (bf16[32,5120]{1,0:T(8,128)(2,1)S(1)}, bf16[32,5120]{1,0:T(8,128)(2,1)S(1)}, u32[]{:S(2)}, u32[]{:S(2)}) collective-permute-start(bf16[32,5120]{1,0:T(8,128)(2,1)S(1)} %shard_map.86), channel_id=1, source_target_pairs={{0,16},{16,32},{32,48},{48,64},{64,80},{80,96},{96,112},{112,0},{1... | collective-permute-start | bytes 983048 | tf_op jit(solution)/shard_map/ppermute | solution.py:219
  71.2 14.8 %collective-permute-start.7 = (bf16[16,6656]{1,0:T(8,128)(2,1)S(1)}, bf16[16,6656]{1,0:T(8,128)(2,1)S(1)}, u32[]{:S(2)}, u32[]{:S(2)}) collective-permute-start(bf16[16,6656]{1,0:T(8,128)(2,1)S(1)} %collective-permute-done.5), channel_id=1, source_target_pairs={{0,16},{16,32},{32,48},{48,64},{64,80},{80,96},{96,112},{112,0},{1... | collective-permute-start | bytes 638984 | tf_op jit(solution)/shard_map/ppermute | solution.py:217
  87.0 9.6 %collective-permute-start.11 = (bf16[3,16,6656]{2,1,0:T(8,128)(2,1)S(1)}, bf16[3,16,6656]{2,1,0:T(8,128)(2,1)S(1)}, u32[]{:S(2)}, u32[]{:S(2)}) collective-permute-start(bf16[3,16,6656]{2,1,0:T(8,128)(2,1)S(1)} %pad_maximum_fusion.1.late_ref), channel_id=1, source_target_pairs={{0,8},{8,0},{1,9},{9,1},{2,10},{10,2},{3,11},{11,3},{4,12},{12,4},... | collective-permute-start | bytes 1916936 | tf_op jit(solution)/shard_map/ppermute | solution.py:225
  90.0 13.2 %collective-permute-start.13 = (bf16[32,5120]{1,0:T(8,128)(2,1)S(1)}, bf16[32,5120]{1,0:T(8,128)(2,1)}, u32[]{:S(2)}, u32[]{:S(2)}) collective-permute-start(bf16[32,5120]{1,0:T(8,128)(2,1)S(1)} %collective-permute-done.9), channel_id=1, source_target_pairs={{0,16},{16,32},{32,48},{48,64},{64,80},{80,96},{96,112},{112,0},{1... | collective-permute-start | bytes 983048 | tf_op jit(solution)/shard_map/ppermute | solution.py:221
  92.0 14.2 %collective-permute-start.14 = (bf16[32,5120]{1,0:T(8,128)(2,1)S(1)}, bf16[32,5120]{1,0:T(8,128)(2,1)S(1)}, u32[]{:S(2)}, u32[]{:S(2)}) collective-permute-start(bf16[32,5120]{1,0:T(8,128)(2,1)S(1)} %collective-permute-done.10), channel_id=1, source_target_pairs={{0,112},{16,0},{32,16},{48,32},{64,48},{80,64},{96,80},{112,96},{1... | collective-permute-start | bytes 983048 | tf_op jit(solution)/shard_map/ppermute | solution.py:222
  96.6 5.7 %copy-start.3 = (bf16[3,16,6656]{2,1,0:T(8,128)(2,1)}, bf16[3,16,6656]{2,1,0:T(8,128)(2,1)S(1)}, u32[]{:S(2)}) copy-start(bf16[3,16,6656]{2,1,0:T(8,128)(2,1)S(1)} %collective-permute-done.11.late_far_ref) | copy-start | bytes 1916932
  103.2 12.9 %collective-permute-start.16 = (bf16[32,5120]{1,0:T(8,128)(2,1)}, bf16[32,5120]{1,0:T(8,128)(2,1)S(1)}, u32[]{:S(2)}, u32[]{:S(2)}) collective-permute-start(bf16[32,5120]{1,0:T(8,128)(2,1)} %collective-permute-done.13), channel_id=1, source_target_pairs={{0,16},{16,32},{32,48},{48,64},{64,80},{80,96},{96,112},{112,0},{1... | collective-permute-start | bytes 983048 | tf_op jit(solution)/shard_map/ppermute | solution.py:238
  106.9 25.5 %all-to-all-start.2 = ((bf16[4,64,2048]{2,1,0:T(8,128)(2,1)}), bf16[4,64,2048]{2,1,0:T(8,128)(2,1)}, u32[]{:S(2)}, u32[]{:S(2)}) async-start(bf16[4,64,2048]{2,1,0:T(8,128)(2,1)} %bitcast.26), calls=%async_computation.2 | async-start | bytes 2097152 | tf_op jit(solution)/shard_map/all_to_all | solution.py:242
  111.5 10.4 %collective-permute-start.17 = (bf16[32,5120]{1,0:T(8,128)(2,1)S(1)}, bf16[32,5120]{1,0:T(8,128)(2,1)S(1)}, u32[]{:S(2)}, u32[]{:S(2)}) collective-permute-start(bf16[32,5120]{1,0:T(8,128)(2,1)S(1)} %copy-done.9), channel_id=1, source_target_pairs={{0,112},{16,0},{32,16},{48,32},{64,48},{80,64},{96,80},{112,96},{1... | collective-permute-start | bytes 983048 | tf_op jit(solution)/shard_map/ppermute | solution.py:239
  116.1 11.0 %copy-start.10 = (bf16[32,5120]{1,0:T(8,128)(2,1)}, bf16[32,5120]{1,0:T(8,128)(2,1)S(1)}, u32[]{:S(2)}) copy-start(bf16[32,5120]{1,0:T(8,128)(2,1)S(1)} %collective-permute-done.16) | copy-start | bytes 983044
  116.1 11.0 %collective-permute-start.18 = (bf16[32,5120]{1,0:T(8,128)(2,1)S(1)}, bf16[32,5120]{1,0:T(8,128)(2,1)S(1)}, u32[]{:S(2)}, u32[]{:S(2)}) collective-permute-start(bf16[32,5120]{1,0:T(8,128)(2,1)S(1)} %collective-permute-done.16), channel_id=1, source_target_pairs={{0,16},{16,32},{32,48},{48,64},{64,80},{80,96},{96,112},{112,0},{1... | collective-permute-start | bytes 983048 | tf_op jit(solution)/shard_map/ppermute | solution.py:245
  118.1 35.5 %collective-permute-start.15 = (bf16[5,32,5120]{2,1,0:T(8,128)(2,1)S(1)}, bf16[5,32,5120]{2,1,0:T(8,128)(2,1)}, u32[]{:S(2)}, u32[]{:S(2)}) collective-permute-start(bf16[5,32,5120]{2,1,0:T(8,128)(2,1)S(1)} %bitcast_dynamic-update-slice_fusion.early_ref), channel_id=1, source_target_pairs={{0,8},{8,0},{1,9},{9,1},{2,10},{10,2},{3,11},{11,3},{4,12},{12,4},... | collective-permute-start | bytes 4915208 | tf_op jit(solution)/shard_map/ppermute | solution.py:241
  128.2 25.3 %collective-permute-start.19 = (bf16[3,32,5120]{2,1,0:T(8,128)(2,1)S(1)}, bf16[3,32,5120]{2,1,0:T(8,128)(2,1)}, u32[]{:S(2)}, u32[]{:S(2)}) collective-permute-start(bf16[3,32,5120]{2,1,0:T(8,128)(2,1)S(1)} %pad_maximum_fusion.late_ref), channel_id=1, source_target_pairs={{0,8},{8,0},{1,9},{9,1},{2,10},{10,2},{3,11},{11,3},{4,12},{12,4},... | collective-permute-start | bytes 2949128 | tf_op jit(solution)/shard_map/ppermute | solution.py:247
  133.9 19.6 %collective-permute-start.12 = (bf16[64,2048]{1,0:T(8,128)(2,1)S(1)}, bf16[64,2048]{1,0:T(8,128)(2,1)S(1)}, u32[]{:S(2)}, u32[]{:S(2)}) collective-permute-start(bf16[64,2048]{1,0:T(8,128)(2,1)S(1)} %convert_element_type.13), channel_id=1, source_target_pairs={{0,1},{1,0},{2,3},{3,2},{4,5},{5,4},{6,7},{7,6},{8,9},{9,8},{10,11... | collective-permute-start | bytes 786440 | tf_op jit(solution)/shard_map/ppermute | solution.py:244
  153.6 23.2 %copy-start.7 = (f32[256,1024]{1,0:T(8,128)S(1)}, f32[256,1024]{1,0:T(8,128)}, u32[]{:S(2)}) copy-start(f32[256,1024]{1,0:T(8,128)} %copy-done.6) | copy-start | bytes 3145732
  158.4 18.4 %copy-start.1 = (s32[1024,1]{1,0:T(8,128)S(1)}, s32[1024,1]{1,0:T(8,128)}, u32[]{:S(2)}) copy-start(s32[1024,1]{1,0:T(8,128)} %copy-done) | copy-start | bytes 12292
  158.4 18.4 %copy-start.4 = (bf16[3,16,6656]{2,1,0:T(8,128)(2,1)S(1)}, bf16[3,16,6656]{2,1,0:T(8,128)(2,1)}, u32[]{:S(2)}) copy-start(bf16[3,16,6656]{2,1,0:T(8,128)(2,1)} %copy-done.3) | copy-start | bytes 1916932
  (3 other events, 6.3 us)

commit v6 on v5

--- a/solution.py
+++ b/solution.py
@@ -92,34 +92,35 @@
     copy.wait()
 
 
-def root_kernel(
-    place_ref, s_ref, early_ref, early_far_ref, late_ref, late_far_ref, out_ref, r_ref, f_ref
-):
-    here, core = place_ref[0], place_ref[1]
-    s0 = s_ref.shape[1]
-    q0 = s0 // ZL
-    rc = early_ref.shape[1]
-
-    def put(blocks_ref, steps, c):
-        for j, step in enumerate(steps):
-            y = lax.rem(here + (step + Y), Y)
-            at = pl.multiple_of(y * (CORE * rc), CORE * rc) + c * rc
-            r_ref[pl.ds(at, rc), :] = blocks_ref[j]
-
-    by_core(core, (early_ref, early_far_ref), (late_ref, late_far_ref), put)
-    left = 0
+def root_kernel(place_ref, s_ref, mine_ref, other_ref, out_ref, r_ref, f_ref):
+    core = place_ref[1]
+    q0 = s_ref.shape[1] // ZL
+    rc = mine_ref.shape[1]
+    step = f_ref.shape[1] // ZL
+
+    def put(blocks_ref, c):
+        for y in range(Y):
+            r_ref[(y * CORE + c) * rc : (y * CORE + c + 1) * rc, :] = blocks_ref[y]
+
+    for mine in range(CORE):
+
+        @pl.when(core == mine)
+        def _():
+            put(mine_ref, mine)
+            put(other_ref, 1 - mine)
+
     spans = []
     for q in range(ZL):
-        spans.append((left, left + s0 - q * q0))
-        left = spans[-1][1]
+        left = spans[-1][1] if q else 0
+        spans.append((left, left + (X - q) * step))
     for q in range(ZL):
         term = dot(s_ref[:, q * q0 : (q + 1) * q0], r_ref[:, spans[q][0] : spans[q][1]])
-        f_ref[:, q * q0 :] = term if q == 0 else f_ref[:, q * q0 :] + term
+        f_ref[:, q * step :] = term if q == 0 else f_ref[:, q * step :] + term
     f = f_ref[...].astype(BF)
     for q in range(ZL):
-        part = dot(f[:, q * q0 :], r_ref[:, spans[q][0] : spans[q][1]], 1, 1).astype(BF)
-        for i in range(out_ref.shape[0]):
-            out_ref[i, :, q * q0 : (q + 1) * q0] = part
+        out_ref[:, q * q0 : (q + 1) * q0] = dot(
+            f[:, q * step :], r_ref[:, spans[q][0] : spans[q][1]], 1, 1
+        )
 
 
 def backward_kernel(
@@ -150,13 +151,12 @@
 
 
 def pack_kernel(place_ref, r_ref, out_ref):
-    block = r_ref.shape[4]
+    block = r_ref.shape[3]
     left = 0
     for q in range(ZL):
         for x in range(q, X):
-            for z in range(ZH):
-                out_ref[:, left : left + block] = r_ref[x, z, q]
-                left += block
+            out_ref[:, left : left + block] = r_ref[x, q]
+            left += block
 
 
 def call(kernel, outs, args, scratch=(), flops=0, far=((), ())):
@@ -202,27 +202,19 @@
 
     up = {1: lax.ppermute(own, "y", FORTH)}
     down = {1: lax.ppermute(own, "y", BACK)}
-    rz = lax.ppermute(rt, "zh", SWAP)
-    low = lax.axis_index("zh") == 0
-    rt = jnp.stack([jnp.where(low, rt, rz), jnp.where(low, rz, rt)])
+    rt = gather_blocks(rt, "x", X)
+    rwidth = block * sum(X - q for q in range(ZL))
+    rt, = call(pack_kernel, [shape((rt.shape[2], rwidth), BF)], [place, rt])
     up[2] = lax.ppermute(up[1], "y", FORTH)
     down[2] = lax.ppermute(down[1], "y", BACK)
-    rt = gather_blocks(rt, "x", X)
-    rwidth = block * ZH * sum(X - q for q in range(ZL))
-    rt, = call(pack_kernel, [shape((rt.shape[3], rwidth), BF)], [place, rt])
     early = jnp.stack([own, up[1], down[1], up[2], down[2]])
     early_far = lax.ppermute(early, "core", SWAP)
     up[3] = lax.ppermute(up[2], "y", FORTH)
     down[3] = lax.ppermute(down[2], "y", BACK)
     up[4] = lax.ppermute(up[3], "y", FORTH)
-    rt = after(rt, up[3], down[3])
-    rup = {1: lax.ppermute(rt, "y", FORTH)}
-    rdown = {1: lax.ppermute(rt, "y", BACK)}
-    rup[2] = lax.ppermute(rup[1], "y", FORTH)
-    rdown[2] = lax.ppermute(rdown[1], "y", BACK)
-    last, ru, rd = lax.optimization_barrier((up[4], rup[1], rdown[1]))
-    late = jnp.stack([up[3], down[3], last])
+    late = jnp.stack([up[3], down[3], up[4]])
     late_far = lax.ppermute(late, "core", SWAP)
+    rmine = gather_blocks(after(rt, up[3], down[3]), "y", Y)
 
     weights = [early, early_far, late, late_far]
     scratch = [pltpu.VMEM((s1, s1), BF), pltpu.VMEM((k, s1), BF)]
@@ -235,26 +227,26 @@
         flops,
         ((), (1,)),
     )
-    rup[3] = lax.ppermute(after(rup[2], placed), "y", FORTH)
-    rdown[3] = lax.ppermute(after(rdown[2], placed), "y", BACK)
-    rearly = jnp.stack([rt, ru, rd, rup[2], rdown[2]])
-    rearly_far = lax.ppermute(rearly, "core", SWAP)
-    parts = lax.all_to_all(placed.reshape(X, n // X, s0), "x", 0, 0, tiled=True)
-    part = jnp.sum(parts.astype(F32), axis=0)
-    far = lax.ppermute(part.astype(BF), "zh", SWAP)
-    rup[4] = lax.ppermute(rup[3], "y", FORTH)
-    rlate = jnp.stack([rup[3], rdown[3], rup[4]])
-    rlate_far = lax.ppermute(rlate, "core", SWAP)
-    s_t = (part + far.astype(F32)).astype(BF)
-
-    x_t, = call(
+    here = lax.axis_index("x")
+    blocks = placed.reshape(X, n // X, s0)
+    block_for = lambda i: lax.dynamic_index_in_dim(blocks, lax.rem(here + i, X), 0, False)
+    parts = [
+        lax.ppermute(block_for(i), "x", [(j, (j + i) % X) for j in range(X)]) for i in (1, 3, 2)
+    ]
+    part = sum((p.astype(F32) for p in parts), block_for(0).astype(F32))
+    rmine = after(rmine, part)
+    rother = lax.ppermute(rmine, "core", SWAP)
+    s_t = (part + lax.ppermute(part.astype(BF), "zh", SWAP).astype(F32)).astype(BF)
+
+    x_part, = call(
         root_kernel,
-        [shape((X, n // X, s0), BF)],
-        [place, s_t, rearly, rearly_far, rlate, rlate_far],
-        [pltpu.VMEM((q0, rwidth), BF), pltpu.VMEM((n // X, s0), F32)],
-        flops=4 * (n // X) * q0 * rwidth,
-    )
-    x_all = lax.all_to_all(x_t, "x", 0, 0, tiled=True).reshape(n, s0)
+        [shape((n // X, s0), F32)],
+        [place, s_t, rmine, rother],
+        [pltpu.VMEM((q0, rwidth), BF), pltpu.VMEM((n // X, s0 // ZH), F32)],
+        4 * (n // X) * q0 * rwidth,
+    )
+    x_t = x_part + lax.ppermute(x_part.astype(BF), "zh", SWAP).astype(F32)
+    x_all = gather_blocks(x_t.astype(BF), "x", X).reshape(n, s0)
 
     child_out, root_out = call(
         backward_kernel,

time: 184 us -> 171 us (0.929)
  starting transfers between devices: 96.1 us -> 76.5 us
  waiting for transfers between devices: 36.1 us -> 44.7 us
  Pallas kernels: 16.4 us -> 12.6 us
  local copies, waits for them, and re-layouts: 8.87 us -> 12.5 us
    ppermute x11 -> x6, starting transfers between devices: 44.7 us -> 23.2 us  [the longest x3 8.81 us: on_device(): lax.ppermute(block_for(i), 'x', [(j, (j + i) % X) for j in range(X)])]
    ppermute x11 -> x6, waiting for transfers between devices: 18.8 us -> 34.5 us  [the longest x1 14.2 us: on_device(): x_t = x_part + lax.ppermute(x_part.astype(BF), 'zh', SWAP).astype(F32)]
    ppermute x1, waiting for transfers between devices: 12.8 us -> 0.01 us  [on_device(): up[4] = lax.ppermute(up[3], 'y', FORTH)]
    all_to_all x2 -> x3, starting transfers between devices: 11.8 us -> 18.3 us  [gather_blocks(): lax.all_to_all(jnp.broadcast_to(x[None], (length, *x.shape)), axis, 0, 0,...]
    all_to_all x1 -> x0, starting transfers between devices: 4.64 us -> none  [on_device(): parts = lax.all_to_all(placed.reshape(X, n // X, s0), 'x', 0, 0, tiled=True)]
    pallas_call x4, Pallas kernels: 16.4 us -> 12.6 us  [call(): pl.pallas_call(kernel, out_shape=outs, in_specs=[pl.BlockSpec(memory_spac...]
    ppermute x1, starting transfers between devices: 7.54 us -> 3.8 us  [on_device(): down = {1: lax.ppermute(own, 'y', BACK)}]
    ppermute x1, starting transfers between devices: 1.92 us -> 5.65 us  [on_device(): up = {1: lax.ppermute(own, 'y', FORTH)}]
  transfers between devices with their start and end apart: 23 -> 18, of which waited for: 6 -> 11; matrix products, arithmetic and copies ran while one was open for 6% -> 6% of each run, Pallas kernels for 3% -> 3%
where the time goes in v6:
time: 171 us; the launch traced here: 170 us
  starting transfers between devices  76.5 us (45%)
  waiting for transfers between devices  44.7 us (26%)
  blocking collectives  17.2 us (10%)
  Pallas kernels  12.6 us (7%)
  local copies, waits for them, and re-layouts  12.5 us (7%)
  other arithmetic  4.25 us (2%)
    all_to_all x3, starting transfers between devices, gather_blocks(): lax.all_to_all(jnp.broadcast_to(x[None], (length, *x.shape)), axis, 0, 0,...  18.3 us
    all_to_all x1, blocking collectives, gather_blocks(): lax.all_to_all(jnp.broadcast_to(x[None], (length, *x.shape)), axis, 0, 0,...  17.2 us
    ppermute x1, waiting for transfers between devices, on_device(): x_t = x_part + lax.ppermute(x_part.astype(BF), 'zh', SWAP).astype(F32)  14.2 us
    pallas_call x4, Pallas kernels, call(): pl.pallas_call(kernel, out_shape=outs, in_specs=[pl.BlockSpec(memory_spac...  12.6 us
    ppermute x1, waiting for transfers between devices, on_device(): lax.ppermute(part.astype(BF), 'zh', SWAP).astype(F32)  12.5 us
    ppermute x3, starting transfers between devices, on_device(): lax.ppermute(block_for(i), 'x', [(j, (j + i) % X) for j in range(X)])  8.81 us
    ppermute x1, starting transfers between devices, on_device(): early_far = lax.ppermute(early, 'core', SWAP)  8.63 us
    all_to_all x3, waiting for transfers between devices, gather_blocks(): lax.all_to_all(jnp.broadcast_to(x[None], (length, *x.shape)), axis, 0, 0,...  7.95 us
  transfers between devices with their start and end apart: 18, of which 11 were waited for; matrix products, arithmetic and copies ran while one was open for 6% of the time, Pallas kernels for 3%

profile of v6, /device:TPU:1, one launch (start us, length us, event | category | flops | bytes accessed | tf_op | source)
XLA Modules:
  0.0 169.5 jit_solution(9618034993396128871)
XLA Ops:
  2.2 7.8 %all-to-all-start = ((bf16[4,32,1280]{2,1,0:T(8,128)(2,1)}), bf16[4,32,1280]{2,1,0:T(8,128)(2,1)S(1)}, u32[]{:S(2)}, u32[]{:S(2)}) async-start(bf16[4,32,1280]{2,1,0:T(8,128)(2,1)} %broadcast_in_dim.10), calls=%async_computation | async-start | bytes 655360 | tf_op jit(solution)/shard_map/all_to_all | solution.py:20
  10.7 5.5 %all-to-all-done = bf16[4,32,1280]{2,1,0:T(8,128)(2,1)S(1)} async-done(((bf16[4,32,1280]{2,1,0:T(8,128)(2,1)}), bf16[4,32,1280]{2,1,0:T(8,128)(2,1)S(1)}, u32[]{:S(2)}, u32[]{:S(2)}) %all-to-all-start) | async-done | bytes 327712 | tf_op jit(solution)/shard_map/all_to_all | solution.py:20
  16.3 5.6 %collective-permute-start = (bf16[16,6656]{1,0:T(8,128)(2,1)S(1)}, bf16[16,6656]{1,0:T(8,128)(2,1)S(1)}, u32[]{:S(2)}, u32[]{:S(2)}) collective-permute-start(bf16[16,6656]{1,0:T(8,128)(2,1)S(1)} %constant_dynamic-update-slice_fusion), channel_id=1, source_target_pairs={{0,16},{16,32},{32,48},{48,64},{64,80},{80,96},{96,112},{112,0},{1... | collective-permute-start | bytes 638984 | tf_op jit(solution)/shard_map/ppermute | solution.py:203
  22.7 4.0 %all-to-all-start.1 = ((bf16[4,4,32,256]{3,2,1,0:T(8,128)(2,1)}), bf16[4,4,32,256]{3,2,1,0:T(8,128)(2,1)S(1)}, u32[]{:S(2)}, u32[]{:S(2)}) async-start(bf16[4,4,32,256]{3,2,1,0:T(8,128)(2,1)} %broadcast_in_dim.11), calls=%async_computation.1 | async-start | bytes 524288 | tf_op jit(solution)/shard_map/all_to_all | solution.py:20
  27.4 3.8 %collective-permute-start.1 = (bf16[16,6656]{1,0:T(8,128)(2,1)S(1)}, bf16[16,6656]{1,0:T(8,128)(2,1)S(1)}, u32[]{:S(2)}, u32[]{:S(2)}) collective-permute-start(bf16[16,6656]{1,0:T(8,128)(2,1)S(1)} %constant_dynamic-update-slice_fusion), channel_id=1, source_target_pairs={{0,112},{16,0},{32,16},{48,32},{64,48},{80,64},{96,80},{112,96},{1... | collective-permute-start | bytes 638984 | tf_op jit(solution)/shard_map/ppermute | solution.py:204
  32.8 3.2 %collective-permute-start.2 = (bf16[16,6656]{1,0:T(8,128)(2,1)S(1)}, bf16[16,6656]{1,0:T(8,128)(2,1)S(1)}, u32[]{:S(2)}, u32[]{:S(2)}) collective-permute-start(bf16[16,6656]{1,0:T(8,128)(2,1)S(1)} %collective-permute-done), channel_id=1, source_target_pairs={{0,16},{16,32},{32,48},{48,64},{64,80},{80,96},{96,112},{112,0},{1... | collective-permute-start | bytes 638984 | tf_op jit(solution)/shard_map/ppermute | solution.py:208
  36.7 3.3 %collective-permute-start.3 = (bf16[16,6656]{1,0:T(8,128)(2,1)S(1)}, bf16[16,6656]{1,0:T(8,128)(2,1)S(1)}, u32[]{:S(2)}, u32[]{:S(2)}) collective-permute-start(bf16[16,6656]{1,0:T(8,128)(2,1)S(1)} %collective-permute-done.1), channel_id=1, source_target_pairs={{0,112},{16,0},{32,16},{48,32},{64,48},{80,64},{96,80},{112,96},{1... | collective-permute-start | bytes 638984 | tf_op jit(solution)/shard_map/ppermute | solution.py:209
  40.7 2.0 %collective-permute-start.5 = (bf16[16,6656]{1,0:T(8,128)(2,1)S(1)}, bf16[16,6656]{1,0:T(8,128)(2,1)S(1)}, u32[]{:S(2)}, u32[]{:S(2)}) collective-permute-start(bf16[16,6656]{1,0:T(8,128)(2,1)S(1)} %collective-permute-done.2), channel_id=1, source_target_pairs={{0,16},{16,32},{32,48},{48,64},{64,80},{80,96},{96,112},{112,0},{1... | collective-permute-start | bytes 638984 | tf_op jit(solution)/shard_map/ppermute | solution.py:212
  43.6 4.3 %collective-permute-start.6 = (bf16[16,6656]{1,0:T(8,128)(2,1)S(1)}, bf16[16,6656]{1,0:T(8,128)(2,1)S(1)}, u32[]{:S(2)}, u32[]{:S(2)}) collective-permute-start(bf16[16,6656]{1,0:T(8,128)(2,1)S(1)} %collective-permute-done.3), channel_id=1, source_target_pairs={{0,112},{16,0},{32,16},{48,32},{64,48},{80,64},{96,80},{112,96},{1... | collective-permute-start | bytes 638984 | tf_op jit(solution)/shard_map/ppermute | solution.py:213
  48.5 1.9 %collective-permute-start.7 = (bf16[16,6656]{1,0:T(8,128)(2,1)S(1)}, bf16[16,6656]{1,0:T(8,128)(2,1)S(1)}, u32[]{:S(2)}, u32[]{:S(2)}) collective-permute-start(bf16[16,6656]{1,0:T(8,128)(2,1)S(1)} %collective-permute-done.5), channel_id=1, source_target_pairs={{0,16},{16,32},{32,48},{48,64},{64,80},{80,96},{96,112},{112,0},{1... | collective-permute-start | bytes 638984 | tf_op jit(solution)/shard_map/ppermute | solution.py:214
  51.1 8.6 %collective-permute-start.4 = (bf16[5,16,6656]{2,1,0:T(8,128)(2,1)}, bf16[5,16,6656]{2,1,0:T(8,128)(2,1)}, u32[]{:S(2)}, u32[]{:S(2)}) collective-permute-start(bf16[5,16,6656]{2,1,0:T(8,128)(2,1)} %bitcast_dynamic-update-slice_fusion.early_ref), channel_id=1, source_target_pairs={{0,8},{8,0},{1,9},{9,1},{2,10},{10,2},{3,11},{11,3},{4,12},{12,4},... | collective-permute-start | bytes 3194888 | tf_op jit(solution)/shard_map/ppermute | solution.py:211
  59.8 1.2 broadcast_in_dim.12
  61.0 6.5 %all-to-all-start.2 = ((bf16[8,32,2560]{2,1,0:T(8,128)(2,1)}), bf16[8,32,2560]{2,1,0:T(8,128)(2,1)S(1)}, u32[]{:S(2)}, u32[]{:S(2)}) async-start(bf16[8,32,2560]{2,1,0:T(8,128)(2,1)} %broadcast_in_dim.12), calls=%async_computation.2 | async-start | bytes 2621440 | tf_op jit(solution)/shard_map/all_to_all | solution.py:20
  67.5 2.2 %collective-permute-start.8 = (bf16[3,16,6656]{2,1,0:T(8,128)(2,1)S(1)}, bf16[3,16,6656]{2,1,0:T(8,128)(2,1)S(1)}, u32[]{:S(2)}, u32[]{:S(2)}) collective-permute-start(bf16[3,16,6656]{2,1,0:T(8,128)(2,1)S(1)} %pad_maximum_fusion.late_ref), channel_id=1, source_target_pairs={{0,8},{8,0},{1,9},{9,1},{2,10},{10,2},{3,11},{11,3},{4,12},{12,4},... | collective-permute-start | bytes 1916936 | tf_op jit(solution)/shard_map/ppermute | solution.py:216
  70.0 1.5 collective-permute-done.8.late_far_ref
  72.3 1.2 copy-done
  75.6 4.5 %shard_map.86 = (bf16[256,2048]{1,0:T(8,128)(2,1)S(1)}, f32[256,1024]{1,0:T(8,128)S(1)}) custom-call(s32[4]{0:T(128)S(1)} %pad_add_fusion.place_ref, bf16[5,16,6656]{2,1,0:T(8,128)(2,1)} %bitcast_dynamic-update-slice_fusion.early_ref, bf16[5,16,6656]{2,1,0:T(8,128)(2,1)} %collective-permute-done.4.early_far_ref, ...), custom_call_target="tpu_custom_call" | custom-call | flops 2147483648 | bytes 6819856 | tf_op jit(solution)/shard_map/pallas_call | solution.py:166
  82.0 3.5 %collective-permute-start.11 = (bf16[64,2048]{1,0:T(8,128)(2,1)}, bf16[64,2048]{1,0:T(8,128)(2,1)}, u32[]{:S(2)}, u32[]{:S(2)}) collective-permute-start(bf16[64,2048]{1,0:T(8,128)(2,1)} %get-tuple-element.19), channel_id=1, source_target_pairs={{0,4},{2,6},{4,0},{6,2},{1,5},{3,7},{5,1},{7,3},{8,12},{10,14},{12... | collective-permute-start | bytes 786440 | tf_op jit(solution)/shard_map/ppermute | solution.py:234
  85.5 2.8 %collective-permute-start.10 = (bf16[64,2048]{1,0:T(8,128)(2,1)}, bf16[64,2048]{1,0:T(8,128)(2,1)}, u32[]{:S(2)}, u32[]{:S(2)}) collective-permute-start(bf16[64,2048]{1,0:T(8,128)(2,1)} %get-tuple-element.20), channel_id=1, source_target_pairs={{0,6},{2,0},{4,2},{6,4},{1,7},{3,1},{5,3},{7,5},{8,14},{10,8},{12,... | collective-permute-start | bytes 786440 | tf_op jit(solution)/shard_map/ppermute | solution.py:234
  88.3 2.5 %collective-permute-start.9 = (bf16[64,2048]{1,0:T(8,128)(2,1)}, bf16[64,2048]{1,0:T(8,128)(2,1)}, u32[]{:S(2)}, u32[]{:S(2)}) collective-permute-start(bf16[64,2048]{1,0:T(8,128)(2,1)} %get-tuple-element.18), channel_id=1, source_target_pairs={{0,2},{2,4},{4,6},{6,0},{1,3},{3,5},{5,7},{7,1},{8,10},{10,12},{12... | collective-permute-start | bytes 786440 | tf_op jit(solution)/shard_map/ppermute | solution.py:234
  90.8 2.5 %collective-permute-done.11 = bf16[64,2048]{1,0:T(8,128)(2,1)} collective-permute-done((bf16[64,2048]{1,0:T(8,128)(2,1)}, bf16[64,2048]{1,0:T(8,128)(2,1)}, u32[]{:S(2)}, u32[]{:S(2)}) %collective-permute-start.11) | collective-permute-done | bytes 262176 | tf_op jit(solution)/shard_map/ppermute | solution.py:234
  93.3 4.6 %collective-permute-done.10 = bf16[64,2048]{1,0:T(8,128)(2,1)} collective-permute-done((bf16[64,2048]{1,0:T(8,128)(2,1)}, bf16[64,2048]{1,0:T(8,128)(2,1)}, u32[]{:S(2)}, u32[]{:S(2)}) %collective-permute-start.10) | collective-permute-done | bytes 262176 | tf_op jit(solution)/shard_map/ppermute | solution.py:234
  98.7 2.1 %fusion.7 = (bf16[64,2048]{1,0:T(8,128)(2,1)}, f32[64,2048]{1,0:T(8,128)}) fusion(bf16[64,2048]{1,0:T(8,128)(2,1)} %collective-permute-done.11, bf16[64,2048]{1,0:T(8,128)(2,1)} %collective-permute-done.10, bf16[64,2048]{1,0:T(8,128)(2,1)} %collective-permute-done.9, bf16[4,64,2048]{2,1,0:T(8,128)(2,1)S(1)} %bitcast.67, s32[]{:T(128)S(6)} %select_n.13), kind=kLoop, calls=%fused_computation.32 | loop fusion | flops 1048576 | bytes 1835012 | tf_op jit(solution)/shard_map/convert_element_type | solution.py:239
  100.8 1.4 all-to-all-done.2.mine_ref
  102.3 2.4 %collective-permute-start.13 = (bf16[8,32,2560]{2,1,0:T(8,128)(2,1)S(1)}, bf16[8,32,2560]{2,1,0:T(8,128)(2,1)S(1)}, u32[]{:S(2)}, u32[]{:S(2)}) collective-permute-start(bf16[8,32,2560]{2,1,0:T(8,128)(2,1)S(1)} %all-to-all-done.2.mine_ref), channel_id=1, source_target_pairs={{0,8},{8,0},{1,9},{9,1},{2,10},{10,2},{3,11},{11,3},{4,12},{12,4},... | collective-permute-start | bytes 3932168 | tf_op jit(solution)/shard_map/ppermute | solution.py:238
  104.6 7.9 %collective-permute-start.12 = (bf16[64,2048]{1,0:T(8,128)(2,1)}, bf16[64,2048]{1,0:T(8,128)(2,1)S(1)}, u32[]{:S(2)}, u32[]{:S(2)}) collective-permute-start(bf16[64,2048]{1,0:T(8,128)(2,1)} %get-tuple-element.16), channel_id=1, source_target_pairs={{0,1},{1,0},{2,3},{3,2},{4,5},{5,4},{6,7},{7,6},{8,9},{9,8},{10,11... | collective-permute-start | bytes 786440 | tf_op jit(solution)/shard_map/ppermute | solution.py:239
  112.6 12.5 %collective-permute-done.12 = bf16[64,2048]{1,0:T(8,128)(2,1)S(1)} collective-permute-done((bf16[64,2048]{1,0:T(8,128)(2,1)}, bf16[64,2048]{1,0:T(8,128)(2,1)S(1)}, u32[]{:S(2)}, u32[]{:S(2)}) %collective-permute-start.12) | collective-permute-done | bytes 262176 | tf_op jit(solution)/shard_map/ppermute | solution.py:239
  126.1 2.1 %shard_map.88 = f32[64,2048]{1,0:T(8,128)S(1)} custom-call(s32[4]{0:T(128)S(1)} %pad_add_fusion.place_ref, bf16[64,2048]{1,0:T(8,128)(2,1)S(1)} %add_convert_fusion.1.s_ref, bf16[8,32,2560]{2,1,0:T(8,128)(2,1)S(1)} %all-to-all-done.2.mine_ref, bf16[8,32,2560]{2,1,0:T(8,128)(2,1)S(1)} %collective-permute-done.13.other_ref), custom_call_target="tpu_custom_call" | custom-call | flops 335544320 | bytes 3407888 | tf_op jit(solution)/shard_map/pallas_call | solution.py:166
  128.3 4.1 %collective-permute-start.14 = (bf16[64,2048]{1,0:T(8,128)(2,1)S(1)}, bf16[64,2048]{1,0:T(8,128)(2,1)S(1)}, u32[]{:S(2)}, u32[]{:S(2)}) collective-permute-start(bf16[64,2048]{1,0:T(8,128)(2,1)S(1)} %convert_element_type.41), channel_id=1, source_target_pairs={{0,1},{1,0},{2,3},{3,2},{4,5},{5,4},{6,7},{7,6},{8,9},{9,8},{10,11... | collective-permute-start | bytes 786440 | tf_op jit(solution)/shard_map/ppermute | solution.py:248
  132.4 14.2 %collective-permute-done.14 = bf16[64,2048]{1,0:T(8,128)(2,1)S(1)} collective-permute-done((bf16[64,2048]{1,0:T(8,128)(2,1)S(1)}, bf16[64,2048]{1,0:T(8,128)(2,1)S(1)}, u32[]{:S(2)}, u32[]{:S(2)}) %collective-permute-start.14) | collective-permute-done | bytes 262176 | tf_op jit(solution)/shard_map/ppermute | solution.py:248
  146.7 17.2 %all_to_all.20 = bf16[4,64,2048]{2,1,0:T(8,128)(2,1)S(1)} all-to-all(bf16[4,64,2048]{2,1,0:T(8,128)(2,1)S(1)} %broadcast_in_dim.13), channel_id=1, replica_groups=mesh['zl'=4,'y'=8,'core'=2,'x'=4,'zh'=2] {'x'}, dimensions={0} | all-to-all | bytes 2097152 | tf_op jit(solution)/shard_map/all_to_all | solution.py:20
  164.0 5.5 %shard_map.89 = (f32[1024,256]{1,0:T(8,128)}, f32[256,256]{1,0:T(8,128)}) custom-call(s32[4]{0:T(128)S(1)} %pad_add_fusion.place_ref, bf16[256,2048]{1,0:T(8,128)(2,1)S(1)} %bitcast.68, f32[256,1024]{1,0:T(8,128)S(1)} %copy-done.6, bf16[5,16,6656]{2,1,0:T(8,128)(2,1)} %bitcast_dynamic-update-slice_fusion.early_ref, ...), custom_call_target="tpu_custom_call" | custom-call | flops 2147483648 | bytes 6819856 | tf_op jit(solution)/shard_map/pallas_call | solution.py:166
  (52 shorter events, 15.4 us)
Async XLA Ops:
  2.2 14.0 %all-to-all-start = ((bf16[4,32,1280]{2,1,0:T(8,128)(2,1)}), bf16[4,32,1280]{2,1,0:T(8,128)(2,1)S(1)}, u32[]{:S(2)}, u32[]{:S(2)}) async-start(bf16[4,32,1280]{2,1,0:T(8,128)(2,1)} %broadcast_in_dim.10), calls=%async_computation | async-start | bytes 655360 | tf_op jit(solution)/shard_map/all_to_all | solution.py:20
  16.3 16.5 %collective-permute-start = (bf16[16,6656]{1,0:T(8,128)(2,1)S(1)}, bf16[16,6656]{1,0:T(8,128)(2,1)S(1)}, u32[]{:S(2)}, u32[]{:S(2)}) collective-permute-start(bf16[16,6656]{1,0:T(8,128)(2,1)S(1)} %constant_dynamic-update-slice_fusion), channel_id=1, source_target_pairs={{0,16},{16,32},{32,48},{48,64},{64,80},{80,96},{96,112},{112,0},{1... | collective-permute-start | bytes 638984 | tf_op jit(solution)/shard_map/ppermute | solution.py:203
  22.7 9.5 %all-to-all-start.1 = ((bf16[4,4,32,256]{3,2,1,0:T(8,128)(2,1)}), bf16[4,4,32,256]{3,2,1,0:T(8,128)(2,1)S(1)}, u32[]{:S(2)}, u32[]{:S(2)}) async-start(bf16[4,4,32,256]{3,2,1,0:T(8,128)(2,1)} %broadcast_in_dim.11), calls=%async_computation.1 | async-start | bytes 524288 | tf_op jit(solution)/shard_map/all_to_all | solution.py:20
  27.4 9.3 %collective-permute-start.1 = (bf16[16,6656]{1,0:T(8,128)(2,1)S(1)}, bf16[16,6656]{1,0:T(8,128)(2,1)S(1)}, u32[]{:S(2)}, u32[]{:S(2)}) collective-permute-start(bf16[16,6656]{1,0:T(8,128)(2,1)S(1)} %constant_dynamic-update-slice_fusion), channel_id=1, source_target_pairs={{0,112},{16,0},{32,16},{48,32},{64,48},{80,64},{96,80},{112,96},{1... | collective-permute-start | bytes 638984 | tf_op jit(solution)/shard_map/ppermute | solution.py:204
  32.8 7.9 %collective-permute-start.2 = (bf16[16,6656]{1,0:T(8,128)(2,1)S(1)}, bf16[16,6656]{1,0:T(8,128)(2,1)S(1)}, u32[]{:S(2)}, u32[]{:S(2)}) collective-permute-start(bf16[16,6656]{1,0:T(8,128)(2,1)S(1)} %collective-permute-done), channel_id=1, source_target_pairs={{0,16},{16,32},{32,48},{48,64},{64,80},{80,96},{96,112},{112,0},{1... | collective-permute-start | bytes 638984 | tf_op jit(solution)/shard_map/ppermute | solution.py:208
  36.7 6.9 %collective-permute-start.3 = (bf16[16,6656]{1,0:T(8,128)(2,1)S(1)}, bf16[16,6656]{1,0:T(8,128)(2,1)S(1)}, u32[]{:S(2)}, u32[]{:S(2)}) collective-permute-start(bf16[16,6656]{1,0:T(8,128)(2,1)S(1)} %collective-permute-done.1), channel_id=1, source_target_pairs={{0,112},{16,0},{32,16},{48,32},{64,48},{80,64},{96,80},{112,96},{1... | collective-permute-start | bytes 638984 | tf_op jit(solution)/shard_map/ppermute | solution.py:209
  40.7 7.8 %collective-permute-start.5 = (bf16[16,6656]{1,0:T(8,128)(2,1)S(1)}, bf16[16,6656]{1,0:T(8,128)(2,1)S(1)}, u32[]{:S(2)}, u32[]{:S(2)}) collective-permute-start(bf16[16,6656]{1,0:T(8,128)(2,1)S(1)} %collective-permute-done.2), channel_id=1, source_target_pairs={{0,16},{16,32},{32,48},{48,64},{64,80},{80,96},{96,112},{112,0},{1... | collective-permute-start | bytes 638984 | tf_op jit(solution)/shard_map/ppermute | solution.py:212
  43.6 16.2 %collective-permute-start.6 = (bf16[16,6656]{1,0:T(8,128)(2,1)S(1)}, bf16[16,6656]{1,0:T(8,128)(2,1)S(1)}, u32[]{:S(2)}, u32[]{:S(2)}) collective-permute-start(bf16[16,6656]{1,0:T(8,128)(2,1)S(1)} %collective-permute-done.3), channel_id=1, source_target_pairs={{0,112},{16,0},{32,16},{48,32},{64,48},{80,64},{96,80},{112,96},{1... | collective-permute-start | bytes 638984 | tf_op jit(solution)/shard_map/ppermute | solution.py:213
  48.5 18.9 %collective-permute-start.7 = (bf16[16,6656]{1,0:T(8,128)(2,1)S(1)}, bf16[16,6656]{1,0:T(8,128)(2,1)S(1)}, u32[]{:S(2)}, u32[]{:S(2)}) collective-permute-start(bf16[16,6656]{1,0:T(8,128)(2,1)S(1)} %collective-permute-done.5), channel_id=1, source_target_pairs={{0,16},{16,32},{32,48},{48,64},{64,80},{80,96},{96,112},{112,0},{1... | collective-permute-start | bytes 638984 | tf_op jit(solution)/shard_map/ppermute | solution.py:214
  51.1 18.9 %collective-permute-start.4 = (bf16[5,16,6656]{2,1,0:T(8,128)(2,1)}, bf16[5,16,6656]{2,1,0:T(8,128)(2,1)}, u32[]{:S(2)}, u32[]{:S(2)}) collective-permute-start(bf16[5,16,6656]{2,1,0:T(8,128)(2,1)} %bitcast_dynamic-update-slice_fusion.early_ref), channel_id=1, source_target_pairs={{0,8},{8,0},{1,9},{9,1},{2,10},{10,2},{3,11},{11,3},{4,12},{12,4},... | collective-permute-start | bytes 3194888 | tf_op jit(solution)/shard_map/ppermute | solution.py:211
  61.0 41.3 %all-to-all-start.2 = ((bf16[8,32,2560]{2,1,0:T(8,128)(2,1)}), bf16[8,32,2560]{2,1,0:T(8,128)(2,1)S(1)}, u32[]{:S(2)}, u32[]{:S(2)}) async-start(bf16[8,32,2560]{2,1,0:T(8,128)(2,1)} %broadcast_in_dim.12), calls=%async_computation.2 | async-start | bytes 2621440 | tf_op jit(solution)/shard_map/all_to_all | solution.py:20
  67.4 2.3 %copy-start.7 = (s32[1,1024]{1,0:T(1,128)S(1)}, s32[1,1024]{1,0:T(1,128)}, u32[]{:S(2)}) copy-start(s32[1,1024]{1,0:T(1,128)} %param.13) | copy-start | bytes 12292
  67.5 4.0 %collective-permute-start.8 = (bf16[3,16,6656]{2,1,0:T(8,128)(2,1)S(1)}, bf16[3,16,6656]{2,1,0:T(8,128)(2,1)S(1)}, u32[]{:S(2)}, u32[]{:S(2)}) collective-permute-start(bf16[3,16,6656]{2,1,0:T(8,128)(2,1)S(1)} %pad_maximum_fusion.late_ref), channel_id=1, source_target_pairs={{0,8},{8,0},{1,9},{9,1},{2,10},{10,2},{3,11},{11,3},{4,12},{12,4},... | collective-permute-start | bytes 1916936 | tf_op jit(solution)/shard_map/ppermute | solution.py:216
  71.5 0.8 copy-start.1
  72.3 1.2 copy-start
  73.5 1.1 copy-start.2
  74.6 0.9 copy-start.4
  80.1 1.0 copy-start.5
  82.0 11.3 %collective-permute-start.11 = (bf16[64,2048]{1,0:T(8,128)(2,1)}, bf16[64,2048]{1,0:T(8,128)(2,1)}, u32[]{:S(2)}, u32[]{:S(2)}) collective-permute-start(bf16[64,2048]{1,0:T(8,128)(2,1)} %get-tuple-element.19), channel_id=1, source_target_pairs={{0,4},{2,6},{4,0},{6,2},{1,5},{3,7},{5,1},{7,3},{8,12},{10,14},{12... | collective-permute-start | bytes 786440 | tf_op jit(solution)/shard_map/ppermute | solution.py:234
  85.5 12.4 %collective-permute-start.10 = (bf16[64,2048]{1,0:T(8,128)(2,1)}, bf16[64,2048]{1,0:T(8,128)(2,1)}, u32[]{:S(2)}, u32[]{:S(2)}) collective-permute-start(bf16[64,2048]{1,0:T(8,128)(2,1)} %get-tuple-element.20), channel_id=1, source_target_pairs={{0,6},{2,0},{4,2},{6,4},{1,7},{3,1},{5,3},{7,5},{8,14},{10,8},{12,... | collective-permute-start | bytes 786440 | tf_op jit(solution)/shard_map/ppermute | solution.py:234
  88.3 10.4 %collective-permute-start.9 = (bf16[64,2048]{1,0:T(8,128)(2,1)}, bf16[64,2048]{1,0:T(8,128)(2,1)}, u32[]{:S(2)}, u32[]{:S(2)}) collective-permute-start(bf16[64,2048]{1,0:T(8,128)(2,1)} %get-tuple-element.18), channel_id=1, source_target_pairs={{0,2},{2,4},{4,6},{6,0},{1,3},{3,5},{5,7},{7,1},{8,10},{10,12},{12... | collective-permute-start | bytes 786440 | tf_op jit(solution)/shard_map/ppermute | solution.py:234
  102.3 23.9 %collective-permute-start.13 = (bf16[8,32,2560]{2,1,0:T(8,128)(2,1)S(1)}, bf16[8,32,2560]{2,1,0:T(8,128)(2,1)S(1)}, u32[]{:S(2)}, u32[]{:S(2)}) collective-permute-start(bf16[8,32,2560]{2,1,0:T(8,128)(2,1)S(1)} %all-to-all-done.2.mine_ref), channel_id=1, source_target_pairs={{0,8},{8,0},{1,9},{9,1},{2,10},{10,2},{3,11},{11,3},{4,12},{12,4},... | collective-permute-start | bytes 3932168 | tf_op jit(solution)/shard_map/ppermute | solution.py:238
  104.6 20.4 %collective-permute-start.12 = (bf16[64,2048]{1,0:T(8,128)(2,1)}, bf16[64,2048]{1,0:T(8,128)(2,1)S(1)}, u32[]{:S(2)}, u32[]{:S(2)}) collective-permute-start(bf16[64,2048]{1,0:T(8,128)(2,1)} %get-tuple-element.16), channel_id=1, source_target_pairs={{0,1},{1,0},{2,3},{3,2},{4,5},{5,4},{6,7},{7,6},{8,9},{9,8},{10,11... | collective-permute-start | bytes 786440 | tf_op jit(solution)/shard_map/ppermute | solution.py:239
  128.3 18.3 %collective-permute-start.14 = (bf16[64,2048]{1,0:T(8,128)(2,1)S(1)}, bf16[64,2048]{1,0:T(8,128)(2,1)S(1)}, u32[]{:S(2)}, u32[]{:S(2)}) collective-permute-start(bf16[64,2048]{1,0:T(8,128)(2,1)S(1)} %convert_element_type.41), channel_id=1, source_target_pairs={{0,1},{1,0},{2,3},{3,2},{4,5},{5,4},{6,7},{7,6},{8,9},{9,8},{10,11... | collective-permute-start | bytes 786440 | tf_op jit(solution)/shard_map/ppermute | solution.py:248
  146.7 17.3 %copy-start.3 = (bf16[3,16,6656]{2,1,0:T(8,128)(2,1)S(1)}, bf16[3,16,6656]{2,1,0:T(8,128)(2,1)}, u32[]{:S(2)}) copy-start(bf16[3,16,6656]{2,1,0:T(8,128)(2,1)} %copy-done.1) | copy-start | bytes 1916932
  146.7 17.3 %copy-start.6 = (f32[256,1024]{1,0:T(8,128)S(1)}, f32[256,1024]{1,0:T(8,128)}, u32[]{:S(2)}) copy-start(f32[256,1024]{1,0:T(8,128)} %copy-done.5) | copy-start | bytes 3145732

commit v7 on v6

--- a/solution.py
+++ b/solution.py
@@ -28,10 +28,17 @@
     return lax.dot_general(a, b, (((ca,), (cb,)), ((), ())), preferred_element_type=F32)
 
 
-def onehot(idx_ref, at, width):
+LANES = 128
+FACTS = 5
+
+
+def window(place_ref, idx_ref, b, block):
     k = idx_ref.shape[0]
-    cols = lax.broadcasted_iota(jnp.int32, (k, width), 1) + at
-    return jnp.where(idx_ref[...] == cols, 1.0, 0.0).astype(BF)
+    wide = min(k, block + LANES)
+    start = jnp.minimum(place_ref[FACTS + b] // LANES * LANES, k - wide)
+    at = pl.ds(pl.multiple_of(start, LANES), wide)
+    cols = lax.broadcasted_iota(jnp.int32, (wide, block), 1) + b * block
+    return at, jnp.where(idx_ref[at, :] == cols, 1.0, 0.0).astype(BF)
 
 
 def by_core(core, early, late, put):
@@ -42,6 +49,13 @@
             for blocks, steps in ((early, EARLY), (late, LATE)):
                 put(blocks[0], steps, mine)
                 put(blocks[1], steps, other)
+
+
+def start(sem, *pairs):
+    copies = [pltpu.make_async_copy(a, b, sem.at[i]) for i, (a, b) in enumerate(pairs)]
+    for copy in copies:
+        copy.start()
+    return copies
 
 
 def child_weights(here, core, early, late, a_ref, c_ref):
@@ -65,14 +79,27 @@
 
 
 def forward_kernel(
-    place_ref, early_ref, early_far_ref, late_ref, late_far_ref, rhs_ref, root_ref, idx_ref,
-    placed_ref, out_ref, solved_ref, a_ref, c_ref, sem,
+    place_ref, early_in_ref, early_far_in_ref, late_in_ref, late_far_in_ref, rhs_in_ref,
+    root_in_ref, idx_ref, *refs,
 ):
-    here, core, sub, order = (place_ref[i] for i in range(4))
+    outs, solved_out_ref = refs[:X], refs[X]
+    (
+        a_ref, c_ref, early_ref, early_far_ref, late_ref, late_far_ref, solved_ref, rhs_ref, root_ref,
+        update_ref, placed_ref, sem,
+    ) = refs[X + 1 :]
+    here, core, sub, order, x = (place_ref[i] for i in range(FACTS))
+    loads = start(
+        sem, (early_in_ref, early_ref), (early_far_in_ref, early_far_ref), (late_in_ref, late_ref),
+        (late_far_in_ref, late_far_ref), (rhs_in_ref, rhs_ref), (root_in_ref, root_ref),
+    )
+    for load in loads[:4]:
+        load.wait()
     s1, n = rhs_ref.shape
     q1 = s1 // ZL
     block = root_ref.shape[0]
     child_weights(here, core, (early_ref, early_far_ref), (late_ref, late_far_ref), a_ref, c_ref)
+    for load in loads[4:]:
+        load.wait()
     rows = lax.broadcasted_iota(jnp.int32, (s1, n), 0)
     source = jnp.where(rows < order, rhs_ref[...], 0.0).astype(BF)
     for q in range(ZL):
@@ -80,21 +107,45 @@
         part = dot(a_ref[q * q1 : top, :top], source[:top])
         part = jnp.where(rows[q * q1 : top] < order, part, 0.0)
         solved_ref[:, q * q1 : top] = part.T
-    copy = pltpu.make_async_copy(solved_ref, out_ref, sem)
-    copy.start()
-    update = dot(solved_ref[...].astype(BF), c_ref[...], 1, 1).astype(BF)
+    store = pltpu.make_async_copy(solved_ref, solved_out_ref, sem.at[6])
+    store.start()
+    update_ref[...] = dot(solved_ref[...].astype(BF), c_ref[...], 1, 1).astype(BF)
     root = root_ref[...].T
     for b in range(placed_ref.shape[1] // block):
-        part = dot(update, onehot(idx_ref, b * block, block))
+        at, hot = window(place_ref, idx_ref, b, block)
         placed_ref[:, b * block : (b + 1) * block] = (
-            jnp.where(sub == b, root, 0.0) - part
+            jnp.where(sub == b, root, 0.0) - dot(update_ref[:, at], hot)
         ).astype(BF)
-    copy.wait()
-
-
-def root_kernel(place_ref, s_ref, mine_ref, other_ref, out_ref, r_ref, f_ref):
+    group = n // X
+    for i, out_ref in enumerate(outs):
+        at = pl.multiple_of(lax.rem(x + i, X) * group, group)
+        out_ref[...] = placed_ref[pl.ds(at, group), :]
+    store.wait()
+
+
+def stack_kernel(place_ref, *refs):
+    *blocks, out_ref, sem = refs
+    copies = [
+        pltpu.make_async_copy(ref, out_ref.at[i], sem.at[i]) for i, ref in enumerate(blocks)
+    ]
+    for copy in copies:
+        copy.start()
+    for copy in copies:
+        copy.wait()
+
+
+def sum_kernel(place_ref, a_ref, b_ref, c_ref, d_ref, out_ref):
+    total = a_ref[...].astype(F32) + b_ref[...].astype(F32)
+    total += c_ref[...].astype(F32) + d_ref[...].astype(F32)
+    out_ref[...] = total.astype(BF)
+
+
+def root_kernel(
+    place_ref, near_ref, far_ref, mine_ref, other_ref, out_ref, sent_ref, r_ref, f_ref
+):
     core = place_ref[1]
-    q0 = s_ref.shape[1] // ZL
+    s = (near_ref[...].astype(F32) + far_ref[...].astype(F32)).astype(BF)
+    q0 = s.shape[1] // ZL
     rc = mine_ref.shape[1]
     step = f_ref.shape[1] // ZL
 
@@ -114,31 +165,36 @@
         left = spans[-1][1] if q else 0
         spans.append((left, left + (X - q) * step))
     for q in range(ZL):
-        term = dot(s_ref[:, q * q0 : (q + 1) * q0], r_ref[:, spans[q][0] : spans[q][1]])
+        term = dot(s[:, q * q0 : (q + 1) * q0], r_ref[:, spans[q][0] : spans[q][1]])
         f_ref[:, q * step :] = term if q == 0 else f_ref[:, q * step :] + term
     f = f_ref[...].astype(BF)
     for q in range(ZL):
-        out_ref[:, q * q0 : (q + 1) * q0] = dot(
-            f[:, q * step :], r_ref[:, spans[q][0] : spans[q][1]], 1, 1
-        )
+        part = dot(f[:, q * step :], r_ref[:, spans[q][0] : spans[q][1]], 1, 1)
+        out_ref[:, q * q0 : (q + 1) * q0] = part
+        sent_ref[:, q * q0 : (q + 1) * q0] = part.astype(BF)
 
 
 def backward_kernel(
-    place_ref, x_ref, in_ref, early_ref, early_far_ref, late_ref, late_far_ref, idx_ref,
-    out_ref, root_ref, solved_ref, a_ref, c_ref, sem,
+    place_ref, x_ref, in_ref, early_in_ref, early_far_in_ref, late_in_ref, late_far_in_ref, idx_ref,
+    out_ref, root_ref, a_ref, c_ref, early_ref, early_far_ref, late_ref, late_far_ref, solved_ref,
+    picked_ref, sem,
 ):
     here, core, sub, order = (place_ref[i] for i in range(4))
-    copy = pltpu.make_async_copy(in_ref, solved_ref, sem)
-    copy.start()
+    *loads, copy = start(
+        sem, (early_in_ref, early_ref), (early_far_in_ref, early_far_ref), (late_in_ref, late_ref),
+        (late_far_in_ref, late_far_ref), (in_ref, solved_ref),
+    )
+    for load in loads:
+        load.wait()
     child_weights(here, core, (early_ref, early_far_ref), (late_ref, late_far_ref), a_ref, c_ref)
     n, s1 = solved_ref.shape
     q1 = s1 // ZL
     block = root_ref.shape[0]
-    picked = None
+    picked_ref[...] = jnp.zeros_like(picked_ref)
     for b in range(x_ref.shape[1] // block):
-        part = dot(x_ref[:, b * block : (b + 1) * block], onehot(idx_ref, b * block, block), 1, 1)
-        picked = part if picked is None else picked + part
-    pulled = dot(picked.astype(BF), c_ref[...])
+        at, hot = window(place_ref, idx_ref, b, block)
+        picked_ref[:, at] += dot(x_ref[:, b * block : (b + 1) * block], hot, 1, 1)
+    pulled = dot(picked_ref[...].astype(BF), c_ref[...])
     cols = lax.broadcasted_iota(jnp.int32, (n, s1), 1)
     copy.wait()
     residue = jnp.where(cols < order, solved_ref[...] - pulled, 0.0).astype(BF)
@@ -155,12 +211,18 @@
     left = 0
     for q in range(ZL):
         for x in range(q, X):
-            out_ref[:, left : left + block] = r_ref[x, q]
+            for y in range(Y):
+                out_ref[y, :, left : left + block] = r_ref[x, q]
             left += block
 
 
 def call(kernel, outs, args, scratch=(), flops=0, far=((), ())):
     moved = sum(a.size * a.dtype.itemsize for a in (*args, *outs))
+    args = [
+        pltpu.with_memory_space_constraint(a, pltpu.HBM) if i in far[0] else a
+        for i, a in enumerate(args)
+    ]
+    outs = [pltpu.HBM(a.shape, a.dtype) if i in far[1] else a for i, a in enumerate(outs)]
     vmem = pl.BlockSpec(memory_space=pltpu.VMEM)
     hbm = pl.BlockSpec(memory_space=pltpu.HBM)
     return pl.pallas_call(
@@ -175,6 +237,12 @@
     )(*args)
 
 
+def stack(place, *blocks):
+    out = jax.ShapeDtypeStruct((len(blocks), *blocks[0].shape), blocks[0].dtype)
+    sems = [pltpu.SemaphoreType.DMA((len(blocks),))]
+    return call(stack_kernel, [out], [place, *blocks], sems, far=((), (0,)))[0]
+
+
 def on_device(
     child_rhs, root_rhs, child_inverse, coupling_block, root_inverse, child_orders, coupling_rows
 ):
@@ -187,8 +255,11 @@
     r1 = child_inverse.shape[1]
     block = root_rhs.shape[0]
     sub = lax.axis_index("x") * ZH + lax.axis_index("zh")
-    place = jnp.stack([lax.axis_index("y"), lax.axis_index("core"), sub, child_orders[0]])
     idx = coupling_rows[0][:, None]
+    edges = lax.iota(jnp.int32, s0 // block) * block
+    below = jnp.sum((coupling_rows < edges[:, None]).astype(jnp.int32), axis=1)
+    facts = [lax.axis_index("y"), lax.axis_index("core"), sub, child_orders[0], lax.axis_index("x")]
+    place = jnp.concatenate([jnp.stack(facts), below])
     shape = jax.ShapeDtypeStruct
 
     pair = jnp.concatenate([child_inverse[0], coupling_block[0]], axis=0)
@@ -203,58 +274,63 @@
     up = {1: lax.ppermute(own, "y", FORTH)}
     down = {1: lax.ppermute(own, "y", BACK)}
     rt = gather_blocks(rt, "x", X)
-    rwidth = block * sum(X - q for q in range(ZL))
-    rt, = call(pack_kernel, [shape((rt.shape[2], rwidth), BF)], [place, rt])
     up[2] = lax.ppermute(up[1], "y", FORTH)
     down[2] = lax.ppermute(down[1], "y", BACK)
-    early = jnp.stack([own, up[1], down[1], up[2], down[2]])
+    rwidth = block * sum(X - q for q in range(ZL))
+    rt = after(rt, up[2], down[2])
+    rt, = call(pack_kernel, [shape((Y, rt.shape[2], rwidth), BF)], [place, rt])
+    early = stack(place, own, up[1], down[1], up[2], down[2])
     early_far = lax.ppermute(early, "core", SWAP)
     up[3] = lax.ppermute(up[2], "y", FORTH)
     down[3] = lax.ppermute(down[2], "y", BACK)
     up[4] = lax.ppermute(up[3], "y", FORTH)
-    late = jnp.stack([up[3], down[3], up[4]])
+    late = stack(place, up[3], down[3], up[4])
     late_far = lax.ppermute(late, "core", SWAP)
-    rmine = gather_blocks(after(rt, up[3], down[3]), "y", Y)
+    rmine = lax.all_to_all(after(rt, up[3], down[3]), "y", 0, 0, tiled=True)
 
     weights = [early, early_far, late, late_far]
     scratch = [pltpu.VMEM((s1, s1), BF), pltpu.VMEM((k, s1), BF)]
+    scratch += [pltpu.VMEM(w.shape, BF) for w in weights] + [pltpu.VMEM((n, s1), F32)]
     flops = 2 * n * (s1 * s1 + k * s1 + k * s0)
-    placed, solved = call(
+    group = n // X
+    *blocks, solved = call(
         forward_kernel,
-        [shape((n, s0), BF), shape((n, s1), F32)],
+        [shape((group, s0), BF)] * X + [shape((n, s1), F32)],
         [place, *weights, child_rhs[0], root_rhs, idx],
-        [pltpu.VMEM((n, s1), F32), *scratch, pltpu.SemaphoreType.DMA],
+        [
+            *scratch, pltpu.VMEM((s1, n), F32), pltpu.VMEM((block, n), F32),
+            pltpu.VMEM((n, k), BF), pltpu.VMEM((n, s0), BF), pltpu.SemaphoreType.DMA((7,)),
+        ],
         flops,
-        ((), (1,)),
-    )
-    here = lax.axis_index("x")
-    blocks = placed.reshape(X, n // X, s0)
-    block_for = lambda i: lax.dynamic_index_in_dim(blocks, lax.rem(here + i, X), 0, False)
+        ((1, 2, 3, 4, 5, 6), (X,)),
+    )
     parts = [
-        lax.ppermute(block_for(i), "x", [(j, (j + i) % X) for j in range(X)]) for i in (1, 3, 2)
+        lax.ppermute(blocks[i], "x", [(j, (j + i) % X) for j in range(X)]) for i in (1, 3, 2)
     ]
-    part = sum((p.astype(F32) for p in parts), block_for(0).astype(F32))
-    rmine = after(rmine, part)
+    near, = call(sum_kernel, [shape((group, s0), BF)], [place, blocks[0], *parts])
+    rmine = after(rmine, near)
     rother = lax.ppermute(rmine, "core", SWAP)
-    s_t = (part + lax.ppermute(part.astype(BF), "zh", SWAP).astype(F32)).astype(BF)
-
-    x_part, = call(
+    far = lax.ppermute(near, "zh", SWAP)
+
+    x_part, x_sent = call(
         root_kernel,
-        [shape((n // X, s0), F32)],
-        [place, s_t, rmine, rother],
-        [pltpu.VMEM((q0, rwidth), BF), pltpu.VMEM((n // X, s0 // ZH), F32)],
-        4 * (n // X) * q0 * rwidth,
-    )
-    x_t = x_part + lax.ppermute(x_part.astype(BF), "zh", SWAP).astype(F32)
+        [shape((group, s0), F32), shape((group, s0), BF)],
+        [place, near, far, rmine, rother],
+        [
+            pltpu.VMEM((q0, rwidth), BF), pltpu.VMEM((group, s0 // ZH), F32),
+        ],
+        4 * group * q0 * rwidth,
+    )
+    x_t = x_part + lax.ppermute(x_sent, "zh", SWAP).astype(F32)
     x_all = gather_blocks(x_t.astype(BF), "x", X).reshape(n, s0)
 
     child_out, root_out = call(
         backward_kernel,
         [shape((s1, n), F32), shape((block, n), F32)],
         [place, x_all, solved, *weights, idx],
-        [pltpu.VMEM((n, s1), F32), *scratch, pltpu.SemaphoreType.DMA],
+        [*scratch, pltpu.VMEM((n, k), F32), pltpu.SemaphoreType.DMA((5,))],
         flops,
-        ((2,), ()),
+        ((2, 3, 4, 5, 6), ()),
     )
     return (child_out[None], root_out)
 

time: 171 us -> 188 us (1.099)
  the two profiles are of different devices: /device:TPU:1 before, /device:TPU:192 now
where the time goes in v7:
time: 188 us; the launch traced here: 187 us
  waiting for transfers between devices  66.8 us (36%)
  starting transfers between devices  63.3 us (34%)
  blocking collectives  32.8 us (17%)
  Pallas kernels  19.8 us (11%)
  local copies, waits for them, and re-layouts  2.07 us (1%)
    all_to_all x2, blocking collectives, gather_blocks(): lax.all_to_all(jnp.broadcast_to(x[None], (length, *x.shape)), axis, 0, 0,...  32.8 us
    ppermute x1, waiting for transfers between devices, on_device(): up[4] = lax.ppermute(up[3], 'y', FORTH)  24.9 us
    pallas_call x7, Pallas kernels, call(): pl.pallas_call(kernel, out_shape=outs, in_specs=[pl.BlockSpec(memory_spac...  19.8 us
    ppermute x1, waiting for transfers between devices, on_device(): x_t = x_part + lax.ppermute(x_sent, 'zh', SWAP).astype(F32)  13 us
    ppermute x1, waiting for transfers between devices, on_device(): far = lax.ppermute(near, 'zh', SWAP)  12.6 us
    ppermute x3, starting transfers between devices, on_device(): lax.ppermute(blocks[i], 'x', [(j, (j + i) % X) for j in range(X)])  10.8 us
    ppermute x1, starting transfers between devices, on_device(): far = lax.ppermute(near, 'zh', SWAP)  8.21 us
    ppermute x3, waiting for transfers between devices, on_device(): lax.ppermute(blocks[i], 'x', [(j, (j + i) % X) for j in range(X)])  7.45 us
  transfers between devices with their start and end apart: 17, of which 9 were waited for; matrix products, arithmetic and copies ran while one was open for 1% of the time, Pallas kernels for 6%

profile of v7, /device:TPU:192, one launch (start us, length us, event | category | flops | bytes accessed | tf_op | source)
XLA Modules:
  0.0 187.3 jit_solution(7977314382108547225)
XLA Ops:
  1.5 12.8 %all_to_all.20 = bf16[4,32,1280]{2,1,0:T(8,128)(2,1)S(1)} all-to-all(bf16[4,32,1280]{2,1,0:T(8,128)(2,1)S(1)} %broadcast_in_dim.8), channel_id=1, replica_groups=mesh['zl'=4,'y'=8,'core'=2,'x'=4,'zh'=2] {'zl'}, dimensions={0} | all-to-all | bytes 655360 | tf_op jit(solution)/shard_map/all_to_all | solution.py:20
  14.4 5.4 %collective-permute-start.1 = (bf16[16,6656]{1,0:T(8,128)(2,1)S(1)}, bf16[16,6656]{1,0:T(8,128)(2,1)S(1)}, u32[]{:S(2)}, u32[]{:S(2)}) collective-permute-start(bf16[16,6656]{1,0:T(8,128)(2,1)S(1)} %constant_dynamic-update-slice_fusion.refs_0_), channel_id=1, source_target_pairs={{0,112},{16,0},{32,16},{48,32},{64,48},{80,64},{96,80},{112,96},{1... | collective-permute-start | bytes 638984 | tf_op jit(solution)/shard_map/ppermute | solution.py:275
  19.7 1.9 %collective-permute-start = (bf16[16,6656]{1,0:T(8,128)(2,1)S(1)}, bf16[16,6656]{1,0:T(8,128)(2,1)S(1)}, u32[]{:S(2)}, u32[]{:S(2)}) collective-permute-start(bf16[16,6656]{1,0:T(8,128)(2,1)S(1)} %constant_dynamic-update-slice_fusion.refs_0_), channel_id=1, source_target_pairs={{0,16},{16,32},{32,48},{48,64},{64,80},{80,96},{96,112},{112,0},{1... | collective-permute-start | bytes 638984 | tf_op jit(solution)/shard_map/ppermute | solution.py:274
  21.7 1.8 collective-permute-done.1.refs_2_
  23.5 5.6 %collective-permute-start.3 = (bf16[16,6656]{1,0:T(8,128)(2,1)S(1)}, bf16[16,6656]{1,0:T(8,128)(2,1)S(1)}, u32[]{:S(2)}, u32[]{:S(2)}) collective-permute-start(bf16[16,6656]{1,0:T(8,128)(2,1)S(1)} %collective-permute-done.1.refs_2_), channel_id=1, source_target_pairs={{0,112},{16,0},{32,16},{48,32},{64,48},{80,64},{96,80},{112,96},{1... | collective-permute-start | bytes 638984 | tf_op jit(solution)/shard_map/ppermute | solution.py:278
  29.1 1.9 %collective-permute-start.2 = (bf16[16,6656]{1,0:T(8,128)(2,1)S(1)}, bf16[16,6656]{1,0:T(8,128)(2,1)S(1)}, u32[]{:S(2)}, u32[]{:S(2)}) collective-permute-start(bf16[16,6656]{1,0:T(8,128)(2,1)S(1)} %collective-permute-done.refs_1_), channel_id=1, source_target_pairs={{0,16},{16,32},{32,48},{48,64},{64,80},{80,96},{96,112},{112,0},{1... | collective-permute-start | bytes 638984 | tf_op jit(solution)/shard_map/ppermute | solution.py:277
  32.4 4.3 %all-to-all-start.1 = ((bf16[4,4,32,256]{3,2,1,0:T(8,128)(2,1)}), bf16[4,4,32,256]{3,2,1,0:T(8,128)(2,1)S(1)}, u32[]{:S(2)}, u32[]{:S(2)}) async-start(bf16[4,4,32,256]{3,2,1,0:T(8,128)(2,1)} %broadcast_in_dim.9), calls=%async_computation.1 | async-start | bytes 524288 | tf_op jit(solution)/shard_map/all_to_all | solution.py:20
  36.7 5.1 %collective-permute-start.6 = (bf16[16,6656]{1,0:T(8,128)(2,1)S(1)}, bf16[16,6656]{1,0:T(8,128)(2,1)S(1)}, u32[]{:S(2)}, u32[]{:S(2)}) collective-permute-start(bf16[16,6656]{1,0:T(8,128)(2,1)S(1)} %collective-permute-done.3.refs_4_), channel_id=1, source_target_pairs={{0,112},{16,0},{32,16},{48,32},{64,48},{80,64},{96,80},{112,96},{1... | collective-permute-start | bytes 638984 | tf_op jit(solution)/shard_map/ppermute | solution.py:285
  41.8 1.9 %collective-permute-start.5 = (bf16[16,6656]{1,0:T(8,128)(2,1)S(1)}, bf16[16,6656]{1,0:T(8,128)(2,1)S(1)}, u32[]{:S(2)}, u32[]{:S(2)}) collective-permute-start(bf16[16,6656]{1,0:T(8,128)(2,1)S(1)} %collective-permute-done.2.refs_3_), channel_id=1, source_target_pairs={{0,16},{16,32},{32,48},{48,64},{64,80},{80,96},{96,112},{112,0},{1... | collective-permute-start | bytes 638984 | tf_op jit(solution)/shard_map/ppermute | solution.py:284
  44.1 1.7 shard_map.90
  45.8 5.0 %collective-permute-done.5.refs_0_ = bf16[16,6656]{1,0:T(8,128)(2,1)S(1)} collective-permute-done((bf16[16,6656]{1,0:T(8,128)(2,1)S(1)}, bf16[16,6656]{1,0:T(8,128)(2,1)S(1)}, u32[]{:S(2)}, u32[]{:S(2)}) %collective-permute-start.5) | collective-permute-done | bytes 213024 | tf_op jit(solution)/shard_map/ppermute | solution.py:284
  50.8 4.1 %all-to-all-start.2 = ((bf16[8,32,2560]{2,1,0:T(8,128)(2,1)}), bf16[8,32,2560]{2,1,0:T(8,128)(2,1)S(1)}, u32[]{:S(2)}, u32[]{:S(2)}) async-start(bf16[8,32,2560]{2,1,0:T(8,128)(2,1)} %shard_map.90), calls=%async_computation.2 | async-start | bytes 2621440 | tf_op jit(solution)/shard_map/all_to_all | solution.py:289
  54.9 1.6 shard_map.86.early_in_ref
  56.4 1.9 %collective-permute-start.4 = (bf16[5,16,6656]{2,1,0:T(8,128)(2,1)}, bf16[5,16,6656]{2,1,0:T(8,128)(2,1)}, u32[]{:S(2)}, u32[]{:S(2)}) collective-permute-start(bf16[5,16,6656]{2,1,0:T(8,128)(2,1)} %shard_map.86.early_in_ref), channel_id=1, source_target_pairs={{0,8},{8,0},{1,9},{9,1},{2,10},{10,2},{3,11},{11,3},{4,12},{12,4},... | collective-permute-start | bytes 3194888 | tf_op jit(solution)/shard_map/ppermute | solution.py:283
  58.4 3.9 %collective-permute-start.7 = (bf16[16,6656]{1,0:T(8,128)(2,1)S(1)}, bf16[16,6656]{1,0:T(8,128)(2,1)S(1)}, u32[]{:S(2)}, u32[]{:S(2)}) collective-permute-start(bf16[16,6656]{1,0:T(8,128)(2,1)S(1)} %collective-permute-done.5.refs_0_), channel_id=1, source_target_pairs={{0,16},{16,32},{32,48},{48,64},{64,80},{80,96},{96,112},{112,0},{1... | collective-permute-start | bytes 638984 | tf_op jit(solution)/shard_map/ppermute | solution.py:286
  62.3 24.9 %collective-permute-done.7.refs_2_ = bf16[16,6656]{1,0:T(8,128)(2,1)S(1)} collective-permute-done((bf16[16,6656]{1,0:T(8,128)(2,1)S(1)}, bf16[16,6656]{1,0:T(8,128)(2,1)S(1)}, u32[]{:S(2)}, u32[]{:S(2)}) %collective-permute-start.7) | collective-permute-done | bytes 213024 | tf_op jit(solution)/shard_map/ppermute | solution.py:286
  88.6 1.9 %collective-permute-start.8 = (bf16[3,16,6656]{2,1,0:T(8,128)(2,1)}, bf16[3,16,6656]{2,1,0:T(8,128)(2,1)S(1)}, u32[]{:S(2)}, u32[]{:S(2)}) collective-permute-start(bf16[3,16,6656]{2,1,0:T(8,128)(2,1)} %shard_map.87.late_in_ref), channel_id=1, source_target_pairs={{0,8},{8,0},{1,9},{9,1},{2,10},{10,2},{3,11},{11,3},{4,12},{12,4},... | collective-permute-start | bytes 1916936 | tf_op jit(solution)/shard_map/ppermute | solution.py:288
  90.8 2.0 %collective-permute-done.8.late_far_in_ref = bf16[3,16,6656]{2,1,0:T(8,128)(2,1)S(1)} collective-permute-done((bf16[3,16,6656]{2,1,0:T(8,128)(2,1)}, bf16[3,16,6656]{2,1,0:T(8,128)(2,1)S(1)}, u32[]{:S(2)}, u32[]{:S(2)}) %collective-permute-start.8) | collective-permute-done | bytes 639008 | tf_op jit(solution)/shard_map/ppermute | solution.py:288
  93.6 5.9 %shard_map.88 = (bf16[64,2048]{1,0:T(8,128)(2,1)S(1)}, bf16[64,2048]{1,0:T(8,128)(2,1)S(1)}, bf16[64,2048]{1,0:T(8,128)(2,1)S(1)}, bf16[64,2048]{1,0:T(8,128)(2,1)S(1)}, f32[256,1024]{1,0:T(8,128)}) custom-call(s32[13]{0:T(128)S(1)} %concatenate.12.place_ref, bf16[5,16,6656]{2,1,0:T(8,128)(2,1)} %shard_map.86.early_in_ref, ...), custom_call_target="tpu_custom_call" | custom-call | flops 2147483648 | bytes 6819892 | tf_op jit(solution)/shard_map/pallas_call | solution.py:228
  99.6 3.4 %collective-permute-start.9 = (bf16[64,2048]{1,0:T(8,128)(2,1)S(1)}, bf16[64,2048]{1,0:T(8,128)(2,1)S(1)}, u32[]{:S(2)}, u32[]{:S(2)}) collective-permute-start(bf16[64,2048]{1,0:T(8,128)(2,1)S(1)} %get-tuple-element.16), channel_id=1, source_target_pairs={{0,2},{2,4},{4,6},{6,0},{1,3},{3,5},{5,7},{7,1},{8,10},{10,12},{12... | collective-permute-start | bytes 786440 | tf_op jit(solution)/shard_map/ppermute | solution.py:308
  103.0 3.6 %collective-permute-start.10 = (bf16[64,2048]{1,0:T(8,128)(2,1)S(1)}, bf16[64,2048]{1,0:T(8,128)(2,1)S(1)}, u32[]{:S(2)}, u32[]{:S(2)}) collective-permute-start(bf16[64,2048]{1,0:T(8,128)(2,1)S(1)} %get-tuple-element.17), channel_id=1, source_target_pairs={{0,6},{2,0},{4,2},{6,4},{1,7},{3,1},{5,3},{7,5},{8,14},{10,8},{12,... | collective-permute-start | bytes 786440 | tf_op jit(solution)/shard_map/ppermute | solution.py:308
  106.6 3.7 %collective-permute-start.11 = (bf16[64,2048]{1,0:T(8,128)(2,1)S(1)}, bf16[64,2048]{1,0:T(8,128)(2,1)S(1)}, u32[]{:S(2)}, u32[]{:S(2)}) collective-permute-start(bf16[64,2048]{1,0:T(8,128)(2,1)S(1)} %get-tuple-element.18), channel_id=1, source_target_pairs={{0,4},{2,6},{4,0},{6,2},{1,5},{3,7},{5,1},{7,3},{8,12},{10,14},{12... | collective-permute-start | bytes 786440 | tf_op jit(solution)/shard_map/ppermute | solution.py:308
  111.0 3.1 %collective-permute-done.10.c_ref = bf16[64,2048]{1,0:T(8,128)(2,1)S(1)} collective-permute-done((bf16[64,2048]{1,0:T(8,128)(2,1)S(1)}, bf16[64,2048]{1,0:T(8,128)(2,1)S(1)}, u32[]{:S(2)}, u32[]{:S(2)}) %collective-permute-start.10) | collective-permute-done | bytes 262176 | tf_op jit(solution)/shard_map/ppermute | solution.py:308
  114.1 3.7 %collective-permute-done.11.d_ref = bf16[64,2048]{1,0:T(8,128)(2,1)S(1)} collective-permute-done((bf16[64,2048]{1,0:T(8,128)(2,1)S(1)}, bf16[64,2048]{1,0:T(8,128)(2,1)S(1)}, u32[]{:S(2)}, u32[]{:S(2)}) %collective-permute-start.11) | collective-permute-done | bytes 262176 | tf_op jit(solution)/shard_map/ppermute | solution.py:308
  118.5 1.9 %collective-permute-start.13 = (bf16[8,32,2560]{2,1,0:T(8,128)(2,1)S(1)}, bf16[8,32,2560]{2,1,0:T(8,128)(2,1)S(1)}, u32[]{:S(2)}, u32[]{:S(2)}) collective-permute-start(bf16[8,32,2560]{2,1,0:T(8,128)(2,1)S(1)} %all-to-all-done.2.mine_ref), channel_id=1, source_target_pairs={{0,8},{8,0},{1,9},{9,1},{2,10},{10,2},{3,11},{11,3},{4,12},{12,4},... | collective-permute-start | bytes 3932168 | tf_op jit(solution)/shard_map/ppermute | solution.py:312
  120.4 8.2 %collective-permute-start.12 = (bf16[64,2048]{1,0:T(8,128)(2,1)S(1)}, bf16[64,2048]{1,0:T(8,128)(2,1)S(1)}, u32[]{:S(2)}, u32[]{:S(2)}) collective-permute-start(bf16[64,2048]{1,0:T(8,128)(2,1)S(1)} %shard_map.89.near_ref), channel_id=1, source_target_pairs={{0,1},{1,0},{2,3},{3,2},{4,5},{5,4},{6,7},{7,6},{8,9},{9,8},{10,11... | collective-permute-start | bytes 786440 | tf_op jit(solution)/shard_map/ppermute | solution.py:313
  128.7 12.6 %collective-permute-done.12.far_ref = bf16[64,2048]{1,0:T(8,128)(2,1)S(1)} collective-permute-done((bf16[64,2048]{1,0:T(8,128)(2,1)S(1)}, bf16[64,2048]{1,0:T(8,128)(2,1)S(1)}, u32[]{:S(2)}, u32[]{:S(2)}) %collective-permute-start.12) | collective-permute-done | bytes 262176 | tf_op jit(solution)/shard_map/ppermute | solution.py:313
  141.3 2.2 %shard_map.91 = (f32[64,2048]{1,0:T(8,128)S(1)}, bf16[64,2048]{1,0:T(8,128)(2,1)S(1)}) custom-call(s32[13]{0:T(128)S(1)} %concatenate.12.place_ref, bf16[64,2048]{1,0:T(8,128)(2,1)S(1)} %shard_map.89.near_ref, bf16[64,2048]{1,0:T(8,128)(2,1)S(1)} %collective-permute-done.12.far_ref, bf16[8,32,2560]{2,1,0:T(8,128)(2,1)S(1)} %all-to-all-done.2.mine_ref, ...), custom_call_target="tpu_custom_call" | custom-call | flops 335544320 | bytes 3932212 | tf_op jit(solution)/shard_map/pallas_call | solution.py:228
  143.5 4.3 %collective-permute-start.14 = (bf16[64,2048]{1,0:T(8,128)(2,1)S(1)}, bf16[64,2048]{1,0:T(8,128)(2,1)S(1)}, u32[]{:S(2)}, u32[]{:S(2)}) collective-permute-start(bf16[64,2048]{1,0:T(8,128)(2,1)S(1)} %get-tuple-element.24), channel_id=1, source_target_pairs={{0,1},{1,0},{2,3},{3,2},{4,5},{5,4},{6,7},{7,6},{8,9},{9,8},{10,11... | collective-permute-start | bytes 786440 | tf_op jit(solution)/shard_map/ppermute | solution.py:324
  147.8 13.0 %collective-permute-done.14 = bf16[64,2048]{1,0:T(8,128)(2,1)S(1)} collective-permute-done((bf16[64,2048]{1,0:T(8,128)(2,1)S(1)}, bf16[64,2048]{1,0:T(8,128)(2,1)S(1)}, u32[]{:S(2)}, u32[]{:S(2)}) %collective-permute-start.14) | collective-permute-done | bytes 262176 | tf_op jit(solution)/shard_map/ppermute | solution.py:324
  161.0 20.0 %all_to_all.21 = bf16[4,64,2048]{2,1,0:T(8,128)(2,1)S(1)} all-to-all(bf16[4,64,2048]{2,1,0:T(8,128)(2,1)S(1)} %broadcast_in_dim.10), channel_id=1, replica_groups=mesh['zl'=4,'y'=8,'core'=2,'x'=4,'zh'=2] {'x'}, dimensions={0} | all-to-all | bytes 2097152 | tf_op jit(solution)/shard_map/all_to_all | solution.py:20
  181.0 6.3 %shard_map.92 = (f32[1024,256]{1,0:T(8,128)}, f32[256,256]{1,0:T(8,128)}) custom-call(s32[13]{0:T(128)S(1)} %concatenate.12.place_ref, bf16[256,2048]{1,0:T(8,128)(2,1)S(1)} %bitcast.44, f32[256,1024]{1,0:T(8,128)} %get-tuple-element.25.in_ref, bf16[5,16,6656]{2,1,0:T(8,128)(2,1)} %shard_map.86.early_in_ref, ...), custom_call_target="tpu_custom_call" | custom-call | flops 2147483648 | bytes 6819892 | tf_op jit(solution)/shard_map/pallas_call | solution.py:228
  (33 shorter events, 5.9 us)
Async XLA Ops:
  0.6 43.1 %copy-start = (s32[1,1024]{1,0:T(1,128)S(1)}, s32[1,1024]{1,0:T(1,128)}, u32[]{:S(2)}) copy-start(s32[1,1024]{1,0:T(1,128)} %param.13) | copy-start | bytes 12292
  14.4 9.1 %collective-permute-start.1 = (bf16[16,6656]{1,0:T(8,128)(2,1)S(1)}, bf16[16,6656]{1,0:T(8,128)(2,1)S(1)}, u32[]{:S(2)}, u32[]{:S(2)}) collective-permute-start(bf16[16,6656]{1,0:T(8,128)(2,1)S(1)} %constant_dynamic-update-slice_fusion.refs_0_), channel_id=1, source_target_pairs={{0,112},{16,0},{32,16},{48,32},{64,48},{80,64},{96,80},{112,96},{1... | collective-permute-start | bytes 638984 | tf_op jit(solution)/shard_map/ppermute | solution.py:275
  19.7 9.3 %collective-permute-start = (bf16[16,6656]{1,0:T(8,128)(2,1)S(1)}, bf16[16,6656]{1,0:T(8,128)(2,1)S(1)}, u32[]{:S(2)}, u32[]{:S(2)}) collective-permute-start(bf16[16,6656]{1,0:T(8,128)(2,1)S(1)} %constant_dynamic-update-slice_fusion.refs_0_), channel_id=1, source_target_pairs={{0,16},{16,32},{32,48},{48,64},{64,80},{80,96},{96,112},{112,0},{1... | collective-permute-start | bytes 638984 | tf_op jit(solution)/shard_map/ppermute | solution.py:274
  23.5 13.2 %collective-permute-start.3 = (bf16[16,6656]{1,0:T(8,128)(2,1)S(1)}, bf16[16,6656]{1,0:T(8,128)(2,1)S(1)}, u32[]{:S(2)}, u32[]{:S(2)}) collective-permute-start(bf16[16,6656]{1,0:T(8,128)(2,1)S(1)} %collective-permute-done.1.refs_2_), channel_id=1, source_target_pairs={{0,112},{16,0},{32,16},{48,32},{64,48},{80,64},{96,80},{112,96},{1... | collective-permute-start | bytes 638984 | tf_op jit(solution)/shard_map/ppermute | solution.py:278
  29.1 12.8 %collective-permute-start.2 = (bf16[16,6656]{1,0:T(8,128)(2,1)S(1)}, bf16[16,6656]{1,0:T(8,128)(2,1)S(1)}, u32[]{:S(2)}, u32[]{:S(2)}) collective-permute-start(bf16[16,6656]{1,0:T(8,128)(2,1)S(1)} %collective-permute-done.refs_1_), channel_id=1, source_target_pairs={{0,16},{16,32},{32,48},{48,64},{64,80},{80,96},{96,112},{112,0},{1... | collective-permute-start | bytes 638984 | tf_op jit(solution)/shard_map/ppermute | solution.py:277
  32.4 11.7 %all-to-all-start.1 = ((bf16[4,4,32,256]{3,2,1,0:T(8,128)(2,1)}), bf16[4,4,32,256]{3,2,1,0:T(8,128)(2,1)S(1)}, u32[]{:S(2)}, u32[]{:S(2)}) async-start(bf16[4,4,32,256]{3,2,1,0:T(8,128)(2,1)} %broadcast_in_dim.9), calls=%async_computation.1 | async-start | bytes 524288 | tf_op jit(solution)/shard_map/all_to_all | solution.py:20
  36.7 9.1 %collective-permute-start.6 = (bf16[16,6656]{1,0:T(8,128)(2,1)S(1)}, bf16[16,6656]{1,0:T(8,128)(2,1)S(1)}, u32[]{:S(2)}, u32[]{:S(2)}) collective-permute-start(bf16[16,6656]{1,0:T(8,128)(2,1)S(1)} %collective-permute-done.3.refs_4_), channel_id=1, source_target_pairs={{0,112},{16,0},{32,16},{48,32},{64,48},{80,64},{96,80},{112,96},{1... | collective-permute-start | bytes 638984 | tf_op jit(solution)/shard_map/ppermute | solution.py:285
  41.8 8.9 %collective-permute-start.5 = (bf16[16,6656]{1,0:T(8,128)(2,1)S(1)}, bf16[16,6656]{1,0:T(8,128)(2,1)S(1)}, u32[]{:S(2)}, u32[]{:S(2)}) collective-permute-start(bf16[16,6656]{1,0:T(8,128)(2,1)S(1)} %collective-permute-done.2.refs_3_), channel_id=1, source_target_pairs={{0,16},{16,32},{32,48},{48,64},{64,80},{80,96},{96,112},{112,0},{1... | collective-permute-start | bytes 638984 | tf_op jit(solution)/shard_map/ppermute | solution.py:284
  50.8 67.7 %all-to-all-start.2 = ((bf16[8,32,2560]{2,1,0:T(8,128)(2,1)}), bf16[8,32,2560]{2,1,0:T(8,128)(2,1)S(1)}, u32[]{:S(2)}, u32[]{:S(2)}) async-start(bf16[8,32,2560]{2,1,0:T(8,128)(2,1)} %shard_map.90), calls=%async_computation.2 | async-start | bytes 2621440 | tf_op jit(solution)/shard_map/all_to_all | solution.py:289
  56.4 36.3 %collective-permute-start.4 = (bf16[5,16,6656]{2,1,0:T(8,128)(2,1)}, bf16[5,16,6656]{2,1,0:T(8,128)(2,1)}, u32[]{:S(2)}, u32[]{:S(2)}) collective-permute-start(bf16[5,16,6656]{2,1,0:T(8,128)(2,1)} %shard_map.86.early_in_ref), channel_id=1, source_target_pairs={{0,8},{8,0},{1,9},{9,1},{2,10},{10,2},{3,11},{11,3},{4,12},{12,4},... | collective-permute-start | bytes 3194888 | tf_op jit(solution)/shard_map/ppermute | solution.py:283
  58.4 28.8 %collective-permute-start.7 = (bf16[16,6656]{1,0:T(8,128)(2,1)S(1)}, bf16[16,6656]{1,0:T(8,128)(2,1)S(1)}, u32[]{:S(2)}, u32[]{:S(2)}) collective-permute-start(bf16[16,6656]{1,0:T(8,128)(2,1)S(1)} %collective-permute-done.5.refs_0_), channel_id=1, source_target_pairs={{0,16},{16,32},{32,48},{48,64},{64,80},{80,96},{96,112},{112,0},{1... | collective-permute-start | bytes 638984 | tf_op jit(solution)/shard_map/ppermute | solution.py:286
  88.6 4.2 %collective-permute-start.8 = (bf16[3,16,6656]{2,1,0:T(8,128)(2,1)}, bf16[3,16,6656]{2,1,0:T(8,128)(2,1)S(1)}, u32[]{:S(2)}, u32[]{:S(2)}) collective-permute-start(bf16[3,16,6656]{2,1,0:T(8,128)(2,1)} %shard_map.87.late_in_ref), channel_id=1, source_target_pairs={{0,8},{8,0},{1,9},{9,1},{2,10},{10,2},{3,11},{11,3},{4,12},{12,4},... | collective-permute-start | bytes 1916936 | tf_op jit(solution)/shard_map/ppermute | solution.py:288
  92.8 0.9 copy-start.1
  99.6 11.5 %collective-permute-start.9 = (bf16[64,2048]{1,0:T(8,128)(2,1)S(1)}, bf16[64,2048]{1,0:T(8,128)(2,1)S(1)}, u32[]{:S(2)}, u32[]{:S(2)}) collective-permute-start(bf16[64,2048]{1,0:T(8,128)(2,1)S(1)} %get-tuple-element.16), channel_id=1, source_target_pairs={{0,2},{2,4},{4,6},{6,0},{1,3},{3,5},{5,7},{7,1},{8,10},{10,12},{12... | collective-permute-start | bytes 786440 | tf_op jit(solution)/shard_map/ppermute | solution.py:308
  103.0 11.1 %collective-permute-start.10 = (bf16[64,2048]{1,0:T(8,128)(2,1)S(1)}, bf16[64,2048]{1,0:T(8,128)(2,1)S(1)}, u32[]{:S(2)}, u32[]{:S(2)}) collective-permute-start(bf16[64,2048]{1,0:T(8,128)(2,1)S(1)} %get-tuple-element.17), channel_id=1, source_target_pairs={{0,6},{2,0},{4,2},{6,4},{1,7},{3,1},{5,3},{7,5},{8,14},{10,8},{12,... | collective-permute-start | bytes 786440 | tf_op jit(solution)/shard_map/ppermute | solution.py:308
  106.6 11.2 %collective-permute-start.11 = (bf16[64,2048]{1,0:T(8,128)(2,1)S(1)}, bf16[64,2048]{1,0:T(8,128)(2,1)S(1)}, u32[]{:S(2)}, u32[]{:S(2)}) collective-permute-start(bf16[64,2048]{1,0:T(8,128)(2,1)S(1)} %get-tuple-element.18), channel_id=1, source_target_pairs={{0,4},{2,6},{4,0},{6,2},{1,5},{3,7},{5,1},{7,3},{8,12},{10,14},{12... | collective-permute-start | bytes 786440 | tf_op jit(solution)/shard_map/ppermute | solution.py:308
  118.5 22.8 %collective-permute-start.13 = (bf16[8,32,2560]{2,1,0:T(8,128)(2,1)S(1)}, bf16[8,32,2560]{2,1,0:T(8,128)(2,1)S(1)}, u32[]{:S(2)}, u32[]{:S(2)}) collective-permute-start(bf16[8,32,2560]{2,1,0:T(8,128)(2,1)S(1)} %all-to-all-done.2.mine_ref), channel_id=1, source_target_pairs={{0,8},{8,0},{1,9},{9,1},{2,10},{10,2},{3,11},{11,3},{4,12},{12,4},... | collective-permute-start | bytes 3932168 | tf_op jit(solution)/shard_map/ppermute | solution.py:312
  120.4 20.8 %collective-permute-start.12 = (bf16[64,2048]{1,0:T(8,128)(2,1)S(1)}, bf16[64,2048]{1,0:T(8,128)(2,1)S(1)}, u32[]{:S(2)}, u32[]{:S(2)}) collective-permute-start(bf16[64,2048]{1,0:T(8,128)(2,1)S(1)} %shard_map.89.near_ref), channel_id=1, source_target_pairs={{0,1},{1,0},{2,3},{3,2},{4,5},{5,4},{6,7},{7,6},{8,9},{9,8},{10,11... | collective-permute-start | bytes 786440 | tf_op jit(solution)/shard_map/ppermute | solution.py:313
  143.5 17.4 %collective-permute-start.14 = (bf16[64,2048]{1,0:T(8,128)(2,1)S(1)}, bf16[64,2048]{1,0:T(8,128)(2,1)S(1)}, u32[]{:S(2)}, u32[]{:S(2)}) collective-permute-start(bf16[64,2048]{1,0:T(8,128)(2,1)S(1)} %get-tuple-element.24), channel_id=1, source_target_pairs={{0,1},{1,0},{2,3},{3,2},{4,5},{5,4},{6,7},{7,6},{8,9},{9,8},{10,11... | collective-permute-start | bytes 786440 | tf_op jit(solution)/shard_map/ppermute | solution.py:324

commit v8 on v7

--- a/solution.py
+++ b/solution.py
@@ -216,10 +216,10 @@
             left += block
 
 
-def call(kernel, outs, args, scratch=(), flops=0, far=((), ())):
+def call(kernel, outs, args, scratch=(), flops=0, far=((), (), ())):
     moved = sum(a.size * a.dtype.itemsize for a in (*args, *outs))
     args = [
-        pltpu.with_memory_space_constraint(a, pltpu.HBM) if i in far[0] else a
+        pltpu.with_memory_space_constraint(a, pltpu.HBM) if i in far[0] and i not in far[2] else a
         for i, a in enumerate(args)
     ]
     outs = [pltpu.HBM(a.shape, a.dtype) if i in far[1] else a for i, a in enumerate(outs)]
@@ -240,7 +240,7 @@
 def stack(place, *blocks):
     out = jax.ShapeDtypeStruct((len(blocks), *blocks[0].shape), blocks[0].dtype)
     sems = [pltpu.SemaphoreType.DMA((len(blocks),))]
-    return call(stack_kernel, [out], [place, *blocks], sems, far=((), (0,)))[0]
+    return call(stack_kernel, [out], [place, *blocks], sems, far=((), (0,), ()))[0]
 
 
 def on_device(
@@ -271,22 +271,21 @@
     )
     rt = after(by_zl[:, :, s1:], own)
 
-    up = {1: lax.ppermute(own, "y", FORTH)}
-    down = {1: lax.ppermute(own, "y", BACK)}
-    rt = gather_blocks(rt, "x", X)
-    up[2] = lax.ppermute(up[1], "y", FORTH)
-    down[2] = lax.ppermute(down[1], "y", BACK)
+    both = lax.optimization_barrier
+    up, down = both((lax.ppermute(own, "y", FORTH), lax.ppermute(own, "y", BACK)))
+    first = (up, down)
+    rt = gather_blocks(after(rt, up, down), "x", X)
+    up, down = both((lax.ppermute(up, "y", FORTH), lax.ppermute(down, "y", BACK)))
+    early = stack(place, own, *first, up, down)
+    early_far = lax.ppermute(early, "core", SWAP)
+    up, down = lax.ppermute(up, "y", FORTH), lax.ppermute(down, "y", BACK)
+    up, down, rt, early_far = both((up, down, rt, early_far))
+    last = lax.ppermute(up, "y", FORTH)
     rwidth = block * sum(X - q for q in range(ZL))
-    rt = after(rt, up[2], down[2])
     rt, = call(pack_kernel, [shape((Y, rt.shape[2], rwidth), BF)], [place, rt])
-    early = stack(place, own, up[1], down[1], up[2], down[2])
-    early_far = lax.ppermute(early, "core", SWAP)
-    up[3] = lax.ppermute(up[2], "y", FORTH)
-    down[3] = lax.ppermute(down[2], "y", BACK)
-    up[4] = lax.ppermute(up[3], "y", FORTH)
-    late = stack(place, up[3], down[3], up[4])
+    late = stack(place, up, down, last)
     late_far = lax.ppermute(late, "core", SWAP)
-    rmine = lax.all_to_all(after(rt, up[3], down[3]), "y", 0, 0, tiled=True)
+    rmine = lax.all_to_all(after(rt, late), "y", 0, 0, tiled=True)
 
     weights = [early, early_far, late, late_far]
     scratch = [pltpu.VMEM((s1, s1), BF), pltpu.VMEM((k, s1), BF)]
@@ -302,7 +301,7 @@
             pltpu.VMEM((n, k), BF), pltpu.VMEM((n, s0), BF), pltpu.SemaphoreType.DMA((7,)),
         ],
         flops,
-        ((1, 2, 3, 4, 5, 6), (X,)),
+        ((1, 2, 3, 4, 5, 6), (X,), (4,)),
     )
     parts = [
         lax.ppermute(blocks[i], "x", [(j, (j + i) % X) for j in range(X)]) for i in (1, 3, 2)
@@ -330,7 +329,7 @@
         [place, x_all, solved, *weights, idx],
         [*scratch, pltpu.VMEM((n, k), F32), pltpu.SemaphoreType.DMA((5,))],
         flops,
-        ((2, 3, 4, 5, 6), ()),
+        ((2, 3, 4, 5, 6), (), (6,)),
     )
     return (child_out[None], root_out)
 

time: 188 us -> 178 us (0.947)
  the two profiles are of different devices: /device:TPU:192 before, /device:TPU:64 now
where the time goes in v8:
time: 178 us; the launch traced here: 177 us
  starting transfers between devices  58.2 us (33%)
  waiting for transfers between devices  52.1 us (29%)
  blocking collectives  44.4 us (25%)
  Pallas kernels  19.4 us (11%)
    all_to_all x3, blocking collectives, gather_blocks(): lax.all_to_all(jnp.broadcast_to(x[None], (length, *x.shape)), axis, 0, 0,...  44.4 us
    pallas_call x7, Pallas kernels, call(): pl.pallas_call(kernel, out_shape=outs, in_specs=[pl.BlockSpec(memory_spac...  19.4 us
    ppermute x1, waiting for transfers between devices, on_device(): far = lax.ppermute(near, 'zh', SWAP)  12.8 us
    ppermute x3, waiting for transfers between devices, on_device(): lax.ppermute(blocks[i], 'x', [(j, (j + i) % X) for j in range(X)])  9.29 us
    ppermute x1, waiting for transfers between devices, on_device(): x_t = x_part + lax.ppermute(x_sent, 'zh', SWAP).astype(F32)  9.12 us
    ppermute x3, starting transfers between devices, on_device(): lax.ppermute(blocks[i], 'x', [(j, (j + i) % X) for j in range(X)])  8.97 us
    ppermute x1, starting transfers between devices, on_device(): far = lax.ppermute(near, 'zh', SWAP)  8.22 us
    ppermute x2, starting transfers between devices, on_device(): up, down = (lax.ppermute(up, 'y', FORTH), lax.ppermute(down, 'y', BACK))  7.52 us
  transfers between devices with their start and end apart: 16, of which 11 were waited for; matrix products, arithmetic and copies ran while one was open for 0% of the time, Pallas kernels for 5%

profile of v8, /device:TPU:64, one launch (start us, length us, event | category | flops | bytes accessed | tf_op | source)
XLA Modules:
  0.0 177.2 jit_solution(17881814731526934127)
XLA Ops:
  1.5 15.4 %all_to_all.20 = bf16[4,32,1280]{2,1,0:T(8,128)(2,1)S(1)} all-to-all(bf16[4,32,1280]{2,1,0:T(8,128)(2,1)S(1)} %broadcast_in_dim.8), channel_id=1, replica_groups=mesh['zl'=4,'y'=8,'core'=2,'x'=4,'zh'=2] {'zl'}, dimensions={0} | all-to-all | bytes 655360 | tf_op jit(solution)/shard_map/all_to_all | solution.py:20
  16.9 5.4 %collective-permute-start.1 = (bf16[16,6656]{1,0:T(8,128)(2,1)S(1)}, bf16[16,6656]{1,0:T(8,128)(2,1)S(1)}, u32[]{:S(2)}, u32[]{:S(2)}) collective-permute-start(bf16[16,6656]{1,0:T(8,128)(2,1)S(1)} %constant_dynamic-update-slice_fusion.refs_0_), channel_id=1, source_target_pairs={{0,112},{16,0},{32,16},{48,32},{64,48},{80,64},{96,80},{112,96},{1... | collective-permute-start | bytes 638984 | tf_op jit(solution)/shard_map/ppermute | solution.py:275
  22.3 1.9 %collective-permute-start = (bf16[16,6656]{1,0:T(8,128)(2,1)S(1)}, bf16[16,6656]{1,0:T(8,128)(2,1)S(1)}, u32[]{:S(2)}, u32[]{:S(2)}) collective-permute-start(bf16[16,6656]{1,0:T(8,128)(2,1)S(1)} %constant_dynamic-update-slice_fusion.refs_0_), channel_id=1, source_target_pairs={{0,16},{16,32},{32,48},{48,64},{64,80},{80,96},{96,112},{112,0},{1... | collective-permute-start | bytes 638984 | tf_op jit(solution)/shard_map/ppermute | solution.py:275
  25.6 5.6 %collective-permute-done.refs_1_ = bf16[16,6656]{1,0:T(8,128)(2,1)S(1)} collective-permute-done((bf16[16,6656]{1,0:T(8,128)(2,1)S(1)}, bf16[16,6656]{1,0:T(8,128)(2,1)S(1)}, u32[]{:S(2)}, u32[]{:S(2)}) %collective-permute-start) | collective-permute-done | bytes 213024 | tf_op jit(solution)/shard_map/ppermute | solution.py:275
  31.2 1.9 %collective-permute-start.2 = (bf16[16,6656]{1,0:T(8,128)(2,1)S(1)}, bf16[16,6656]{1,0:T(8,128)(2,1)S(1)}, u32[]{:S(2)}, u32[]{:S(2)}) collective-permute-start(bf16[16,6656]{1,0:T(8,128)(2,1)S(1)} %collective-permute-done.refs_1_), channel_id=1, source_target_pairs={{0,16},{16,32},{32,48},{48,64},{64,80},{80,96},{96,112},{112,0},{1... | collective-permute-start | bytes 638984 | tf_op jit(solution)/shard_map/ppermute | solution.py:278
  33.1 5.1 %collective-permute-start.3 = (bf16[16,6656]{1,0:T(8,128)(2,1)S(1)}, bf16[16,6656]{1,0:T(8,128)(2,1)S(1)}, u32[]{:S(2)}, u32[]{:S(2)}) collective-permute-start(bf16[16,6656]{1,0:T(8,128)(2,1)S(1)} %collective-permute-done.1.refs_2_), channel_id=1, source_target_pairs={{0,112},{16,0},{32,16},{48,32},{64,48},{80,64},{96,80},{112,96},{1... | collective-permute-start | bytes 638984 | tf_op jit(solution)/shard_map/ppermute | solution.py:278
  38.6 1.6 collective-permute-done.2.refs_3_
  43.2 1.9 %collective-permute-start.6 = (bf16[5,16,6656]{2,1,0:T(8,128)(2,1)}, bf16[5,16,6656]{2,1,0:T(8,128)(2,1)S(1)}, u32[]{:S(2)}, u32[]{:S(2)}) collective-permute-start(bf16[5,16,6656]{2,1,0:T(8,128)(2,1)} %shard_map.86.early_in_ref), channel_id=1, source_target_pairs={{0,8},{8,0},{1,9},{9,1},{2,10},{10,2},{3,11},{11,3},{4,12},{12,4},... | collective-permute-start | bytes 3194888 | tf_op jit(solution)/shard_map/ppermute | solution.py:280
  45.1 1.9 %collective-permute-start.4 = (bf16[16,6656]{1,0:T(8,128)(2,1)S(1)}, bf16[16,6656]{1,0:T(8,128)(2,1)S(1)}, u32[]{:S(2)}, u32[]{:S(2)}) collective-permute-start(bf16[16,6656]{1,0:T(8,128)(2,1)S(1)} %collective-permute-done.2.refs_3_), channel_id=1, source_target_pairs={{0,16},{16,32},{32,48},{48,64},{64,80},{80,96},{96,112},{112,0},{1... | collective-permute-start | bytes 638984 | tf_op jit(solution)/shard_map/ppermute | solution.py:281
  47.1 5.6 %collective-permute-start.5 = (bf16[16,6656]{1,0:T(8,128)(2,1)S(1)}, bf16[16,6656]{1,0:T(8,128)(2,1)S(1)}, u32[]{:S(2)}, u32[]{:S(2)}) collective-permute-start(bf16[16,6656]{1,0:T(8,128)(2,1)S(1)} %collective-permute-done.3.refs_4_), channel_id=1, source_target_pairs={{0,112},{16,0},{32,16},{48,32},{64,48},{80,64},{96,80},{112,96},{1... | collective-permute-start | bytes 638984 | tf_op jit(solution)/shard_map/ppermute | solution.py:281
  52.7 11.1 %all_to_all.21.r_ref = bf16[4,4,32,256]{3,2,1,0:T(8,128)(2,1)S(1)} all-to-all(bf16[4,4,32,256]{3,2,1,0:T(8,128)(2,1)S(1)} %broadcast_in_dim.9), channel_id=1, replica_groups=mesh['zl'=4,'y'=8,'core'=2,'x'=4,'zh'=2] {'x'}, dimensions={0} | all-to-all | bytes 524288 | tf_op jit(solution)/shard_map/all_to_all | solution.py:20
  63.9 1.9 %collective-permute-start.7 = (bf16[16,6656]{1,0:T(8,128)(2,1)S(1)}, bf16[16,6656]{1,0:T(8,128)(2,1)S(1)}, u32[]{:S(2)}, u32[]{:S(2)}) collective-permute-start(bf16[16,6656]{1,0:T(8,128)(2,1)S(1)} %collective-permute-done.4.refs_0_), channel_id=1, source_target_pairs={{0,16},{16,32},{32,48},{48,64},{64,80},{80,96},{96,112},{112,0},{1... | collective-permute-start | bytes 638984 | tf_op jit(solution)/shard_map/ppermute | solution.py:283
  65.8 1.7 shard_map.90
  67.5 5.7 %collective-permute-done.7.refs_2_ = bf16[16,6656]{1,0:T(8,128)(2,1)S(1)} collective-permute-done((bf16[16,6656]{1,0:T(8,128)(2,1)S(1)}, bf16[16,6656]{1,0:T(8,128)(2,1)S(1)}, u32[]{:S(2)}, u32[]{:S(2)}) %collective-permute-start.7) | collective-permute-done | bytes 213024 | tf_op jit(solution)/shard_map/ppermute | solution.py:283
  74.6 4.2 %all-to-all-start.2 = ((bf16[8,32,2560]{2,1,0:T(8,128)(2,1)}), bf16[8,32,2560]{2,1,0:T(8,128)(2,1)S(1)}, u32[]{:S(2)}, u32[]{:S(2)}) async-start(bf16[8,32,2560]{2,1,0:T(8,128)(2,1)} %shard_map.90), calls=%async_computation.2 | async-start | bytes 2621440 | tf_op jit(solution)/shard_map/all_to_all | solution.py:288
  78.9 1.9 %collective-permute-start.8 = (bf16[3,16,6656]{2,1,0:T(8,128)(2,1)S(1)}, bf16[3,16,6656]{2,1,0:T(8,128)(2,1)S(1)}, u32[]{:S(2)}, u32[]{:S(2)}) collective-permute-start(bf16[3,16,6656]{2,1,0:T(8,128)(2,1)S(1)} %copy-done), channel_id=1, source_target_pairs={{0,8},{8,0},{1,9},{9,1},{2,10},{10,2},{3,11},{11,3},{4,12},{12,4},... | collective-permute-start | bytes 1916936 | tf_op jit(solution)/shard_map/ppermute | solution.py:287
  81.0 1.8 %collective-permute-done.8.late_far_in_ref = bf16[3,16,6656]{2,1,0:T(8,128)(2,1)S(1)} collective-permute-done((bf16[3,16,6656]{2,1,0:T(8,128)(2,1)S(1)}, bf16[3,16,6656]{2,1,0:T(8,128)(2,1)S(1)}, u32[]{:S(2)}, u32[]{:S(2)}) %collective-permute-start.8) | collective-permute-done | bytes 639008 | tf_op jit(solution)/shard_map/ppermute | solution.py:287
  82.8 5.7 %shard_map.88 = (bf16[64,2048]{1,0:T(8,128)(2,1)S(1)}, bf16[64,2048]{1,0:T(8,128)(2,1)S(1)}, bf16[64,2048]{1,0:T(8,128)(2,1)S(1)}, bf16[64,2048]{1,0:T(8,128)(2,1)S(1)}, f32[256,1024]{1,0:T(8,128)}) custom-call(s32[13]{0:T(128)S(1)} %concatenate.12.place_ref, bf16[5,16,6656]{2,1,0:T(8,128)(2,1)} %shard_map.86.early_in_ref, bf16[5,16,6656]{2,1,0:T(8,128)(2,1)} %copy-done.2, ...), custom_call_target="tpu_custom_call" | custom-call | flops 2147483648 | bytes 6819892 | tf_op jit(solution)/shard_map/pallas_call | solution.py:228
  88.6 2.5 %collective-permute-start.9 = (bf16[64,2048]{1,0:T(8,128)(2,1)S(1)}, bf16[64,2048]{1,0:T(8,128)(2,1)S(1)}, u32[]{:S(2)}, u32[]{:S(2)}) collective-permute-start(bf16[64,2048]{1,0:T(8,128)(2,1)S(1)} %get-tuple-element.33), channel_id=1, source_target_pairs={{0,2},{2,4},{4,6},{6,0},{1,3},{3,5},{5,7},{7,1},{8,10},{10,12},{12... | collective-permute-start | bytes 786440 | tf_op jit(solution)/shard_map/ppermute | solution.py:307
  91.1 4.6 %collective-permute-start.10 = (bf16[64,2048]{1,0:T(8,128)(2,1)S(1)}, bf16[64,2048]{1,0:T(8,128)(2,1)S(1)}, u32[]{:S(2)}, u32[]{:S(2)}) collective-permute-start(bf16[64,2048]{1,0:T(8,128)(2,1)S(1)} %get-tuple-element.34), channel_id=1, source_target_pairs={{0,6},{2,0},{4,2},{6,4},{1,7},{3,1},{5,3},{7,5},{8,14},{10,8},{12,... | collective-permute-start | bytes 786440 | tf_op jit(solution)/shard_map/ppermute | solution.py:307
  95.7 1.9 %collective-permute-start.11 = (bf16[64,2048]{1,0:T(8,128)(2,1)S(1)}, bf16[64,2048]{1,0:T(8,128)(2,1)S(1)}, u32[]{:S(2)}, u32[]{:S(2)}) collective-permute-start(bf16[64,2048]{1,0:T(8,128)(2,1)S(1)} %get-tuple-element.35), channel_id=1, source_target_pairs={{0,4},{2,6},{4,0},{6,2},{1,5},{3,7},{5,1},{7,3},{8,12},{10,14},{12... | collective-permute-start | bytes 786440 | tf_op jit(solution)/shard_map/ppermute | solution.py:307
  97.6 2.5 %collective-permute-done.9.b_ref = bf16[64,2048]{1,0:T(8,128)(2,1)S(1)} collective-permute-done((bf16[64,2048]{1,0:T(8,128)(2,1)S(1)}, bf16[64,2048]{1,0:T(8,128)(2,1)S(1)}, u32[]{:S(2)}, u32[]{:S(2)}) %collective-permute-start.9) | collective-permute-done | bytes 262176 | tf_op jit(solution)/shard_map/ppermute | solution.py:307
  100.0 6.8 %collective-permute-done.10.c_ref = bf16[64,2048]{1,0:T(8,128)(2,1)S(1)} collective-permute-done((bf16[64,2048]{1,0:T(8,128)(2,1)S(1)}, bf16[64,2048]{1,0:T(8,128)(2,1)S(1)}, u32[]{:S(2)}, u32[]{:S(2)}) %collective-permute-start.10) | collective-permute-done | bytes 262176 | tf_op jit(solution)/shard_map/ppermute | solution.py:307
  107.6 4.0 %all-to-all-done.2.mine_ref = bf16[8,32,2560]{2,1,0:T(8,128)(2,1)S(1)} async-done(((bf16[8,32,2560]{2,1,0:T(8,128)(2,1)}), bf16[8,32,2560]{2,1,0:T(8,128)(2,1)S(1)}, u32[]{:S(2)}, u32[]{:S(2)}) %all-to-all-start.2) | async-done | bytes 1310752 | tf_op jit(solution)/shard_map/all_to_all | solution.py:288
  111.5 1.9 %collective-permute-start.13 = (bf16[8,32,2560]{2,1,0:T(8,128)(2,1)S(1)}, bf16[8,32,2560]{2,1,0:T(8,128)(2,1)S(1)}, u32[]{:S(2)}, u32[]{:S(2)}) collective-permute-start(bf16[8,32,2560]{2,1,0:T(8,128)(2,1)S(1)} %all-to-all-done.2.mine_ref), channel_id=1, source_target_pairs={{0,8},{8,0},{1,9},{9,1},{2,10},{10,2},{3,11},{11,3},{4,12},{12,4},... | collective-permute-start | bytes 3932168 | tf_op jit(solution)/shard_map/ppermute | solution.py:311
  113.5 8.2 %collective-permute-start.12 = (bf16[64,2048]{1,0:T(8,128)(2,1)S(1)}, bf16[64,2048]{1,0:T(8,128)(2,1)S(1)}, u32[]{:S(2)}, u32[]{:S(2)}) collective-permute-start(bf16[64,2048]{1,0:T(8,128)(2,1)S(1)} %shard_map.89.near_ref), channel_id=1, source_target_pairs={{0,1},{1,0},{2,3},{3,2},{4,5},{5,4},{6,7},{7,6},{8,9},{9,8},{10,11... | collective-permute-start | bytes 786440 | tf_op jit(solution)/shard_map/ppermute | solution.py:312
  121.7 12.8 %collective-permute-done.12.far_ref = bf16[64,2048]{1,0:T(8,128)(2,1)S(1)} collective-permute-done((bf16[64,2048]{1,0:T(8,128)(2,1)S(1)}, bf16[64,2048]{1,0:T(8,128)(2,1)S(1)}, u32[]{:S(2)}, u32[]{:S(2)}) %collective-permute-start.12) | collective-permute-done | bytes 262176 | tf_op jit(solution)/shard_map/ppermute | solution.py:312
  134.5 2.2 %shard_map.91 = (f32[64,2048]{1,0:T(8,128)S(1)}, bf16[64,2048]{1,0:T(8,128)(2,1)S(1)}) custom-call(s32[13]{0:T(128)S(1)} %concatenate.12.place_ref, bf16[64,2048]{1,0:T(8,128)(2,1)S(1)} %shard_map.89.near_ref, bf16[64,2048]{1,0:T(8,128)(2,1)S(1)} %collective-permute-done.12.far_ref, bf16[8,32,2560]{2,1,0:T(8,128)(2,1)S(1)} %all-to-all-done.2.mine_ref, ...), custom_call_target="tpu_custom_call" | custom-call | flops 335544320 | bytes 3932212 | tf_op jit(solution)/shard_map/pallas_call | solution.py:228
  136.7 7.3 %collective-permute-start.14 = (bf16[64,2048]{1,0:T(8,128)(2,1)S(1)}, bf16[64,2048]{1,0:T(8,128)(2,1)S(1)}, u32[]{:S(2)}, u32[]{:S(2)}) collective-permute-start(bf16[64,2048]{1,0:T(8,128)(2,1)S(1)} %get-tuple-element.40), channel_id=1, source_target_pairs={{0,1},{1,0},{2,3},{3,2},{4,5},{5,4},{6,7},{7,6},{8,9},{9,8},{10,11... | collective-permute-start | bytes 786440 | tf_op jit(solution)/shard_map/ppermute | solution.py:323
  144.0 9.1 %collective-permute-done.14 = bf16[64,2048]{1,0:T(8,128)(2,1)S(1)} collective-permute-done((bf16[64,2048]{1,0:T(8,128)(2,1)S(1)}, bf16[64,2048]{1,0:T(8,128)(2,1)S(1)}, u32[]{:S(2)}, u32[]{:S(2)}) %collective-permute-start.14) | collective-permute-done | bytes 262176 | tf_op jit(solution)/shard_map/ppermute | solution.py:323
  153.3 17.9 %all_to_all.22 = bf16[4,64,2048]{2,1,0:T(8,128)(2,1)S(1)} all-to-all(bf16[4,64,2048]{2,1,0:T(8,128)(2,1)S(1)} %broadcast_in_dim.10), channel_id=1, replica_groups=mesh['zl'=4,'y'=8,'core'=2,'x'=4,'zh'=2] {'x'}, dimensions={0} | all-to-all | bytes 2097152 | tf_op jit(solution)/shard_map/all_to_all | solution.py:20
  171.2 6.1 %shard_map.92 = (f32[1024,256]{1,0:T(8,128)}, f32[256,256]{1,0:T(8,128)}) custom-call(s32[13]{0:T(128)S(1)} %concatenate.12.place_ref, bf16[256,2048]{1,0:T(8,128)(2,1)S(1)} %bitcast.44, f32[256,1024]{1,0:T(8,128)} %get-tuple-element.41.in_ref, bf16[5,16,6656]{2,1,0:T(8,128)(2,1)} %shard_map.86.early_in_ref, bf16[5,16,6656]{2,1,0:T(8,128)(2,1)} %copy-done.2, ...), custom_call_target="tpu_custom_call" | custom-call | flops 2147483648 | bytes 6819892 | tf_op jit(solution)/shard_map/pallas_call | solution.py:228
  (34 shorter events, 7.4 us)
Async XLA Ops:
  0.6 37.7 %copy-start.1 = (s32[1,1024]{1,0:T(1,128)S(1)}, s32[1,1024]{1,0:T(1,128)}, u32[]{:S(2)}) copy-start(s32[1,1024]{1,0:T(1,128)} %param.13) | copy-start | bytes 12292
  16.9 8.7 %collective-permute-start.1 = (bf16[16,6656]{1,0:T(8,128)(2,1)S(1)}, bf16[16,6656]{1,0:T(8,128)(2,1)S(1)}, u32[]{:S(2)}, u32[]{:S(2)}) collective-permute-start(bf16[16,6656]{1,0:T(8,128)(2,1)S(1)} %constant_dynamic-update-slice_fusion.refs_0_), channel_id=1, source_target_pairs={{0,112},{16,0},{32,16},{48,32},{64,48},{80,64},{96,80},{112,96},{1... | collective-permute-start | bytes 638984 | tf_op jit(solution)/shard_map/ppermute | solution.py:275
  22.3 8.9 %collective-permute-start = (bf16[16,6656]{1,0:T(8,128)(2,1)S(1)}, bf16[16,6656]{1,0:T(8,128)(2,1)S(1)}, u32[]{:S(2)}, u32[]{:S(2)}) collective-permute-start(bf16[16,6656]{1,0:T(8,128)(2,1)S(1)} %constant_dynamic-update-slice_fusion.refs_0_), channel_id=1, source_target_pairs={{0,16},{16,32},{32,48},{48,64},{64,80},{80,96},{96,112},{112,0},{1... | collective-permute-start | bytes 638984 | tf_op jit(solution)/shard_map/ppermute | solution.py:275
  31.2 8.9 %collective-permute-start.2 = (bf16[16,6656]{1,0:T(8,128)(2,1)S(1)}, bf16[16,6656]{1,0:T(8,128)(2,1)S(1)}, u32[]{:S(2)}, u32[]{:S(2)}) collective-permute-start(bf16[16,6656]{1,0:T(8,128)(2,1)S(1)} %collective-permute-done.refs_1_), channel_id=1, source_target_pairs={{0,16},{16,32},{32,48},{48,64},{64,80},{80,96},{96,112},{112,0},{1... | collective-permute-start | bytes 638984 | tf_op jit(solution)/shard_map/ppermute | solution.py:278
  33.1 8.5 %collective-permute-start.3 = (bf16[16,6656]{1,0:T(8,128)(2,1)S(1)}, bf16[16,6656]{1,0:T(8,128)(2,1)S(1)}, u32[]{:S(2)}, u32[]{:S(2)}) collective-permute-start(bf16[16,6656]{1,0:T(8,128)(2,1)S(1)} %collective-permute-done.1.refs_2_), channel_id=1, source_target_pairs={{0,112},{16,0},{32,16},{48,32},{64,48},{80,64},{96,80},{112,96},{1... | collective-permute-start | bytes 638984 | tf_op jit(solution)/shard_map/ppermute | solution.py:278
  43.2 20.7 %collective-permute-start.6 = (bf16[5,16,6656]{2,1,0:T(8,128)(2,1)}, bf16[5,16,6656]{2,1,0:T(8,128)(2,1)S(1)}, u32[]{:S(2)}, u32[]{:S(2)}) collective-permute-start(bf16[5,16,6656]{2,1,0:T(8,128)(2,1)} %shard_map.86.early_in_ref), channel_id=1, source_target_pairs={{0,8},{8,0},{1,9},{9,1},{2,10},{10,2},{3,11},{11,3},{4,12},{12,4},... | collective-permute-start | bytes 3194888 | tf_op jit(solution)/shard_map/ppermute | solution.py:280
  45.1 18.7 %collective-permute-start.4 = (bf16[16,6656]{1,0:T(8,128)(2,1)S(1)}, bf16[16,6656]{1,0:T(8,128)(2,1)S(1)}, u32[]{:S(2)}, u32[]{:S(2)}) collective-permute-start(bf16[16,6656]{1,0:T(8,128)(2,1)S(1)} %collective-permute-done.2.refs_3_), channel_id=1, source_target_pairs={{0,16},{16,32},{32,48},{48,64},{64,80},{80,96},{96,112},{112,0},{1... | collective-permute-start | bytes 638984 | tf_op jit(solution)/shard_map/ppermute | solution.py:281
  47.1 16.8 %collective-permute-start.5 = (bf16[16,6656]{1,0:T(8,128)(2,1)S(1)}, bf16[16,6656]{1,0:T(8,128)(2,1)S(1)}, u32[]{:S(2)}, u32[]{:S(2)}) collective-permute-start(bf16[16,6656]{1,0:T(8,128)(2,1)S(1)} %collective-permute-done.3.refs_4_), channel_id=1, source_target_pairs={{0,112},{16,0},{32,16},{48,32},{64,48},{80,64},{96,80},{112,96},{1... | collective-permute-start | bytes 638984 | tf_op jit(solution)/shard_map/ppermute | solution.py:281
  63.9 10.8 %copy-start.2 = (bf16[5,16,6656]{2,1,0:T(8,128)(2,1)}, bf16[5,16,6656]{2,1,0:T(8,128)(2,1)S(1)}, u32[]{:S(2)}) copy-start(bf16[5,16,6656]{2,1,0:T(8,128)(2,1)S(1)} %collective-permute-done.6.early_far_in_ref) | copy-start | bytes 3194884
  63.9 9.3 %collective-permute-start.7 = (bf16[16,6656]{1,0:T(8,128)(2,1)S(1)}, bf16[16,6656]{1,0:T(8,128)(2,1)S(1)}, u32[]{:S(2)}, u32[]{:S(2)}) collective-permute-start(bf16[16,6656]{1,0:T(8,128)(2,1)S(1)} %collective-permute-done.4.refs_0_), channel_id=1, source_target_pairs={{0,16},{16,32},{32,48},{48,64},{64,80},{80,96},{96,112},{112,0},{1... | collective-permute-start | bytes 638984 | tf_op jit(solution)/shard_map/ppermute | solution.py:283
  74.6 4.2 %copy-start = (bf16[3,16,6656]{2,1,0:T(8,128)(2,1)S(1)}, bf16[3,16,6656]{2,1,0:T(8,128)(2,1)}, u32[]{:S(2)}) copy-start(bf16[3,16,6656]{2,1,0:T(8,128)(2,1)} %shard_map.87.late_in_ref) | copy-start | bytes 1916932
  74.6 36.9 %all-to-all-start.2 = ((bf16[8,32,2560]{2,1,0:T(8,128)(2,1)}), bf16[8,32,2560]{2,1,0:T(8,128)(2,1)S(1)}, u32[]{:S(2)}, u32[]{:S(2)}) async-start(bf16[8,32,2560]{2,1,0:T(8,128)(2,1)} %shard_map.90), calls=%async_computation.2 | async-start | bytes 2621440 | tf_op jit(solution)/shard_map/all_to_all | solution.py:288
  78.9 4.0 %collective-permute-start.8 = (bf16[3,16,6656]{2,1,0:T(8,128)(2,1)S(1)}, bf16[3,16,6656]{2,1,0:T(8,128)(2,1)S(1)}, u32[]{:S(2)}, u32[]{:S(2)}) collective-permute-start(bf16[3,16,6656]{2,1,0:T(8,128)(2,1)S(1)} %copy-done), channel_id=1, source_target_pairs={{0,8},{8,0},{1,9},{9,1},{2,10},{10,2},{3,11},{11,3},{4,12},{12,4},... | collective-permute-start | bytes 1916936 | tf_op jit(solution)/shard_map/ppermute | solution.py:287
  88.6 11.5 %collective-permute-start.9 = (bf16[64,2048]{1,0:T(8,128)(2,1)S(1)}, bf16[64,2048]{1,0:T(8,128)(2,1)S(1)}, u32[]{:S(2)}, u32[]{:S(2)}) collective-permute-start(bf16[64,2048]{1,0:T(8,128)(2,1)S(1)} %get-tuple-element.33), channel_id=1, source_target_pairs={{0,2},{2,4},{4,6},{6,0},{1,3},{3,5},{5,7},{7,1},{8,10},{10,12},{12... | collective-permute-start | bytes 786440 | tf_op jit(solution)/shard_map/ppermute | solution.py:307
  91.1 15.8 %collective-permute-start.10 = (bf16[64,2048]{1,0:T(8,128)(2,1)S(1)}, bf16[64,2048]{1,0:T(8,128)(2,1)S(1)}, u32[]{:S(2)}, u32[]{:S(2)}) collective-permute-start(bf16[64,2048]{1,0:T(8,128)(2,1)S(1)} %get-tuple-element.34), channel_id=1, source_target_pairs={{0,6},{2,0},{4,2},{6,4},{1,7},{3,1},{5,3},{7,5},{8,14},{10,8},{12,... | collective-permute-start | bytes 786440 | tf_op jit(solution)/shard_map/ppermute | solution.py:307
  95.7 11.2 %collective-permute-start.11 = (bf16[64,2048]{1,0:T(8,128)(2,1)S(1)}, bf16[64,2048]{1,0:T(8,128)(2,1)S(1)}, u32[]{:S(2)}, u32[]{:S(2)}) collective-permute-start(bf16[64,2048]{1,0:T(8,128)(2,1)S(1)} %get-tuple-element.35), channel_id=1, source_target_pairs={{0,4},{2,6},{4,0},{6,2},{1,5},{3,7},{5,1},{7,3},{8,12},{10,14},{12... | collective-permute-start | bytes 786440 | tf_op jit(solution)/shard_map/ppermute | solution.py:307
  111.5 23.0 %collective-permute-start.13 = (bf16[8,32,2560]{2,1,0:T(8,128)(2,1)S(1)}, bf16[8,32,2560]{2,1,0:T(8,128)(2,1)S(1)}, u32[]{:S(2)}, u32[]{:S(2)}) collective-permute-start(bf16[8,32,2560]{2,1,0:T(8,128)(2,1)S(1)} %all-to-all-done.2.mine_ref), channel_id=1, source_target_pairs={{0,8},{8,0},{1,9},{9,1},{2,10},{10,2},{3,11},{11,3},{4,12},{12,4},... | collective-permute-start | bytes 3932168 | tf_op jit(solution)/shard_map/ppermute | solution.py:311
  113.5 21.1 %collective-permute-start.12 = (bf16[64,2048]{1,0:T(8,128)(2,1)S(1)}, bf16[64,2048]{1,0:T(8,128)(2,1)S(1)}, u32[]{:S(2)}, u32[]{:S(2)}) collective-permute-start(bf16[64,2048]{1,0:T(8,128)(2,1)S(1)} %shard_map.89.near_ref), channel_id=1, source_target_pairs={{0,1},{1,0},{2,3},{3,2},{4,5},{5,4},{6,7},{7,6},{8,9},{9,8},{10,11... | collective-permute-start | bytes 786440 | tf_op jit(solution)/shard_map/ppermute | solution.py:312
  136.7 16.4 %collective-permute-start.14 = (bf16[64,2048]{1,0:T(8,128)(2,1)S(1)}, bf16[64,2048]{1,0:T(8,128)(2,1)S(1)}, u32[]{:S(2)}, u32[]{:S(2)}) collective-permute-start(bf16[64,2048]{1,0:T(8,128)(2,1)S(1)} %get-tuple-element.40), channel_id=1, source_target_pairs={{0,1},{1,0},{2,3},{3,2},{4,5},{5,4},{6,7},{7,6},{8,9},{9,8},{10,11... | collective-permute-start | bytes 786440 | tf_op jit(solution)/shard_map/ppermute | solution.py:323

commit v9 on v7

--- a/solution.py
+++ b/solution.py
@@ -123,17 +123,6 @@
     store.wait()
 
 
-def stack_kernel(place_ref, *refs):
-    *blocks, out_ref, sem = refs
-    copies = [
-        pltpu.make_async_copy(ref, out_ref.at[i], sem.at[i]) for i, ref in enumerate(blocks)
-    ]
-    for copy in copies:
-        copy.start()
-    for copy in copies:
-        copy.wait()
-
-
 def sum_kernel(place_ref, a_ref, b_ref, c_ref, d_ref, out_ref):
     total = a_ref[...].astype(F32) + b_ref[...].astype(F32)
     total += c_ref[...].astype(F32) + d_ref[...].astype(F32)
@@ -211,15 +200,14 @@
     left = 0
     for q in range(ZL):
         for x in range(q, X):
-            for y in range(Y):
-                out_ref[y, :, left : left + block] = r_ref[x, q]
+            out_ref[:, left : left + block] = r_ref[x, q]
             left += block
 
 
-def call(kernel, outs, args, scratch=(), flops=0, far=((), ())):
+def call(kernel, outs, args, scratch=(), flops=0, far=((), (), ())):
     moved = sum(a.size * a.dtype.itemsize for a in (*args, *outs))
     args = [
-        pltpu.with_memory_space_constraint(a, pltpu.HBM) if i in far[0] else a
+        pltpu.with_memory_space_constraint(a, pltpu.HBM) if i in far[0] and i not in far[2] else a
         for i, a in enumerate(args)
     ]
     outs = [pltpu.HBM(a.shape, a.dtype) if i in far[1] else a for i, a in enumerate(outs)]
@@ -235,12 +223,6 @@
         cost_estimate=pl.CostEstimate(flops=flops, transcendentals=0, bytes_accessed=moved),
         compiler_params=pltpu.CompilerParams(vmem_limit_bytes=20 << 20),
     )(*args)
-
-
-def stack(place, *blocks):
-    out = jax.ShapeDtypeStruct((len(blocks), *blocks[0].shape), blocks[0].dtype)
-    sems = [pltpu.SemaphoreType.DMA((len(blocks),))]
-    return call(stack_kernel, [out], [place, *blocks], sems, far=((), (0,)))[0]
 
 
 def on_device(
@@ -274,19 +256,18 @@
     up = {1: lax.ppermute(own, "y", FORTH)}
     down = {1: lax.ppermute(own, "y", BACK)}
     rt = gather_blocks(rt, "x", X)
+    rwidth = block * sum(X - q for q in range(ZL))
+    rt, = call(pack_kernel, [shape((rt.shape[2], rwidth), BF)], [place, rt])
     up[2] = lax.ppermute(up[1], "y", FORTH)
     down[2] = lax.ppermute(down[1], "y", BACK)
-    rwidth = block * sum(X - q for q in range(ZL))
-    rt = after(rt, up[2], down[2])
-    rt, = call(pack_kernel, [shape((Y, rt.shape[2], rwidth), BF)], [place, rt])
-    early = stack(place, own, up[1], down[1], up[2], down[2])
+    early = jnp.stack([own, up[1], down[1], up[2], down[2]])
     early_far = lax.ppermute(early, "core", SWAP)
     up[3] = lax.ppermute(up[2], "y", FORTH)
     down[3] = lax.ppermute(down[2], "y", BACK)
     up[4] = lax.ppermute(up[3], "y", FORTH)
-    late = stack(place, up[3], down[3], up[4])
+    late = jnp.stack([up[3], down[3], up[4]])
     late_far = lax.ppermute(late, "core", SWAP)
-    rmine = lax.all_to_all(after(rt, up[3], down[3]), "y", 0, 0, tiled=True)
+    rmine = gather_blocks(after(rt, up[4]), "y", Y)
 
     weights = [early, early_far, late, late_far]
     scratch = [pltpu.VMEM((s1, s1), BF), pltpu.VMEM((k, s1), BF)]
@@ -302,7 +283,7 @@
             pltpu.VMEM((n, k), BF), pltpu.VMEM((n, s0), BF), pltpu.SemaphoreType.DMA((7,)),
         ],
         flops,
-        ((1, 2, 3, 4, 5, 6), (X,)),
+        ((1, 2, 3, 4, 5, 6), (X,), (1, 2, 3, 4)),
     )
     parts = [
         lax.ppermute(blocks[i], "x", [(j, (j + i) % X) for j in range(X)]) for i in (1, 3, 2)
@@ -330,7 +311,7 @@
         [place, x_all, solved, *weights, idx],
         [*scratch, pltpu.VMEM((n, k), F32), pltpu.SemaphoreType.DMA((5,))],
         flops,
-        ((2, 3, 4, 5, 6), ()),
+        ((2, 3, 4, 5, 6), (), (3, 4, 5, 6)),
     )
     return (child_out[None], root_out)
 

time: 188 us -> 180 us (0.957)
  the two profiles are of different devices: /device:TPU:192 before, /device:TPU:1 now
where the time goes in v9:
time: 180 us; the launch traced here: 178 us
  starting transfers between devices  76.3 us (42%)
  waiting for transfers between devices  58.8 us (33%)
  blocking collectives  18.6 us (10%)
  Pallas kernels  14.9 us (8%)
  local copies, waits for them, and re-layouts  6.63 us (4%)
    all_to_all x1, blocking collectives, gather_blocks(): lax.all_to_all(jnp.broadcast_to(x[None], (length, *x.shape)), axis, 0, 0,...  18.6 us
    all_to_all x3, starting transfers between devices, gather_blocks(): lax.all_to_all(jnp.broadcast_to(x[None], (length, *x.shape)), axis, 0, 0,...  15.6 us
    pallas_call x5, Pallas kernels, call(): pl.pallas_call(kernel, out_shape=outs, in_specs=[pl.BlockSpec(memory_spac...  14.9 us
    ppermute x1, waiting for transfers between devices, on_device(): x_t = x_part + lax.ppermute(x_sent, 'zh', SWAP).astype(F32)  14.1 us
    ppermute x1, waiting for transfers between devices, on_device(): far = lax.ppermute(near, 'zh', SWAP)  12.3 us
    ppermute x1, starting transfers between devices, on_device(): early_far = lax.ppermute(early, 'core', SWAP)  10.5 us
    all_to_all x3, waiting for transfers between devices, gather_blocks(): lax.all_to_all(jnp.broadcast_to(x[None], (length, *x.shape)), axis, 0, 0,...  10.1 us
    ppermute x3, waiting for transfers between devices, on_device(): lax.ppermute(blocks[i], 'x', [(j, (j + i) % X) for j in range(X)])  8.59 us
  transfers between devices with their start and end apart: 18, of which 11 were waited for; matrix products, arithmetic and copies ran while one was open for 3% of the time, Pallas kernels for 4%

profile of v9, /device:TPU:1, one launch (start us, length us, event | category | flops | bytes accessed | tf_op | source)
XLA Modules:
  0.0 178.0 jit_solution(15541649900336719255)
XLA Ops:
  2.2 7.8 %all-to-all-start = ((bf16[4,32,1280]{2,1,0:T(8,128)(2,1)}), bf16[4,32,1280]{2,1,0:T(8,128)(2,1)S(1)}, u32[]{:S(2)}, u32[]{:S(2)}) async-start(bf16[4,32,1280]{2,1,0:T(8,128)(2,1)} %broadcast_in_dim.10), calls=%async_computation | async-start | bytes 655360 | tf_op jit(solution)/shard_map/all_to_all | solution.py:20
  10.9 5.3 %all-to-all-done = bf16[4,32,1280]{2,1,0:T(8,128)(2,1)S(1)} async-done(((bf16[4,32,1280]{2,1,0:T(8,128)(2,1)}), bf16[4,32,1280]{2,1,0:T(8,128)(2,1)S(1)}, u32[]{:S(2)}, u32[]{:S(2)}) %all-to-all-start) | async-done | bytes 327712 | tf_op jit(solution)/shard_map/all_to_all | solution.py:20
  16.3 7.5 %collective-permute-start.1 = (bf16[16,6656]{1,0:T(8,128)(2,1)S(1)}, bf16[16,6656]{1,0:T(8,128)(2,1)S(1)}, u32[]{:S(2)}, u32[]{:S(2)}) collective-permute-start(bf16[16,6656]{1,0:T(8,128)(2,1)S(1)} %constant_dynamic-update-slice_fusion), channel_id=1, source_target_pairs={{0,112},{16,0},{32,16},{48,32},{64,48},{80,64},{96,80},{112,96},{1... | collective-permute-start | bytes 638984 | tf_op jit(solution)/shard_map/ppermute | solution.py:257
  23.8 1.9 %collective-permute-start = (bf16[16,6656]{1,0:T(8,128)(2,1)S(1)}, bf16[16,6656]{1,0:T(8,128)(2,1)S(1)}, u32[]{:S(2)}, u32[]{:S(2)}) collective-permute-start(bf16[16,6656]{1,0:T(8,128)(2,1)S(1)} %constant_dynamic-update-slice_fusion), channel_id=1, source_target_pairs={{0,16},{16,32},{32,48},{48,64},{64,80},{80,96},{96,112},{112,0},{1... | collective-permute-start | bytes 638984 | tf_op jit(solution)/shard_map/ppermute | solution.py:256
  26.5 4.0 %all-to-all-start.1 = ((bf16[4,4,32,256]{3,2,1,0:T(8,128)(2,1)}), bf16[4,4,32,256]{3,2,1,0:T(8,128)(2,1)S(1)}, u32[]{:S(2)}, u32[]{:S(2)}) async-start(bf16[4,4,32,256]{3,2,1,0:T(8,128)(2,1)} %broadcast_in_dim.11), calls=%async_computation.1 | async-start | bytes 524288 | tf_op jit(solution)/shard_map/all_to_all | solution.py:20
  31.2 4.8 %all-to-all-done.1.r_ref = bf16[4,4,32,256]{3,2,1,0:T(8,128)(2,1)S(1)} async-done(((bf16[4,4,32,256]{3,2,1,0:T(8,128)(2,1)}), bf16[4,4,32,256]{3,2,1,0:T(8,128)(2,1)S(1)}, u32[]{:S(2)}, u32[]{:S(2)}) %all-to-all-start.1) | async-done | bytes 262176 | tf_op jit(solution)/shard_map/all_to_all | solution.py:20
  36.6 4.6 %collective-permute-start.3 = (bf16[16,6656]{1,0:T(8,128)(2,1)S(1)}, bf16[16,6656]{1,0:T(8,128)(2,1)S(1)}, u32[]{:S(2)}, u32[]{:S(2)}) collective-permute-start(bf16[16,6656]{1,0:T(8,128)(2,1)S(1)} %collective-permute-done.1), channel_id=1, source_target_pairs={{0,112},{16,0},{32,16},{48,32},{64,48},{80,64},{96,80},{112,96},{1... | collective-permute-start | bytes 638984 | tf_op jit(solution)/shard_map/ppermute | solution.py:262
  41.2 1.9 %collective-permute-start.2 = (bf16[16,6656]{1,0:T(8,128)(2,1)S(1)}, bf16[16,6656]{1,0:T(8,128)(2,1)S(1)}, u32[]{:S(2)}, u32[]{:S(2)}) collective-permute-start(bf16[16,6656]{1,0:T(8,128)(2,1)S(1)} %collective-permute-done), channel_id=1, source_target_pairs={{0,16},{16,32},{32,48},{48,64},{64,80},{80,96},{96,112},{112,0},{1... | collective-permute-start | bytes 638984 | tf_op jit(solution)/shard_map/ppermute | solution.py:261
  43.9 5.2 %collective-permute-done.2 = bf16[16,6656]{1,0:T(8,128)(2,1)S(1)} collective-permute-done((bf16[16,6656]{1,0:T(8,128)(2,1)S(1)}, bf16[16,6656]{1,0:T(8,128)(2,1)S(1)}, u32[]{:S(2)}, u32[]{:S(2)}) %collective-permute-start.2) | collective-permute-done | bytes 213024 | tf_op jit(solution)/shard_map/ppermute | solution.py:261
  49.0 1.9 %collective-permute-start.5 = (bf16[16,6656]{1,0:T(8,128)(2,1)S(1)}, bf16[16,6656]{1,0:T(8,128)(2,1)S(1)}, u32[]{:S(2)}, u32[]{:S(2)}) collective-permute-start(bf16[16,6656]{1,0:T(8,128)(2,1)S(1)} %collective-permute-done.2), channel_id=1, source_target_pairs={{0,16},{16,32},{32,48},{48,64},{64,80},{80,96},{96,112},{112,0},{1... | collective-permute-start | bytes 638984 | tf_op jit(solution)/shard_map/ppermute | solution.py:265
  51.6 4.6 %collective-permute-start.6 = (bf16[16,6656]{1,0:T(8,128)(2,1)S(1)}, bf16[16,6656]{1,0:T(8,128)(2,1)S(1)}, u32[]{:S(2)}, u32[]{:S(2)}) collective-permute-start(bf16[16,6656]{1,0:T(8,128)(2,1)S(1)} %collective-permute-done.3), channel_id=1, source_target_pairs={{0,112},{16,0},{32,16},{48,32},{64,48},{80,64},{96,80},{112,96},{1... | collective-permute-start | bytes 638984 | tf_op jit(solution)/shard_map/ppermute | solution.py:266
  56.8 1.9 %collective-permute-start.7 = (bf16[16,6656]{1,0:T(8,128)(2,1)S(1)}, bf16[16,6656]{1,0:T(8,128)(2,1)S(1)}, u32[]{:S(2)}, u32[]{:S(2)}) collective-permute-start(bf16[16,6656]{1,0:T(8,128)(2,1)S(1)} %collective-permute-done.5), channel_id=1, source_target_pairs={{0,16},{16,32},{32,48},{48,64},{64,80},{80,96},{96,112},{112,0},{1... | collective-permute-start | bytes 638984 | tf_op jit(solution)/shard_map/ppermute | solution.py:267
  59.4 6.2 %collective-permute-done.7 = bf16[16,6656]{1,0:T(8,128)(2,1)S(1)} collective-permute-done((bf16[16,6656]{1,0:T(8,128)(2,1)S(1)}, bf16[16,6656]{1,0:T(8,128)(2,1)S(1)}, u32[]{:S(2)}, u32[]{:S(2)}) %collective-permute-start.7) | collective-permute-done | bytes 213024 | tf_op jit(solution)/shard_map/ppermute | solution.py:267
  66.8 3.8 %all-to-all-start.2 = ((bf16[8,32,2560]{2,1,0:T(8,128)(2,1)}), bf16[8,32,2560]{2,1,0:T(8,128)(2,1)S(1)}, u32[]{:S(2)}, u32[]{:S(2)}) async-start(bf16[8,32,2560]{2,1,0:T(8,128)(2,1)} %broadcast_in_dim.12), calls=%async_computation.2 | async-start | bytes 2621440 | tf_op jit(solution)/shard_map/all_to_all | solution.py:20
  71.3 10.5 %collective-permute-start.4 = (bf16[5,16,6656]{2,1,0:T(8,128)(2,1)}, bf16[5,16,6656]{2,1,0:T(8,128)(2,1)}, u32[]{:S(2)}, u32[]{:S(2)}) collective-permute-start(bf16[5,16,6656]{2,1,0:T(8,128)(2,1)} %bitcast_dynamic-update-slice_fusion.early_in_ref), channel_id=1, source_target_pairs={{0,8},{8,0},{1,9},{9,1},{2,10},{10,2},{3,11},{11,3},{4,12},{12,4},... | collective-permute-start | bytes 3194888 | tf_op jit(solution)/shard_map/ppermute | solution.py:264
  81.8 1.9 %collective-permute-start.8 = (bf16[3,16,6656]{2,1,0:T(8,128)(2,1)S(1)}, bf16[3,16,6656]{2,1,0:T(8,128)(2,1)S(1)}, u32[]{:S(2)}, u32[]{:S(2)}) collective-permute-start(bf16[3,16,6656]{2,1,0:T(8,128)(2,1)S(1)} %pad_maximum_fusion.late_in_ref), channel_id=1, source_target_pairs={{0,8},{8,0},{1,9},{9,1},{2,10},{10,2},{3,11},{11,3},{4,12},{12,4},... | collective-permute-start | bytes 1916936 | tf_op jit(solution)/shard_map/ppermute | solution.py:269
  84.0 1.8 %collective-permute-done.8.late_far_in_ref = bf16[3,16,6656]{2,1,0:T(8,128)(2,1)S(1)} collective-permute-done((bf16[3,16,6656]{2,1,0:T(8,128)(2,1)S(1)}, bf16[3,16,6656]{2,1,0:T(8,128)(2,1)S(1)}, u32[]{:S(2)}, u32[]{:S(2)}) %collective-permute-start.8) | collective-permute-done | bytes 639008 | tf_op jit(solution)/shard_map/ppermute | solution.py:269
  85.8 5.6 %shard_map.86 = (bf16[64,2048]{1,0:T(8,128)(2,1)S(1)}, bf16[64,2048]{1,0:T(8,128)(2,1)S(1)}, bf16[64,2048]{1,0:T(8,128)(2,1)S(1)}, bf16[64,2048]{1,0:T(8,128)(2,1)S(1)}, f32[256,1024]{1,0:T(8,128)}) custom-call(s32[13]{0:T(128)S(1)} %concatenate.12.place_ref, bf16[5,16,6656]{2,1,0:T(8,128)(2,1)} %bitcast_dynamic-update-slice_fusion.early_in_ref, ...), custom_call_target="tpu_custom_call" | custom-call | flops 2147483648 | bytes 6819892 | tf_op jit(solution)/shard_map/pallas_call | solution.py:216
  91.4 2.2 %collective-permute-start.9 = (bf16[64,2048]{1,0:T(8,128)(2,1)S(1)}, bf16[64,2048]{1,0:T(8,128)(2,1)S(1)}, u32[]{:S(2)}, u32[]{:S(2)}) collective-permute-start(bf16[64,2048]{1,0:T(8,128)(2,1)S(1)} %get-tuple-element.15), channel_id=1, source_target_pairs={{0,2},{2,4},{4,6},{6,0},{1,3},{3,5},{5,7},{7,1},{8,10},{10,12},{12... | collective-permute-start | bytes 786440 | tf_op jit(solution)/shard_map/ppermute | solution.py:289
  93.6 4.3 %collective-permute-start.10 = (bf16[64,2048]{1,0:T(8,128)(2,1)S(1)}, bf16[64,2048]{1,0:T(8,128)(2,1)S(1)}, u32[]{:S(2)}, u32[]{:S(2)}) collective-permute-start(bf16[64,2048]{1,0:T(8,128)(2,1)S(1)} %get-tuple-element.16), channel_id=1, source_target_pairs={{0,6},{2,0},{4,2},{6,4},{1,7},{3,1},{5,3},{7,5},{8,14},{10,8},{12,... | collective-permute-start | bytes 786440 | tf_op jit(solution)/shard_map/ppermute | solution.py:289
  97.9 1.9 %collective-permute-start.11 = (bf16[64,2048]{1,0:T(8,128)(2,1)S(1)}, bf16[64,2048]{1,0:T(8,128)(2,1)S(1)}, u32[]{:S(2)}, u32[]{:S(2)}) collective-permute-start(bf16[64,2048]{1,0:T(8,128)(2,1)S(1)} %get-tuple-element.17), channel_id=1, source_target_pairs={{0,4},{2,6},{4,0},{6,2},{1,5},{3,7},{5,1},{7,3},{8,12},{10,14},{12... | collective-permute-start | bytes 786440 | tf_op jit(solution)/shard_map/ppermute | solution.py:289
  99.8 2.4 %collective-permute-done.9.b_ref = bf16[64,2048]{1,0:T(8,128)(2,1)S(1)} collective-permute-done((bf16[64,2048]{1,0:T(8,128)(2,1)S(1)}, bf16[64,2048]{1,0:T(8,128)(2,1)S(1)}, u32[]{:S(2)}, u32[]{:S(2)}) %collective-permute-start.9) | collective-permute-done | bytes 262176 | tf_op jit(solution)/shard_map/ppermute | solution.py:289
  102.3 1.6 collective-permute-done.10.c_ref
  103.8 4.6 %collective-permute-done.11.d_ref = bf16[64,2048]{1,0:T(8,128)(2,1)S(1)} collective-permute-done((bf16[64,2048]{1,0:T(8,128)(2,1)S(1)}, bf16[64,2048]{1,0:T(8,128)(2,1)S(1)}, u32[]{:S(2)}, u32[]{:S(2)}) %collective-permute-start.11) | collective-permute-done | bytes 262176 | tf_op jit(solution)/shard_map/ppermute | solution.py:289
  109.1 3.5 %collective-permute-start.13 = (bf16[8,32,2560]{2,1,0:T(8,128)(2,1)S(1)}, bf16[8,32,2560]{2,1,0:T(8,128)(2,1)S(1)}, u32[]{:S(2)}, u32[]{:S(2)}) collective-permute-start(bf16[8,32,2560]{2,1,0:T(8,128)(2,1)S(1)} %all-to-all-done.2.mine_ref), channel_id=1, source_target_pairs={{0,8},{8,0},{1,9},{9,1},{2,10},{10,2},{3,11},{11,3},{4,12},{12,4},... | collective-permute-start | bytes 3932168 | tf_op jit(solution)/shard_map/ppermute | solution.py:293
  112.7 7.9 %collective-permute-start.12 = (bf16[64,2048]{1,0:T(8,128)(2,1)S(1)}, bf16[64,2048]{1,0:T(8,128)(2,1)S(1)}, u32[]{:S(2)}, u32[]{:S(2)}) collective-permute-start(bf16[64,2048]{1,0:T(8,128)(2,1)S(1)} %shard_map.87.near_ref), channel_id=1, source_target_pairs={{0,1},{1,0},{2,3},{3,2},{4,5},{5,4},{6,7},{7,6},{8,9},{9,8},{10,11... | collective-permute-start | bytes 786440 | tf_op jit(solution)/shard_map/ppermute | solution.py:294
  120.6 12.3 %collective-permute-done.12.far_ref = bf16[64,2048]{1,0:T(8,128)(2,1)S(1)} collective-permute-done((bf16[64,2048]{1,0:T(8,128)(2,1)S(1)}, bf16[64,2048]{1,0:T(8,128)(2,1)S(1)}, u32[]{:S(2)}, u32[]{:S(2)}) %collective-permute-start.12) | collective-permute-done | bytes 262176 | tf_op jit(solution)/shard_map/ppermute | solution.py:294
  132.9 2.2 %shard_map.89 = (f32[64,2048]{1,0:T(8,128)S(1)}, bf16[64,2048]{1,0:T(8,128)(2,1)S(1)}) custom-call(s32[13]{0:T(128)S(1)} %concatenate.12.place_ref, bf16[64,2048]{1,0:T(8,128)(2,1)S(1)} %shard_map.87.near_ref, bf16[64,2048]{1,0:T(8,128)(2,1)S(1)} %collective-permute-done.12.far_ref, bf16[8,32,2560]{2,1,0:T(8,128)(2,1)S(1)} %all-to-all-done.2.mine_ref, ...), custom_call_target="tpu_custom_call" | custom-call | flops 335544320 | bytes 3932212 | tf_op jit(solution)/shard_map/pallas_call | solution.py:216
  135.1 4.1 %collective-permute-start.14 = (bf16[64,2048]{1,0:T(8,128)(2,1)S(1)}, bf16[64,2048]{1,0:T(8,128)(2,1)S(1)}, u32[]{:S(2)}, u32[]{:S(2)}) collective-permute-start(bf16[64,2048]{1,0:T(8,128)(2,1)S(1)} %get-tuple-element.22), channel_id=1, source_target_pairs={{0,1},{1,0},{2,3},{3,2},{4,5},{5,4},{6,7},{7,6},{8,9},{9,8},{10,11... | collective-permute-start | bytes 786440 | tf_op jit(solution)/shard_map/ppermute | solution.py:305
  139.2 14.1 %collective-permute-done.14 = bf16[64,2048]{1,0:T(8,128)(2,1)S(1)} collective-permute-done((bf16[64,2048]{1,0:T(8,128)(2,1)S(1)}, bf16[64,2048]{1,0:T(8,128)(2,1)S(1)}, u32[]{:S(2)}, u32[]{:S(2)}) %collective-permute-start.14) | collective-permute-done | bytes 262176 | tf_op jit(solution)/shard_map/ppermute | solution.py:305
  153.5 18.6 %all_to_all.20 = bf16[4,64,2048]{2,1,0:T(8,128)(2,1)S(1)} all-to-all(bf16[4,64,2048]{2,1,0:T(8,128)(2,1)S(1)} %broadcast_in_dim.13), channel_id=1, replica_groups=mesh['zl'=4,'y'=8,'core'=2,'x'=4,'zh'=2] {'x'}, dimensions={0} | all-to-all | bytes 2097152 | tf_op jit(solution)/shard_map/all_to_all | solution.py:20
  172.0 5.9 %shard_map.90 = (f32[1024,256]{1,0:T(8,128)}, f32[256,256]{1,0:T(8,128)}) custom-call(s32[13]{0:T(128)S(1)} %concatenate.12.place_ref, bf16[256,2048]{1,0:T(8,128)(2,1)S(1)} %bitcast.57, f32[256,1024]{1,0:T(8,128)} %get-tuple-element.23.in_ref, bf16[5,16,6656]{2,1,0:T(8,128)(2,1)} %bitcast_dynamic-update-slice_fusion.early_in_ref, ...), custom_call_target="tpu_custom_call" | custom-call | flops 2147483648 | bytes 6819892 | tf_op jit(solution)/shard_map/pallas_call | solution.py:216
  (37 shorter events, 9.6 us)
Async XLA Ops:
  0.6 10.0 %copy-start = (s32[1,1024]{1,0:T(1,128)S(1)}, s32[1,1024]{1,0:T(1,128)}, u32[]{:S(2)}) copy-start(s32[1,1024]{1,0:T(1,128)} %param.13) | copy-start | bytes 12292
  2.2 14.0 %all-to-all-start = ((bf16[4,32,1280]{2,1,0:T(8,128)(2,1)}), bf16[4,32,1280]{2,1,0:T(8,128)(2,1)S(1)}, u32[]{:S(2)}, u32[]{:S(2)}) async-start(bf16[4,32,1280]{2,1,0:T(8,128)(2,1)} %broadcast_in_dim.10), calls=%async_computation | async-start | bytes 655360 | tf_op jit(solution)/shard_map/all_to_all | solution.py:20
  16.3 20.3 %collective-permute-start.1 = (bf16[16,6656]{1,0:T(8,128)(2,1)S(1)}, bf16[16,6656]{1,0:T(8,128)(2,1)S(1)}, u32[]{:S(2)}, u32[]{:S(2)}) collective-permute-start(bf16[16,6656]{1,0:T(8,128)(2,1)S(1)} %constant_dynamic-update-slice_fusion), channel_id=1, source_target_pairs={{0,112},{16,0},{32,16},{48,32},{64,48},{80,64},{96,80},{112,96},{1... | collective-permute-start | bytes 638984 | tf_op jit(solution)/shard_map/ppermute | solution.py:257
  23.8 17.4 %collective-permute-start = (bf16[16,6656]{1,0:T(8,128)(2,1)S(1)}, bf16[16,6656]{1,0:T(8,128)(2,1)S(1)}, u32[]{:S(2)}, u32[]{:S(2)}) collective-permute-start(bf16[16,6656]{1,0:T(8,128)(2,1)S(1)} %constant_dynamic-update-slice_fusion), channel_id=1, source_target_pairs={{0,16},{16,32},{32,48},{48,64},{64,80},{80,96},{96,112},{112,0},{1... | collective-permute-start | bytes 638984 | tf_op jit(solution)/shard_map/ppermute | solution.py:256
  26.5 9.5 %all-to-all-start.1 = ((bf16[4,4,32,256]{3,2,1,0:T(8,128)(2,1)}), bf16[4,4,32,256]{3,2,1,0:T(8,128)(2,1)S(1)}, u32[]{:S(2)}, u32[]{:S(2)}) async-start(bf16[4,4,32,256]{3,2,1,0:T(8,128)(2,1)} %broadcast_in_dim.11), calls=%async_computation.1 | async-start | bytes 524288 | tf_op jit(solution)/shard_map/all_to_all | solution.py:20
  36.6 15.0 %collective-permute-start.3 = (bf16[16,6656]{1,0:T(8,128)(2,1)S(1)}, bf16[16,6656]{1,0:T(8,128)(2,1)S(1)}, u32[]{:S(2)}, u32[]{:S(2)}) collective-permute-start(bf16[16,6656]{1,0:T(8,128)(2,1)S(1)} %collective-permute-done.1), channel_id=1, source_target_pairs={{0,112},{16,0},{32,16},{48,32},{64,48},{80,64},{96,80},{112,96},{1... | collective-permute-start | bytes 638984 | tf_op jit(solution)/shard_map/ppermute | solution.py:262
  41.2 7.8 %collective-permute-start.2 = (bf16[16,6656]{1,0:T(8,128)(2,1)S(1)}, bf16[16,6656]{1,0:T(8,128)(2,1)S(1)}, u32[]{:S(2)}, u32[]{:S(2)}) collective-permute-start(bf16[16,6656]{1,0:T(8,128)(2,1)S(1)} %collective-permute-done), channel_id=1, source_target_pairs={{0,16},{16,32},{32,48},{48,64},{64,80},{80,96},{96,112},{112,0},{1... | collective-permute-start | bytes 638984 | tf_op jit(solution)/shard_map/ppermute | solution.py:261
  49.0 7.8 %collective-permute-start.5 = (bf16[16,6656]{1,0:T(8,128)(2,1)S(1)}, bf16[16,6656]{1,0:T(8,128)(2,1)S(1)}, u32[]{:S(2)}, u32[]{:S(2)}) collective-permute-start(bf16[16,6656]{1,0:T(8,128)(2,1)S(1)} %collective-permute-done.2), channel_id=1, source_target_pairs={{0,16},{16,32},{32,48},{48,64},{64,80},{80,96},{96,112},{112,0},{1... | collective-permute-start | bytes 638984 | tf_op jit(solution)/shard_map/ppermute | solution.py:265
  51.6 30.1 %collective-permute-start.6 = (bf16[16,6656]{1,0:T(8,128)(2,1)S(1)}, bf16[16,6656]{1,0:T(8,128)(2,1)S(1)}, u32[]{:S(2)}, u32[]{:S(2)}) collective-permute-start(bf16[16,6656]{1,0:T(8,128)(2,1)S(1)} %collective-permute-done.3), channel_id=1, source_target_pairs={{0,112},{16,0},{32,16},{48,32},{64,48},{80,64},{96,80},{112,96},{1... | collective-permute-start | bytes 638984 | tf_op jit(solution)/shard_map/ppermute | solution.py:266
  56.8 8.8 %collective-permute-start.7 = (bf16[16,6656]{1,0:T(8,128)(2,1)S(1)}, bf16[16,6656]{1,0:T(8,128)(2,1)S(1)}, u32[]{:S(2)}, u32[]{:S(2)}) collective-permute-start(bf16[16,6656]{1,0:T(8,128)(2,1)S(1)} %collective-permute-done.5), channel_id=1, source_target_pairs={{0,16},{16,32},{32,48},{48,64},{64,80},{80,96},{96,112},{112,0},{1... | collective-permute-start | bytes 638984 | tf_op jit(solution)/shard_map/ppermute | solution.py:267
  66.8 42.4 %all-to-all-start.2 = ((bf16[8,32,2560]{2,1,0:T(8,128)(2,1)}), bf16[8,32,2560]{2,1,0:T(8,128)(2,1)S(1)}, u32[]{:S(2)}, u32[]{:S(2)}) async-start(bf16[8,32,2560]{2,1,0:T(8,128)(2,1)} %broadcast_in_dim.12), calls=%async_computation.2 | async-start | bytes 2621440 | tf_op jit(solution)/shard_map/all_to_all | solution.py:20
  71.3 14.5 %collective-permute-start.4 = (bf16[5,16,6656]{2,1,0:T(8,128)(2,1)}, bf16[5,16,6656]{2,1,0:T(8,128)(2,1)}, u32[]{:S(2)}, u32[]{:S(2)}) collective-permute-start(bf16[5,16,6656]{2,1,0:T(8,128)(2,1)} %bitcast_dynamic-update-slice_fusion.early_in_ref), channel_id=1, source_target_pairs={{0,8},{8,0},{1,9},{9,1},{2,10},{10,2},{3,11},{11,3},{4,12},{12,4},... | collective-permute-start | bytes 3194888 | tf_op jit(solution)/shard_map/ppermute | solution.py:264
  81.8 4.0 %collective-permute-start.8 = (bf16[3,16,6656]{2,1,0:T(8,128)(2,1)S(1)}, bf16[3,16,6656]{2,1,0:T(8,128)(2,1)S(1)}, u32[]{:S(2)}, u32[]{:S(2)}) collective-permute-start(bf16[3,16,6656]{2,1,0:T(8,128)(2,1)S(1)} %pad_maximum_fusion.late_in_ref), channel_id=1, source_target_pairs={{0,8},{8,0},{1,9},{9,1},{2,10},{10,2},{3,11},{11,3},{4,12},{12,4},... | collective-permute-start | bytes 1916936 | tf_op jit(solution)/shard_map/ppermute | solution.py:269
  91.4 10.9 %collective-permute-start.9 = (bf16[64,2048]{1,0:T(8,128)(2,1)S(1)}, bf16[64,2048]{1,0:T(8,128)(2,1)S(1)}, u32[]{:S(2)}, u32[]{:S(2)}) collective-permute-start(bf16[64,2048]{1,0:T(8,128)(2,1)S(1)} %get-tuple-element.15), channel_id=1, source_target_pairs={{0,2},{2,4},{4,6},{6,0},{1,3},{3,5},{5,7},{7,1},{8,10},{10,12},{12... | collective-permute-start | bytes 786440 | tf_op jit(solution)/shard_map/ppermute | solution.py:289
  93.6 10.2 %collective-permute-start.10 = (bf16[64,2048]{1,0:T(8,128)(2,1)S(1)}, bf16[64,2048]{1,0:T(8,128)(2,1)S(1)}, u32[]{:S(2)}, u32[]{:S(2)}) collective-permute-start(bf16[64,2048]{1,0:T(8,128)(2,1)S(1)} %get-tuple-element.16), channel_id=1, source_target_pairs={{0,6},{2,0},{4,2},{6,4},{1,7},{3,1},{5,3},{7,5},{8,14},{10,8},{12,... | collective-permute-start | bytes 786440 | tf_op jit(solution)/shard_map/ppermute | solution.py:289
  97.9 10.5 %collective-permute-start.11 = (bf16[64,2048]{1,0:T(8,128)(2,1)S(1)}, bf16[64,2048]{1,0:T(8,128)(2,1)S(1)}, u32[]{:S(2)}, u32[]{:S(2)}) collective-permute-start(bf16[64,2048]{1,0:T(8,128)(2,1)S(1)} %get-tuple-element.17), channel_id=1, source_target_pairs={{0,4},{2,6},{4,0},{6,2},{1,5},{3,7},{5,1},{7,3},{8,12},{10,14},{12... | collective-permute-start | bytes 786440 | tf_op jit(solution)/shard_map/ppermute | solution.py:289
  109.1 23.8 %collective-permute-start.13 = (bf16[8,32,2560]{2,1,0:T(8,128)(2,1)S(1)}, bf16[8,32,2560]{2,1,0:T(8,128)(2,1)S(1)}, u32[]{:S(2)}, u32[]{:S(2)}) collective-permute-start(bf16[8,32,2560]{2,1,0:T(8,128)(2,1)S(1)} %all-to-all-done.2.mine_ref), channel_id=1, source_target_pairs={{0,8},{8,0},{1,9},{9,1},{2,10},{10,2},{3,11},{11,3},{4,12},{12,4},... | collective-permute-start | bytes 3932168 | tf_op jit(solution)/shard_map/ppermute | solution.py:293
  112.7 20.2 %collective-permute-start.12 = (bf16[64,2048]{1,0:T(8,128)(2,1)S(1)}, bf16[64,2048]{1,0:T(8,128)(2,1)S(1)}, u32[]{:S(2)}, u32[]{:S(2)}) collective-permute-start(bf16[64,2048]{1,0:T(8,128)(2,1)S(1)} %shard_map.87.near_ref), channel_id=1, source_target_pairs={{0,1},{1,0},{2,3},{3,2},{4,5},{5,4},{6,7},{7,6},{8,9},{9,8},{10,11... | collective-permute-start | bytes 786440 | tf_op jit(solution)/shard_map/ppermute | solution.py:294
  135.1 18.2 %collective-permute-start.14 = (bf16[64,2048]{1,0:T(8,128)(2,1)S(1)}, bf16[64,2048]{1,0:T(8,128)(2,1)S(1)}, u32[]{:S(2)}, u32[]{:S(2)}) collective-permute-start(bf16[64,2048]{1,0:T(8,128)(2,1)S(1)} %get-tuple-element.22), channel_id=1, source_target_pairs={{0,1},{1,0},{2,3},{3,2},{4,5},{5,4},{6,7},{7,6},{8,9},{9,8},{10,11... | collective-permute-start | bytes 786440 | tf_op jit(solution)/shard_map/ppermute | solution.py:305
